TPU v7x, 32 devices: a whole 2x2x4 slice. The times are simulated.
32 devices in a mesh: group: 4 (over z), dev: 8 (over y, x, core).
Axes of the slice: x: 2, y: 2, z: 4, core: 2. Of those that a mesh axis runs over, the one named last changes fastest.
Arguments:
- populations: float32 [128, 19, 4096], P(('group', 'dev')), may hold values from -3 to 3
- fluid_flags: int32 [128, 4096], P(('group', 'dev')), may hold values from 0 to 1, as said below
- neighbours: int32 [128, 18], P(('group', 'dev')), may hold values from -1 to 11, as said below
- relax_rate: float32 [128], P(('group', 'dev')), may hold values from 1 to 1.9
Outputs:
- advanced: float32 [128, 19, 4096], P(('group', 'dev'))
Inputs may be any that keep to these rules, and one draw needn't show every extreme that they name: `fluid_flags`: on every device the slots that hold a block come first and the later slots have no fluid cell. In every group some device holds a block in all 4 slots. `neighbours`: an entry is -1 or (dz + 1) * 4 + t, where dz is the third component of the direction; it names slot t of the device dz places further along dev in the same group, a slot that holds a block, and that block's entry in the opposite direction names back. Slots that hold no block have -1 in every direction.
All inputs are finite; a program needn't handle non-finite values.
Results may differ from a plain program's by a relative error of at most 0.0003.
Values sent between devices are 32-bit elements; how exact they have to be, the bound alone decides.
No kernel may reach another device: no remote copies, remote signals or barrier semaphores. Data moves between devices by JAX's collectives and lax.ppermute only.
A program may use at most 128 MiB of HBM per device.

v0:
```python
import jax
import jax.numpy as jnp
import numpy as np
from jax import lax
from jax.sharding import PartitionSpec as P

BLOCK = 16
STEPS = 2


def extended(x, sides, width):
    for axis, dim in sides:
        peers, length = (lax.axis_size(axis), x.shape[dim])
        up = [(i, (i + 1) % peers) for i in range(peers - 1)]
        down = [(j, i) for i, j in up]
        last = lax.slice_in_dim(x, length - width, length, axis=dim)
        first = lax.slice_in_dim(x, 0, width, axis=dim)
        before = lax.ppermute(last, axis, up)
        after = lax.ppermute(first, axis, down)
        x = jnp.concatenate([before, x, after], axis=dim)
    return x


def invert_matrix(rows_in):
    size_n = len(rows_in)
    work = [
        list(rows_in[row_num]) + [1.0 if col_num == row_num else 0.0 for col_num in range(size_n)]
        for row_num in range(size_n)
    ]
    for col_num in range(size_n):
        pivot_row = max(range(col_num, size_n), key=lambda row_num: abs(work[row_num][col_num]))
        work[col_num], work[pivot_row] = (work[pivot_row], work[col_num])
        pivot_val = work[col_num][col_num]
        work[col_num] = [entry / pivot_val for entry in work[col_num]]
        for row_num in range(size_n):
            if row_num != col_num:
                factor = work[row_num][col_num]
                if factor != 0.0:
                    work[row_num] = [
                        entry - factor * pivot_entry
                        for entry, pivot_entry in zip(work[row_num], work[col_num])
                    ]
    return [row_list[size_n:] for row_list in work]


def lattice():
    velocity = [[0, 0, 0]]
    for axis_num in range(3):
        for side_sign in (1, -1):
            vector = [0, 0, 0]
            vector[axis_num] = side_sign
            velocity.append(vector)
    for axis_one, axis_two in ((0, 1), (0, 2), (1, 2)):
        for sign_one in (1, -1):
            for sign_two in (1, -1):
                vector = [0, 0, 0]
                vector[axis_one] = sign_one
                vector[axis_two] = sign_two
                velocity.append(vector)
    weights = [1.0 / 3.0] + [1.0 / 18.0] * 6 + [1.0 / 36.0] * 12
    opposite = [velocity.index([-entry for entry in velocity[lane_num]]) for lane_num in range(19)]
    comp_x = [float(vector[0]) for vector in velocity]
    comp_y = [float(vector[1]) for vector in velocity]
    comp_z = [float(vector[2]) for vector in velocity]
    makers = [
        lambda a, b, c: 1.0,
        lambda a, b, c: a,
        lambda a, b, c: b,
        lambda a, b, c: c,
        lambda a, b, c: a * b,
        lambda a, b, c: a * c,
        lambda a, b, c: b * c,
        lambda a, b, c: a * a - b * b,
        lambda a, b, c: a * a - c * c,
        lambda a, b, c: a * a + b * b + c * c,
        lambda a, b, c: a * b * b,
        lambda a, b, c: a * c * c,
        lambda a, b, c: b * a * a,
        lambda a, b, c: b * c * c,
        lambda a, b, c: c * a * a,
        lambda a, b, c: c * b * b,
        lambda a, b, c: a * a * b * b,
        lambda a, b, c: a * a * c * c,
        lambda a, b, c: b * b * c * c,
    ]
    moment_rows = [
        [maker(comp_x[col_num], comp_y[col_num], comp_z[col_num]) for col_num in range(19)]
        for maker in makers
    ]
    inverse = invert_matrix(moment_rows)
    table_other = []
    table_shear = []
    for row_num in range(19):
        other_row = []
        shear_row = []
        for col_num in range(19):
            other_sum = sum(
                (
                    inverse[row_num][mom_num] * moment_rows[mom_num][col_num]
                    for mom_num in range(9, 19)
                )
            )
            shear_sum = sum(
                (
                    inverse[row_num][mom_num] * moment_rows[mom_num][col_num]
                    for mom_num in range(4, 9)
                )
            )
            ratio = weights[col_num] / weights[row_num]
            other_row.append(other_sum * ratio)
            shear_row.append(shear_sum * ratio)
        table_other.append(other_row)
        table_shear.append(shear_row)
    return (
        np.array(velocity),
        np.array(weights),
        opposite,
        np.array(table_other),
        np.array(table_shear),
    )


def collide(current, rates):
    velocity, weights, opposite, table_other, table_shear = lattice()
    moment_in = np.concatenate([weights[None, :], (weights[:, None] * velocity).T], 0)
    density_momentum = jnp.einsum(
        "ki,nic->nkc", jnp.asarray(moment_in, jnp.float32), current, precision=lax.Precision.HIGHEST
    )
    density = density_momentum[:, 0]
    momentum = density_momentum[:, 1:]
    projected = jnp.einsum(
        "ik,nkc->nic", jnp.asarray(velocity, jnp.float32), momentum, precision=lax.Precision.HIGHEST
    )
    speed_sq = jnp.sum(momentum * momentum, axis=1)
    equilibrium = (
        density[:, None] + 3.0 * projected + 4.5 * projected * projected - 1.5 * speed_sq[:, None]
    )
    departure = current - equilibrium
    matrices = (
        jnp.asarray(table_other, jnp.float32)[None]
        + rates[:, None, None] * jnp.asarray(table_shear, jnp.float32)[None]
    )
    return current - jnp.einsum(
        "nij,njc->nic", matrices, departure, precision=lax.Precision.HIGHEST
    )


def make_slabs(collided, fluid_flags):
    velocity = lattice()[0]
    block_count = collided.shape[0]
    blocked = collided.reshape(block_count, 19, BLOCK, BLOCK, BLOCK)
    wet_cells = fluid_flags.reshape(block_count, BLOCK, BLOCK, BLOCK).astype(jnp.float32)
    face_list = []
    for lane_num in range(1, 7):
        axis_num = int(np.argmax(np.abs(velocity[lane_num])))
        side_sign = int(velocity[lane_num][axis_num])
        layer_index = BLOCK - 1 if side_sign > 0 else 0
        members = [
            lane_two for lane_two in range(19) if int(velocity[lane_two][axis_num]) == side_sign
        ]
        layer_values = lax.index_in_dim(blocked, layer_index, axis_num + 2, keepdims=False)[
            :, members
        ]
        layer_flags = lax.index_in_dim(wet_cells, layer_index, axis_num + 1, keepdims=False)
        face_list.append(
            jnp.concatenate([layer_values, layer_flags[:, None]], 1).reshape(
                block_count, 6, BLOCK * BLOCK
            )
        )
    edge_list = []
    for lane_num in range(7, 19):
        nonzero = [axis_num for axis_num in range(3) if int(velocity[lane_num][axis_num]) != 0]
        axis_one, axis_two = nonzero
        end_one = BLOCK - 1 if velocity[lane_num][axis_one] > 0 else 0
        end_two = BLOCK - 1 if velocity[lane_num][axis_two] > 0 else 0
        line_values = lax.index_in_dim(
            lax.index_in_dim(blocked[:, lane_num], end_one, axis_one + 1, keepdims=False),
            end_two,
            axis_two,
            keepdims=False,
        )
        line_flags = lax.index_in_dim(
            lax.index_in_dim(wet_cells, end_one, axis_one + 1, keepdims=False),
            end_two,
            axis_two,
            keepdims=False,
        )
        edge_list.append(jnp.stack([line_values, line_flags], 1))
    return (jnp.stack(face_list, 1), jnp.stack(edge_list, 1))


def propagate(current, collided, fluid_flags, rim_faces, rim_edges):
    velocity, weights, opposite, table_other, table_shear = lattice()
    block_count = current.shape[0]
    blocked = collided.reshape(block_count, 19, BLOCK, BLOCK, BLOCK)
    wet_cells = fluid_flags.reshape(block_count, BLOCK, BLOCK, BLOCK).astype(jnp.float32)
    padded = jnp.zeros((block_count, 19, BLOCK + 2, BLOCK + 2, BLOCK + 2), collided.dtype)
    padded = padded.at[:, :, 1:-1, 1:-1, 1:-1].set(blocked)
    open_mask = jnp.zeros((block_count, BLOCK + 2, BLOCK + 2, BLOCK + 2), wet_cells.dtype)
    open_mask = open_mask.at[:, 1:-1, 1:-1, 1:-1].set(wet_cells)
    inner = slice(1, BLOCK + 1)
    for face_num in range(6):
        lane_num = face_num + 1
        axis_num = int(np.argmax(np.abs(velocity[lane_num])))
        side_sign = int(velocity[lane_num][axis_num])
        rim_at = BLOCK + 1 if side_sign > 0 else 0
        spatial = tuple((rim_at if axis_two == axis_num else inner for axis_two in range(3)))
        members = [
            lane_two for lane_two in range(19) if int(velocity[lane_two][axis_num]) == -side_sign
        ]
        face_values = rim_faces[:, face_num].reshape(block_count, 6, BLOCK, BLOCK)
        for member_num, lane_two in enumerate(members):
            padded = padded.at[(slice(None), lane_two) + spatial].set(face_values[:, member_num])
        open_mask = open_mask.at[(slice(None),) + spatial].set(face_values[:, 5])
    for edge_num in range(12):
        lane_num = edge_num + 7
        spatial = tuple(
            (
                (
                    (BLOCK + 1 if velocity[lane_num][axis_two] > 0 else 0)
                    if int(velocity[lane_num][axis_two]) != 0
                    else inner
                )
                for axis_two in range(3)
            )
        )
        padded = padded.at[(slice(None), opposite[lane_num]) + spatial].set(
            rim_edges[:, edge_num, 0]
        )
        open_mask = open_mask.at[(slice(None),) + spatial].set(rim_edges[:, edge_num, 1])
    arrived_list = []
    for lane_num in range(19):
        window = tuple(
            (
                slice(1 - int(component), 1 - int(component) + BLOCK)
                for component in velocity[lane_num]
            )
        )
        pulled = padded[(slice(None), lane_num) + window]
        open_here = open_mask[(slice(None),) + window]
        arrived_list.append(jnp.where(open_here > 0, pulled, blocked[:, opposite[lane_num]]))
    arrived = jnp.stack(arrived_list, 1).reshape(block_count, 19, BLOCK * BLOCK * BLOCK)
    return jnp.where(fluid_flags[:, None, :] > 0, arrived, current)


def live_slots(fluid_flags):
    holds = jnp.max(fluid_flags, axis=1) > 0
    ranks = jnp.arange(1, fluid_flags.shape[0] + 1, dtype=jnp.int32)
    return jnp.max(jnp.where(holds, ranks, 0)).astype(jnp.int32)


def collide_live(current, rates, fluid_flags, occupied):
    slot_count = current.shape[0]
    batch_size = min(8, slot_count)
    turn_count = (occupied + batch_size - 1) // batch_size
    face_init = jnp.zeros((slot_count, 6, 6, BLOCK * BLOCK), jnp.float32)
    edge_init = jnp.zeros((slot_count, 12, 2, BLOCK), jnp.float32)

    def collide_one_turn(turn_num, carried):
        collided_all, face_all, edge_all = carried
        first_slot = turn_num * batch_size
        part_now = lax.dynamic_slice_in_dim(current, first_slot, batch_size, 0)
        rates_now = lax.dynamic_slice_in_dim(rates, first_slot, batch_size, 0)
        flags_now = lax.dynamic_slice_in_dim(fluid_flags, first_slot, batch_size, 0)
        collided = collide(part_now, rates_now)
        face_part, edge_part = make_slabs(collided, flags_now)
        return (
            lax.dynamic_update_slice_in_dim(collided_all, collided, first_slot, 0),
            lax.dynamic_update_slice_in_dim(face_all, face_part, first_slot, 0),
            lax.dynamic_update_slice_in_dim(edge_all, edge_part, first_slot, 0),
        )

    return lax.fori_loop(
        0, turn_count, collide_one_turn, (jnp.zeros_like(current), face_init, edge_init)
    )


def propagate_live(current, collided_all, fluid_flags, rim_faces, rim_edges, occupied):
    slot_count = current.shape[0]
    batch_size = min(8, slot_count)
    turn_count = (occupied + batch_size - 1) // batch_size

    def propagate_one_turn(turn_num, carried):
        first_slot = turn_num * batch_size
        part_now = lax.dynamic_slice_in_dim(carried, first_slot, batch_size, 0)
        collided = lax.dynamic_slice_in_dim(collided_all, first_slot, batch_size, 0)
        flags_now = lax.dynamic_slice_in_dim(fluid_flags, first_slot, batch_size, 0)
        faces_now = lax.dynamic_slice_in_dim(rim_faces, first_slot, batch_size, 0)
        edges_now = lax.dynamic_slice_in_dim(rim_edges, first_slot, batch_size, 0)
        updated = propagate(part_now, collided, flags_now, faces_now, edges_now)
        return lax.dynamic_update_slice_in_dim(carried, updated, first_slot, 0)

    return lax.fori_loop(0, turn_count, propagate_one_turn, current)


def gather_rims(face_slabs, edge_slabs, neighbours):
    slot_count = face_slabs.shape[0]
    face_len = 6 * BLOCK * BLOCK
    upper_edges = [4, 6, 8, 10]
    lower_edges = [5, 7, 9, 11]
    upward = jnp.concatenate(
        [
            face_slabs[:, 4].reshape(slot_count, -1),
            edge_slabs[:, upper_edges].reshape(slot_count, -1),
        ],
        1,
    )
    downward = jnp.concatenate(
        [
            face_slabs[:, 5].reshape(slot_count, -1),
            edge_slabs[:, lower_edges].reshape(slot_count, -1),
        ],
        1,
    )
    stacked = jnp.stack([downward, upward], 0)
    widened = extended(stacked, (("dev", 0),), 1)
    from_below = widened[0]
    from_above = widened[3]
    below_faces = from_below[:, :face_len].reshape(slot_count, 6, BLOCK * BLOCK)
    below_edges = from_below[:, face_len:].reshape(slot_count, 4, 2, BLOCK)
    above_faces = from_above[:, :face_len].reshape(slot_count, 6, BLOCK * BLOCK)
    above_edges = from_above[:, face_len:].reshape(slot_count, 4, 2, BLOCK)
    present = neighbours >= 0
    target = jnp.where(present, neighbours % slot_count, 0)
    face_list = []
    for face_num in range(6):
        if face_num < 4:
            source = face_slabs[:, face_num ^ 1]
        elif face_num == 4:
            source = above_faces
        else:
            source = below_faces
        face_list.append(
            jnp.where(present[:, face_num, None, None], source[target[:, face_num]], 0.0)
        )
    edge_list = []
    for edge_num in range(12):
        column = 6 + edge_num
        opposite_edge = 4 * (edge_num // 4) + 3 - edge_num % 4
        if edge_num < 4:
            source = edge_slabs[:, opposite_edge]
        elif edge_num % 2 == 0:
            source = above_edges[:, lower_edges.index(opposite_edge)]
        else:
            source = below_edges[:, upper_edges.index(opposite_edge)]
        edge_list.append(jnp.where(present[:, column, None, None], source[target[:, column]], 0.0))
    return (jnp.stack(face_list, 1), jnp.stack(edge_list, 1))


def body(populations, fluid_flags, neighbours, relax_rate):
    live_count = live_slots(fluid_flags)
    current = populations
    for step_num in range(STEPS):
        collided, face_slabs, edge_slabs = collide_live(
            current, relax_rate, fluid_flags, live_count
        )
        rim_faces, rim_edges = gather_rims(face_slabs, edge_slabs, neighbours)
        current = propagate_live(current, collided, fluid_flags, rim_faces, rim_edges, live_count)
    return current


def solution(mesh):
    placed = (
        P(("group", "dev"), None, None),
        P(("group", "dev"), None),
        P(("group", "dev"), None),
        P(("group", "dev")),
    )
    return jax.shard_map(
        body, mesh=mesh, in_specs=placed, out_specs=P(("group", "dev"), None, None), check_vma=False
    )
```

profile of v0, /device:TPU:0, one launch (start us, length us, event | category | flops | bytes accessed | tf_op | source)
XLA Modules:
  0.0 1033.4 jit_solution(15091290475001150199)
XLA Ops:
  138.2 384.7 %while.191 = (s32[]{:T(128)}, f32[4,19,4096]{2,0,1:T(4,128)S(1)}, s32[]{:T(128)}, s32[4,4096]{1,0:T(4,128)S(1)}, f32[4,16,16,16]{3,2,1,0:T(8,128)S(1)}, /*index=...) while((s32[]{:T(128)}, f32[4,19,4096]{2,0,1:T(4,128)S(1)}, ...), condition=%wide.region_6.7_spmd, body=%wide.region_5.6_spmd.sunk | while | flops 950274 | bytes 42097896 | solution.py:293
  146.5 11.6 %scatter.744 = f32[4,19,18,18,18]{4,3,2,0,1:T(8,128)} pad(f32[4,19,16,16,16]{4,3,2,0,1:T(8,128)} %reshape.7441, f32[]{:T(128)} %constant.5125.clone.1..sunk), padding=0_0x0_0x1_1x1_1x1_1 | pad | bytes 3018116 | tf_op jit(solution)/shard_map/while/body/scatter | solution.py:198
  206.6 10.4 %scatter.757 = f32[4,19,18,18,18]{4,3,2,0,1:T(8,128)} dynamic-update-slice(f32[4,19,18,18,18]{4,3,2,0,1:T(8,128)} %scatter.756, f32[4,1,16,1,16]{4,3,2,0,1:T(1,128)S(1)} %bitcast.1380, s32[]{:T(128)} %constant.5119.clone.1..sunk, s32[]{:T(128)} %constant.5084.clone.1..sunk, s32[]{:T(128)} %constant.5121.clone.1..sunk.1, s32[]{:T(128)} %constant.5081.clone.1..sunk, s32[]{:T(128)} %constant.5121.clone.1..sunk.1) | dynamic-update-slice | bytes 8196 | tf_op jit(solution)/shard_map/while/body/scatter | solution.py:213
  217.0 10.4 %scatter.758 = f32[4,19,18,18,18]{4,3,2,0,1:T(8,128)} dynamic-update-slice(f32[4,19,18,18,18]{4,3,2,0,1:T(8,128)} %scatter.757, f32[4,1,16,1,16]{4,3,2,0,1:T(1,128)S(1)} %bitcast.1376, s32[]{:T(128)} %constant.5119.clone.1..sunk, s32[]{:T(128)} %constant.5081.clone.1..sunk, s32[]{:T(128)} %constant.5121.clone.1..sunk.1, s32[]{:T(128)} %constant.5081.clone.1..sunk, s32[]{:T(128)} %constant.5121.clone.1..sunk.1) | dynamic-update-slice | bytes 8196 | tf_op jit(solution)/shard_map/while/body/scatter | solution.py:213
  238.1 10.4 %scatter.760 = f32[4,19,18,18,18]{4,3,2,0,1:T(8,128)} dynamic-update-slice(f32[4,19,18,18,18]{4,3,2,0,1:T(8,128)} %scatter.759, f32[4,1,16,1,16]{4,3,2,0,1:T(1,128)S(1)} %bitcast.1389, s32[]{:T(128)} %constant.5119.clone.1..sunk, s32[]{:T(128)} %constant.5122.clone.1..sunk, s32[]{:T(128)} %constant.5121.clone.1..sunk.1, s32[]{:T(128)} %constant.5119.clone.1..sunk, s32[]{:T(128)} %constant.5121.clone.1..sunk.1) | dynamic-update-slice | bytes 8196 | tf_op jit(solution)/shard_map/while/body/scatter | solution.py:213
  248.5 10.4 %scatter.761 = f32[4,19,18,18,18]{4,3,2,0,1:T(8,128)} dynamic-update-slice(f32[4,19,18,18,18]{4,3,2,0,1:T(8,128)} %scatter.760, f32[4,1,16,1,16]{4,3,2,0,1:T(1,128)S(1)} %bitcast.1385, s32[]{:T(128)} %constant.5119.clone.1..sunk, s32[]{:T(128)} %constant.5087.clone.1..sunk, s32[]{:T(128)} %constant.5121.clone.1..sunk.1, s32[]{:T(128)} %constant.5119.clone.1..sunk, s32[]{:T(128)} %constant.5121.clone.1..sunk.1) | dynamic-update-slice | bytes 8196 | tf_op jit(solution)/shard_map/while/body/scatter | solution.py:213
  279.9 10.4 %scatter.764 = f32[4,19,18,18,18]{4,3,2,0,1:T(8,128)} dynamic-update-slice(f32[4,19,18,18,18]{4,3,2,0,1:T(8,128)} %scatter.763, f32[4,1,16,1,16]{4,3,2,0,1:T(1,128)S(1)} %bitcast.1373, s32[]{:T(128)} %constant.5119.clone.1..sunk, s32[]{:T(128)} %constant.5095.clone.1..sunk, s32[]{:T(128)} %constant.5121.clone.1..sunk.1, s32[]{:T(128)} %constant.5119.clone.1..sunk, s32[]{:T(128)} %constant.5121.clone.1..sunk.1) | dynamic-update-slice | bytes 8196 | tf_op jit(solution)/shard_map/while/body/scatter | solution.py:213
  291.0 12.9 %scatter.765 = f32[4,19,18,18,18]{4,3,2,0,1:T(8,128)} dynamic-update-slice(f32[4,19,18,18,18]{4,3,2,0,1:T(8,128)} %scatter.764, f32[4,1,16,16,1]{4,3,2,0,1:T(8,128)S(1)} %copy.753, s32[]{:T(128)} %constant.5119.clone.1..sunk, s32[]{:T(128)} %constant.5096.clone.1..sunk, s32[]{:T(128)} %constant.5121.clone.1..sunk.1, s32[]{:T(128)} %constant.5121.clone.1..sunk.1, s32[]{:T(128)} %constant.5081.clone.1..sunk) | dynamic-update-slice | bytes 8196 | tf_op jit(solution)/shard_map/while/body/scatter | solution.py:213
  304.3 12.5 %scatter.766 = f32[4,19,18,18,18]{4,3,2,0,1:T(8,128)} dynamic-update-slice(f32[4,19,18,18,18]{4,3,2,0,1:T(8,128)} %scatter.765, f32[4,1,16,16,1]{4,3,2,0,1:T(8,128)S(1)} %copy.754, s32[]{:T(128)} %constant.5119.clone.1..sunk, s32[]{:T(128)} %constant.5090.clone.1..sunk, s32[]{:T(128)} %constant.5121.clone.1..sunk.1, s32[]{:T(128)} %constant.5121.clone.1..sunk.1, s32[]{:T(128)} %constant.5081.clone.1..sunk) | dynamic-update-slice | bytes 8196 | tf_op jit(solution)/shard_map/while/body/scatter | solution.py:213
  317.3 12.5 %scatter.767 = f32[4,19,18,18,18]{4,3,2,0,1:T(8,128)} dynamic-update-slice(f32[4,19,18,18,18]{4,3,2,0,1:T(8,128)} %scatter.766, f32[4,1,16,16,1]{4,3,2,0,1:T(8,128)S(1)} %copy.755, s32[]{:T(128)} %constant.5119.clone.1..sunk, s32[]{:T(128)} %constant.5086.clone.1..sunk, s32[]{:T(128)} %constant.5121.clone.1..sunk.1, s32[]{:T(128)} %constant.5121.clone.1..sunk.1, s32[]{:T(128)} %constant.5081.clone.1..sunk) | dynamic-update-slice | bytes 8196 | tf_op jit(solution)/shard_map/while/body/scatter | solution.py:213
  330.3 12.5 %scatter.768 = f32[4,19,18,18,18]{4,3,2,0,1:T(8,128)} dynamic-update-slice(f32[4,19,18,18,18]{4,3,2,0,1:T(8,128)} %scatter.767, f32[4,1,16,16,1]{4,3,2,0,1:T(8,128)S(1)} %copy.756, s32[]{:T(128)} %constant.5119.clone.1..sunk, s32[]{:T(128)} %constant.5095.clone.1..sunk, s32[]{:T(128)} %constant.5121.clone.1..sunk.1, s32[]{:T(128)} %constant.5121.clone.1..sunk.1, s32[]{:T(128)} %constant.5081.clone.1..sunk) | dynamic-update-slice | bytes 8196 | tf_op jit(solution)/shard_map/while/body/scatter | solution.py:213
  343.2 12.5 %scatter.769 = f32[4,19,18,18,18]{4,3,2,0,1:T(8,128)} dynamic-update-slice(f32[4,19,18,18,18]{4,3,2,0,1:T(8,128)} %scatter.768, f32[4,1,16,16,1]{4,3,2,0,1:T(8,128)S(1)} %copy.757, s32[]{:T(128)} %constant.5119.clone.1..sunk, s32[]{:T(128)} %constant.5092.clone.1..sunk, s32[]{:T(128)} %constant.5121.clone.1..sunk.1, s32[]{:T(128)} %constant.5121.clone.1..sunk.1, s32[]{:T(128)} %constant.5081.clone.1..sunk) | dynamic-update-slice | bytes 8196 | tf_op jit(solution)/shard_map/while/body/scatter | solution.py:213
  432.8 11.2 %scatter.792 = f32[4,18,18,18]{3,2,1,0:T(8,128)S(1)} dynamic-update-slice(f32[4,18,18,18]{3,2,1,0:T(8,128)S(1)} %scatter.791, f32[4,16,16,1]{3,2,1,0:T(8,128)S(1)} %copy.771, s32[]{:T(128)} %constant.5119.clone.1..sunk, s32[]{:T(128)} %constant.5121.clone.1..sunk.1, s32[]{:T(128)} %constant.5121.clone.1..sunk.1, s32[]{:T(128)} %constant.5081.clone.1..sunk) | dynamic-update-slice | bytes 8196 | tf_op jit(solution)/shard_map/while/body/scatter | solution.py:214
  651.9 380.2 %while.193 = (s32[]{:T(128)}, f32[4,19,4096]{2,0,1:T(4,128)S(1)}, s32[]{:T(128)}, s32[4,4096]{1,0:T(4,128)S(1)}, f32[4,16,16,16]{3,2,1,0:T(8,128)S(1)}, /*index=...) while((s32[]{:T(128)}, f32[4,19,4096]{2,0,1:T(4,128)S(1)}, ...), condition=%wide.region_11.12_spmd, body=%wide.region_10.11_spmd.sunk | while | flops 950274 | bytes 42097896 | solution.py:293
  660.3 11.8 %scatter.806 = f32[4,19,18,18,18]{4,3,2,0,1:T(8,128)} pad(f32[4,19,16,16,16]{4,3,2,0,1:T(8,128)} %reshape.7442, f32[]{:T(128)} %constant.5125.clone.1..sunk.1), padding=0_0x0_0x1_1x1_1x1_1 | pad | bytes 3018116 | tf_op jit(solution)/shard_map/while/body/scatter | solution.py:198
  699.6 10.4 %scatter.817 = f32[4,19,18,18,18]{4,3,2,0,1:T(8,128)} dynamic-update-slice(f32[4,19,18,18,18]{4,3,2,0,1:T(8,128)} %scatter.816, f32[4,1,16,1,16]{4,3,2,0,1:T(1,128)S(1)} %bitcast.1390, s32[]{:T(128)} %constant.5119.clone.1..sunk.1, s32[]{:T(128)} %constant.5091.clone.1..sunk.1, s32[]{:T(128)} %constant.5121.clone.1..sunk.3, s32[]{:T(128)} %constant.5081.clone.1..sunk.1, s32[]{:T(128)} %constant.5121.clone.1..sunk.3) | dynamic-update-slice | bytes 8196 | tf_op jit(solution)/shard_map/while/body/scatter | solution.py:213
  731.0 10.4 %scatter.820 = f32[4,19,18,18,18]{4,3,2,0,1:T(8,128)} dynamic-update-slice(f32[4,19,18,18,18]{4,3,2,0,1:T(8,128)} %scatter.819, f32[4,1,16,1,16]{4,3,2,0,1:T(1,128)S(1)} %bitcast.1378, s32[]{:T(128)} %constant.5119.clone.1..sunk.1, s32[]{:T(128)} %constant.5081.clone.1..sunk.1, s32[]{:T(128)} %constant.5121.clone.1..sunk.3, s32[]{:T(128)} %constant.5081.clone.1..sunk.1, s32[]{:T(128)} %constant.5121.clone.1..sunk.3) | dynamic-update-slice | bytes 8196 | tf_op jit(solution)/shard_map/while/body/scatter | solution.py:213
  741.4 10.4 %scatter.821 = f32[4,19,18,18,18]{4,3,2,0,1:T(8,128)} dynamic-update-slice(f32[4,19,18,18,18]{4,3,2,0,1:T(8,128)} %scatter.820, f32[4,1,16,1,16]{4,3,2,0,1:T(1,128)S(1)} %bitcast.1374, s32[]{:T(128)} %constant.5119.clone.1..sunk.1, s32[]{:T(128)} %constant.5092.clone.1..sunk.1, s32[]{:T(128)} %constant.5121.clone.1..sunk.3, s32[]{:T(128)} %constant.5081.clone.1..sunk.1, s32[]{:T(128)} %constant.5121.clone.1..sunk.3) | dynamic-update-slice | bytes 8196 | tf_op jit(solution)/shard_map/while/body/scatter | solution.py:213
  804.9 12.7 %scatter.827 = f32[4,19,18,18,18]{4,3,2,0,1:T(8,128)} dynamic-update-slice(f32[4,19,18,18,18]{4,3,2,0,1:T(8,128)} %scatter.826, f32[4,1,16,16,1]{4,3,2,0,1:T(8,128)S(1)} %copy.781, s32[]{:T(128)} %constant.5119.clone.1..sunk.1, s32[]{:T(128)} %constant.5096.clone.1..sunk.1, s32[]{:T(128)} %constant.5121.clone.1..sunk.3, s32[]{:T(128)} %constant.5121.clone.1..sunk.3, s32[]{:T(128)} %constant.5081.clone.1..sunk.1) | dynamic-update-slice | bytes 8196 | tf_op jit(solution)/shard_map/while/body/scatter | solution.py:213
  818.0 12.5 %scatter.828 = f32[4,19,18,18,18]{4,3,2,0,1:T(8,128)} dynamic-update-slice(f32[4,19,18,18,18]{4,3,2,0,1:T(8,128)} %scatter.827, f32[4,1,16,16,1]{4,3,2,0,1:T(8,128)S(1)} %copy.782, s32[]{:T(128)} %constant.5119.clone.1..sunk.1, s32[]{:T(128)} %constant.5090.clone.1..sunk.1, s32[]{:T(128)} %constant.5121.clone.1..sunk.3, s32[]{:T(128)} %constant.5121.clone.1..sunk.3, s32[]{:T(128)} %constant.5081.clone.1..sunk.1) | dynamic-update-slice | bytes 8196 | tf_op jit(solution)/shard_map/while/body/scatter | solution.py:213
  831.0 12.5 %scatter.829 = f32[4,19,18,18,18]{4,3,2,0,1:T(8,128)} dynamic-update-slice(f32[4,19,18,18,18]{4,3,2,0,1:T(8,128)} %scatter.828, f32[4,1,16,16,1]{4,3,2,0,1:T(8,128)S(1)} %copy.783, s32[]{:T(128)} %constant.5119.clone.1..sunk.1, s32[]{:T(128)} %constant.5086.clone.1..sunk.1, s32[]{:T(128)} %constant.5121.clone.1..sunk.3, s32[]{:T(128)} %constant.5121.clone.1..sunk.3, s32[]{:T(128)} %constant.5081.clone.1..sunk.1) | dynamic-update-slice | bytes 8196 | tf_op jit(solution)/shard_map/while/body/scatter | solution.py:213
  844.0 12.5 %scatter.830 = f32[4,19,18,18,18]{4,3,2,0,1:T(8,128)} dynamic-update-slice(f32[4,19,18,18,18]{4,3,2,0,1:T(8,128)} %scatter.829, f32[4,1,16,16,1]{4,3,2,0,1:T(8,128)S(1)} %copy.784, s32[]{:T(128)} %constant.5119.clone.1..sunk.1, s32[]{:T(128)} %constant.5095.clone.1..sunk.1, s32[]{:T(128)} %constant.5121.clone.1..sunk.3, s32[]{:T(128)} %constant.5121.clone.1..sunk.3, s32[]{:T(128)} %constant.5081.clone.1..sunk.1) | dynamic-update-slice | bytes 8196 | tf_op jit(solution)/shard_map/while/body/scatter | solution.py:213
  856.9 12.5 %scatter.831 = f32[4,19,18,18,18]{4,3,2,0,1:T(8,128)} dynamic-update-slice(f32[4,19,18,18,18]{4,3,2,0,1:T(8,128)} %scatter.830, f32[4,1,16,16,1]{4,3,2,0,1:T(8,128)S(1)} %copy.785, s32[]{:T(128)} %constant.5119.clone.1..sunk.1, s32[]{:T(128)} %constant.5092.clone.1..sunk.1, s32[]{:T(128)} %constant.5121.clone.1..sunk.3, s32[]{:T(128)} %constant.5121.clone.1..sunk.3, s32[]{:T(128)} %constant.5081.clone.1..sunk.1) | dynamic-update-slice | bytes 8196 | tf_op jit(solution)/shard_map/while/body/scatter | solution.py:213
  946.5 11.2 %scatter.854 = f32[4,18,18,18]{3,2,1,0:T(8,128)S(1)} dynamic-update-slice(f32[4,18,18,18]{3,2,1,0:T(8,128)S(1)} %scatter.853, f32[4,16,16,1]{3,2,1,0:T(8,128)S(1)} %copy.799, s32[]{:T(128)} %constant.5119.clone.1..sunk.1, s32[]{:T(128)} %constant.5121.clone.1..sunk.3, s32[]{:T(128)} %constant.5121.clone.1..sunk.3, s32[]{:T(128)} %constant.5081.clone.1..sunk.1) | dynamic-update-slice | bytes 8196 | tf_op jit(solution)/shard_map/while/body/scatter | solution.py:214
  (922 shorter events, 770.1 us)
Async XLA Ops:
  4.2 48.0 %copy-start.64 = (f32[4,1,16]{2,1,0:T(1,128)}, f32[4,1,16]{2,1,0:T(1,128)S(1)}, u32[]{:S(2)}) copy-start(f32[4,1,16]{2,1,0:T(1,128)S(1)} %get-tuple-element.3506) | copy-start | bytes 772
  4.2 48.0 %copy-start.60 = (f32[4,1,16]{2,1,0:T(1,128)}, f32[4,1,16]{2,1,0:T(1,128)S(1)}, u32[]{:S(2)}) copy-start(f32[4,1,16]{2,1,0:T(1,128)S(1)} %get-tuple-element.3505) | copy-start | bytes 772
  4.4 47.9 %copy-start.42 = (f32[4,16]{1,0:T(4,128)}, f32[4,16]{1,0:T(4,128)S(1)}, u32[]{:S(2)}) copy-start(f32[4,16]{1,0:T(4,128)S(1)} %get-tuple-element.3170) | copy-start | bytes 772
  4.4 48.0 %copy-start.44 = (f32[4,16]{1,0:T(4,128)}, f32[4,16]{1,0:T(4,128)S(1)}, u32[]{:S(2)}) copy-start(f32[4,16]{1,0:T(4,128)S(1)} %get-tuple-element.3169) | copy-start | bytes 772
  4.4 47.9 %copy-start.62 = (f32[4,1,16]{2,1,0:T(1,128)}, f32[4,1,16]{2,1,0:T(1,128)S(1)}, u32[]{:S(2)}) copy-start(f32[4,1,16]{2,1,0:T(1,128)S(1)} %get-tuple-element.3504) | copy-start | bytes 772
  4.4 47.9 %copy-start.58 = (f32[4,1,16]{2,1,0:T(1,128)}, f32[4,1,16]{2,1,0:T(1,128)S(1)}, u32[]{:S(2)}) copy-start(f32[4,1,16]{2,1,0:T(1,128)S(1)} %get-tuple-element.3503) | copy-start | bytes 772
  4.6 47.8 %copy-start.46 = (f32[4,16]{1,0:T(4,128)}, f32[4,16]{1,0:T(4,128)S(1)}, u32[]{:S(2)}) copy-start(f32[4,16]{1,0:T(4,128)S(1)} %get-tuple-element.3168) | copy-start | bytes 772
  4.6 47.8 %copy-start.48 = (f32[4,16]{1,0:T(4,128)}, f32[4,16]{1,0:T(4,128)S(1)}, u32[]{:S(2)}) copy-start(f32[4,16]{1,0:T(4,128)S(1)} %get-tuple-element.3167) | copy-start | bytes 772
  65.9 29.1 %copy-start.35 = (f32[4,1,1,256]{3,0,2,1:T(4,128)}, f32[4,1,1,256]{3,0,2,1:T(4,128)S(1)}, u32[]{:S(2)}) copy-start(f32[4,1,1,256]{3,0,2,1:T(4,128)S(1)} %concatenate.901) | copy-start | bytes 12292
  69.1 27.2 %copy-start.37 = (f32[4,1,1,256]{3,0,2,1:T(4,128)}, f32[4,1,1,256]{3,0,2,1:T(4,128)S(1)}, u32[]{:S(2)}) copy-start(f32[4,1,1,256]{3,0,2,1:T(4,128)S(1)} %concatenate.904) | copy-start | bytes 12292
  108.7 19.7 %collective-permute-start = (f32[1,4,1664]{2,1,0:T(4,128)S(1)}, f32[1,4,1664]{2,1,0:T(4,128)S(1)}, u32[]{:S(2)}, u32[]{:S(2)}) collective-permute-start(f32[1,4,1664]{2,1,0:T(4,128)S(1)} %maximum_bitcast_fusion), channel_id=1, source_target_pairs={{1,0},{2,1},{3,2},{4,3},{5,4},{6,5},{7,6},{9,8},{10,9},{11,10},{12... | collective-permute-start | bytes 79880 | tf_op jit(solution)/shard_map/ppermute | solution.py:19
  111.6 16.8 %collective-permute-start.1 = (f32[1,4,1664]{2,1,0:T(4,128)S(1)}, f32[1,4,1664]{2,1,0:T(4,128)S(1)}, u32[]{:S(2)}, u32[]{:S(2)}) collective-permute-start(f32[1,4,1664]{2,1,0:T(4,128)S(1)} %maximum_bitcast_fusion.1), channel_id=1, source_target_pairs={{0,1},{1,2},{2,3},{3,4},{4,5},{5,6},{6,7},{8,9},{9,10},{10,11},{11... | collective-permute-start | bytes 79880 | tf_op jit(solution)/shard_map/ppermute | solution.py:18
  138.2 384.8 %copy-start.68 = (f32[4,19,1]{1,0,2:T(4,128)S(1)}, f32[4,19,1]{1,0,2:T(4,128)}, u32[]{:S(2)}) copy-start(f32[4,19,1]{1,0,2:T(4,128)} %constant.5204) | copy-start | bytes 916
  146.5 25.2 %copy-start.20 = (f32[4,1,6,256]{3,0,2,1:T(4,128)S(1)}, f32[4,1,6,256]{3,0,2,1:T(4,128)}, u32[]{:S(2)}) copy-start(f32[4,1,6,256]{3,0,2,1:T(4,128)} %get-tuple-element.3882) | copy-start | bytes 73732 | tf_op jit(solution)/shard_map/while
  146.5 39.0 %copy-start.18 = (f32[4,1,6,256]{3,0,2,1:T(4,128)S(1)}, f32[4,1,6,256]{3,0,2,1:T(4,128)}, u32[]{:S(2)}) copy-start(f32[4,1,6,256]{3,0,2,1:T(4,128)} %get-tuple-element.3888) | copy-start | bytes 73732 | tf_op jit(solution)/shard_map/while
  615.6 20.9 %copy-start.128 = (pred[4]{0:T(512)(128)(4,1)S(1)}, pred[4]{0:T(512)(128)(4,1)}, u32[]{:S(2)}) copy-start(pred[4]{0:T(512)(128)(4,1)} %copy-done.127) | copy-start | bytes 16
  615.6 20.9 %copy-start.106 = (pred[4]{0:T(512)(128)(4,1)S(1)}, pred[4]{0:T(512)(128)(4,1)}, u32[]{:S(2)}) copy-start(pred[4]{0:T(512)(128)(4,1)} %copy-done.105) | copy-start | bytes 16
  615.6 21.6 %copy-start.104 = (pred[4]{0:T(512)(128)(4,1)S(1)}, pred[4]{0:T(512)(128)(4,1)}, u32[]{:S(2)}) copy-start(pred[4]{0:T(512)(128)(4,1)} %copy-done.103) | copy-start | bytes 16
  615.6 22.3 %copy-start.102 = (pred[4]{0:T(512)(128)(4,1)S(1)}, pred[4]{0:T(512)(128)(4,1)}, u32[]{:S(2)}) copy-start(pred[4]{0:T(512)(128)(4,1)} %copy-done.101) | copy-start | bytes 16
  615.6 23.0 %copy-start.126 = (pred[4]{0:T(512)(128)(4,1)S(1)}, pred[4]{0:T(512)(128)(4,1)}, u32[]{:S(2)}) copy-start(pred[4]{0:T(512)(128)(4,1)} %copy-done.125) | copy-start | bytes 16
  626.4 14.6 %collective-permute-start.2 = (f32[1,4,1664]{2,1,0:T(4,128)S(1)}, f32[1,4,1664]{2,1,0:T(4,128)S(1)}, u32[]{:S(2)}, u32[]{:S(2)}) collective-permute-start(f32[1,4,1664]{2,1,0:T(4,128)S(1)} %maximum_bitcast_fusion.2), channel_id=1, source_target_pairs={{1,0},{2,1},{3,2},{4,3},{5,4},{6,5},{7,6},{9,8},{10,9},{11,10},{12... | collective-permute-start | bytes 79880 | tf_op jit(solution)/shard_map/ppermute | solution.py:19
  627.8 13.2 %collective-permute-start.3 = (f32[1,4,1664]{2,1,0:T(4,128)S(1)}, f32[1,4,1664]{2,1,0:T(4,128)S(1)}, u32[]{:S(2)}, u32[]{:S(2)}) collective-permute-start(f32[1,4,1664]{2,1,0:T(4,128)S(1)} %maximum_bitcast_fusion.3), channel_id=1, source_target_pairs={{0,1},{1,2},{2,3},{3,4},{4,5},{5,6},{6,7},{8,9},{9,10},{10,11},{11... | collective-permute-start | bytes 79880 | tf_op jit(solution)/shard_map/ppermute | solution.py:18
  660.3 25.4 %copy-start.21 = (f32[4,1,6,256]{3,0,2,1:T(4,128)S(1)}, f32[4,1,6,256]{3,0,2,1:T(4,128)}, u32[]{:S(2)}) copy-start(f32[4,1,6,256]{3,0,2,1:T(4,128)} %get-tuple-element.3979) | copy-start | bytes 73732 | tf_op jit(solution)/shard_map/while
  660.3 39.2 %copy-start.19 = (f32[4,1,6,256]{3,0,2,1:T(4,128)S(1)}, f32[4,1,6,256]{3,0,2,1:T(4,128)}, u32[]{:S(2)}) copy-start(f32[4,1,6,256]{3,0,2,1:T(4,128)} %get-tuple-element.3985) | copy-start | bytes 73732 | tf_op jit(solution)/shard_map/while
  (123 other events, 985.8 us)
where the time goes:
time: 1050 us; the launch traced here: 1030 us
  local copies, waits for them, and re-layouts  930 us (89%)
  other arithmetic  67.3 us (6%)
  matrix products  12 us (1%)
  starting transfers between devices  11.4 us (1%)
    scatter x60, local copies, waits for them, and re-layouts, propagate(): padded.at[(slice(None), lane_two) + spatial].set(face_values[:, member_num])  429 us
    scatter x12, local copies, waits for them, and re-layouts, propagate(): open_mask = open_mask.at[(slice(None),) + spatial].set(face_values[:, 5])  72.5 us
    scatter x24, local copies, waits for them, and re-layouts, propagate(): padded.at[(slice(None), opposite[lane_num]) + spatial]  61 us
    squeeze x6, local copies, waits for them, and re-layouts, make_slabs(): lax.index_in_dim(blocked, layer_index, axis_num + 2, keepdims=False)  41.3 us
    another operation x40, local copies, waits for them, and re-layouts, propagate(): jnp.stack(arrived_list, 1).reshape(block_count, 19, BLOCK * BLOCK * BLOCK)  39.5 us
    select_n x8, other arithmetic, propagate(): jnp.where(open_here > 0, pulled, blocked[:, opposite[lane_num]])  39.1 us
    another operation x68, local copies, waits for them, and re-layouts  33.8 us
    scatter x24, local copies, waits for them, and re-layouts, propagate(): open_mask.at[(slice(None),) + spatial].set(rim_edges[:, edge_num, 1])  31.9 us
  transfers between devices with their start and end apart: 4, of which 0 were waited for; matrix products, arithmetic and copies ran while one was open for 2% of the time, Pallas kernels for 0%

commit v1 on v0

v1 whole, which is shorter than its diff:
```python
import functools

import jax
import jax.numpy as jnp
import numpy as np
from jax import lax
from jax.experimental import pallas as pl
from jax.experimental.pallas import tpu as pltpu
from jax.sharding import PartitionSpec as P

LANES = 128
ROWS = 32
PAD = 8
HEIGHT = ROWS + 2 * PAD
CLOSED = 1.0e30
LIMIT = 1.0e29


def directions():
    listed = [(0, 0, 0)]
    for axis in range(3):
        for sign in (1, -1):
            vector = [0, 0, 0]
            vector[axis] = sign
            listed.append(tuple(vector))
    for one, two in ((0, 1), (0, 2), (1, 2)):
        for sign_one in (1, -1):
            for sign_two in (1, -1):
                vector = [0, 0, 0]
                vector[one] = sign_one
                vector[two] = sign_two
                listed.append(tuple(vector))
    return listed


C = directions()
INDEX = {vector: num for num, vector in enumerate(C)}
OPP = [INDEX[tuple(-part for part in vector)] for vector in C]
FLAT = ((0, 0), (1, 0), (-1, 0), (0, 1), (0, -1))
UPWARD = [INDEX[(a, b, 1)] for a, b in FLAT]
DOWNWARD = [INDEX[(a, b, -1)] for a, b in FLAT]
N_MOM = 9
N_MSG = N_MOM + 5 + 1


def column(vector):
    return INDEX[vector] - 1


def moments(g):
    sx, dx = g[1] + g[2], g[1] - g[2]
    sy, dy = g[3] + g[4], g[3] - g[4]
    sz, dz = g[5] + g[6], g[5] - g[6]
    pairs = []
    for base in (7, 11, 15):
        pairs.append((g[base] + g[base + 3], g[base] - g[base + 3], g[base + 1] + g[base + 2], g[base + 1] - g[base + 2]))
    (xys, xyd, xyt, xye), (xzs, xzd, xzt, xze), (yzs, yzd, yzt, yze) = pairs
    exy, exz, eyz = xys + xyt, xzs + xzt, yzs + yzt
    rho = g[0] * (1.0 / 3.0) + (sx + sy + sz) * (1.0 / 18.0) + (exy + exz + eyz) * (1.0 / 36.0)
    ux = dx * (1.0 / 6.0) + (xyd + xye + xzd + xze) * (1.0 / 12.0)
    uy = dy * (1.0 / 6.0) + (xyd - xye + yzd + yze) * (1.0 / 12.0)
    uz = dz * (1.0 / 6.0) + (xzd - xze + yzd - yze) * (1.0 / 12.0)
    qxy = (xys - xyt) * 0.25
    qxz = (xzs - xzt) * 0.25
    qyz = (yzs - yzt) * 0.25
    gxz = (sx - sz) * 0.5 + (exy - eyz) * 0.25
    gyz = (sy - sz) * 0.5 + (exy - exz) * 0.25
    return [rho, ux, uy, uz, qxy, qxz, qyz, gxz, gyz]


def add_crossing(mom, e, sign):
    ez, xp, xm, yp, ym = e
    rho, ux, uy, uz, qxy, qxz, qyz, gxz, gyz = mom
    xs, xd, ys, yd = xp + xm, xp - xm, yp + ym, yp - ym
    four = xs + ys
    half = ez * 0.5
    return [
        rho + ez * (1.0 / 18.0) + four * (1.0 / 36.0),
        ux + xd * (1.0 / 12.0),
        uy + yd * (1.0 / 12.0),
        uz + sign * (ez * (1.0 / 6.0) + four * (1.0 / 12.0)),
        qxy,
        qxz + (sign * 0.25) * xd,
        qyz + (sign * 0.25) * yd,
        gxz - ys * 0.25 - half,
        gyz - xs * 0.25 - half,
    ]


def collided_from(mom, tau, wanted=None):
    rho, ux, uy, uz, qxy, qxz, qyz, gxz, gyz = mom
    xx, yy, zz = ux * ux, uy * uy, uz * uz
    base = rho - (xx + yy + zz) * (1.0 / 6.0)
    hx = gxz - (xx - zz)
    hy = gyz - (yy - zz)
    third = tau * (1.0 / 3.0)
    shear = {
        (0,): third * (hx + hx - hy),
        (1,): third * (hy + hy - hx),
        (2,): -third * (hx + hy),
        (0, 1): tau * (qxy - ux * uy),
        (0, 2): tau * (qxz - ux * uz),
        (1, 2): tau * (qyz - uy * uz),
    }
    u = (ux, uy, uz)
    out = {0: base}
    wanted = range(19) if wanted is None else wanted
    for num in wanted:
        if num in out:
            continue
        vector = C[num]
        axes = tuple(axis for axis in range(3) if vector[axis])
        if len(axes) == 1:
            speed = u[axes[0]]
            lead = vector[axes[0]]
            even = base + speed * speed * 0.5 + shear[axes]
        else:
            first, second = vector[axes[0]], vector[axes[1]]
            speed = u[axes[0]] + u[axes[1]] if first == second else u[axes[0]] - u[axes[1]]
            lead = first
            even = base + speed * speed * 0.5
            even = even + shear[axes] if first == second else even - shear[axes]
        plus = num if lead > 0 else OPP[num]
        out[plus] = even + speed
        out[OPP[plus]] = even - speed
    return out


def turned(value, shift):
    shift = shift % LANES
    return value if shift == 0 else pltpu.roll(value, shift, 1)


def iotas():
    lane = lax.broadcasted_iota(jnp.int32, (8, LANES), 1)
    row = lax.broadcasted_iota(jnp.int32, (8, LANES), 0)
    return row, lane


def fill_closed(pops, slots):
    blank = jnp.full((8, LANES), CLOSED, jnp.float32)
    for num in range(1, 19):
        if C[num][0] or C[num][1]:
            for group in range(4):
                pops[num, slots, PAD + 8 * group : PAD + 8 * group + 8, :] = blank


def plane_slot(nbr, block, vector, slots):
    entry = nbr[block, column(vector)]
    return jnp.where(entry >= 0, entry - slots, slots)


def fill_x_rims(pops, nbr, slots):
    for block in range(slots):
        before = plane_slot(nbr, block, (-1, 0, 0), slots)
        after = plane_slot(nbr, block, (1, 0, 0), slots)
        for num in range(1, 19):
            if C[num][0] > 0:
                pops[num, block, PAD - 2 : PAD, :] = pops[num, before, PAD + ROWS - 2 : PAD + ROWS, :]
            elif C[num][0] < 0:
                pops[num, block, PAD + ROWS : PAD + ROWS + 2, :] = pops[num, after, PAD : PAD + 2, :]


def pulled(pops, nbr, block, group, num, slots, row, lane):
    cx, cy, cz = C[num]
    start = PAD + 8 * group - 2 * cx
    value = pops[num, block, start : start + 8, :]
    if cy:
        own = pops[num, block, start - cy : start - cy + 8, :]
        beside = plane_slot(nbr, block, (0, -cy, 0), slots)
        other = pops[num, beside, start + cy : start + cy + 8, :]
        if cx and group == (0 if cx > 0 else 3):
            corner = plane_slot(nbr, block, (-cx, -cy, 0), slots)
            at = start + cy + (ROWS if cx > 0 else -ROWS)
            edge = pops[num, corner, at : at + 8, :]
            other = jnp.where((row < 2) if cx > 0 else (row >= 6), edge, other)
        high = (row & 1) == 1
        crossing = jnp.where(high, own, other) if cy > 0 else jnp.where(high, other, own)
        value = jnp.where((lane >= 112) if cy > 0 else (lane < 16), crossing, value)
    return turned(value, 16 * cy + cz)


def slot_vector(entries, base, lane, slots):
    own = (lane >> 2) & 3
    found = jnp.full((8, LANES), -1, jnp.int32)
    for slot in range(slots):
        entry = entries[slot]
        found = jnp.where((own == slot) & (entry >= 0), entry - base, found)
    return found


def naming_vector(entries, base, lane, slots):
    own = (lane >> 2) & 3
    found = jnp.full((8, LANES), -1, jnp.int32)
    for block in range(slots):
        found = jnp.where(own == entries[block] - base, block, found)
    return found


def face_sources(flat, straight, corner, row, lane):
    cx, cy = flat
    up = (lane >> 4) & 7
    part = lane & 3
    if cx:
        edge_row = (row < 2) if cx > 0 else (row >= 6)
        leaves = edge_row & (part == (0 if cx > 0 else 3))
        part = jnp.where(edge_row, (part - cx) & 3, part)
        slot = jnp.where(leaves, corner, straight)
    elif cy:
        at = up == (0 if cy > 0 else 7)
        leaves = at & ((row & 1) == (0 if cy > 0 else 1))
        up = (up - cy) & 7
        slot = jnp.where(leaves, corner, straight)
    else:
        slot = straight
    return jnp.where(slot >= 0, up * 16 + slot * 4 + part, -1)


def face_pull(plane, flat, source, row, lane):
    cx, cy = flat
    if cx:
        plane = pltpu.roll(plane, (2 * cx) % 8, 0)
    elif cy:
        swapped = jnp.where((row & 1) == 1, pltpu.roll(plane, 1, 0), pltpu.roll(plane, 7, 0))
        plane = jnp.where((lane >= 112) if cy > 0 else (lane < 16), swapped, plane)
    moved = jnp.take_along_axis(plane, jnp.maximum(source, 0), axis=1)
    return jnp.where(source >= 0, moved, CLOSED)


def stage_flags(flags, flag_tiles, slots):
    for tile in range(ROWS):
        flag_tiles[8 * tile : 8 * tile + slots, :] = flags[:, LANES * tile : LANES * tile + LANES]


def wet(flag_tiles, block, group):
    return flag_tiles[pl.ds(64 * group + block, 8, stride=8), :] > 0


def tile_row(block, num, tile):
    return ((block * 3 + num // 8) * ROWS + tile) * 8


def first_kernel(pop_hbm, flags, nbr, rate, mom_out, msg_even, msg_odd, raw, tiles, flag_tiles, pops, sides, sems):
    slots = flags.shape[0]
    copies = [pltpu.make_async_copy(pop_hbm.at[b], raw.at[b], sems.at[b]) for b in range(slots)]
    for copy in copies:
        copy.start()
    row, lane = iotas()
    stage_flags(flags, flag_tiles, slots)
    fill_closed(pops, slots)
    depth = lane & 15
    for block in range(slots):
        copies[block].wait()
        for first in (0, 8, 16):
            high = min(first + 8, 19)
            for tile in range(ROWS):
                at = tile_row(block, first, tile)
                tiles[at : at + high - first, :] = raw[block, first:high, LANES * tile : LANES * tile + LANES]
        tau = 1.0 - rate[block]
        for group in range(4):
            g = [tiles[pl.ds(tile_row(block, num, 8 * group) + num % 8, 8, stride=8), :] for num in range(19)]
            h = collided_from(moments(g), tau)
            fluid = wet(flag_tiles, block, group)
            spot = depth == 4 * block + group
            for num in range(19):
                value = jnp.where(fluid, h[num], CLOSED)
                pops[num, block, PAD + 8 * group : PAD + 8 * group + 8, :] = value
                if num in UPWARD:
                    pltpu.store(sides.at[0, N_MOM + UPWARD.index(num)], turned(value, 4 * block + group - 15), mask=spot)
                if num in DOWNWARD:
                    pltpu.store(sides.at[1, N_MOM + DOWNWARD.index(num)], turned(value, 4 * block + group), mask=spot)
    fill_x_rims(pops, nbr, slots)
    for block in range(slots):
        for group in range(4):
            g = []
            for num in range(19):
                if num == 0:
                    g.append(pops[0, block, PAD + 8 * group : PAD + 8 * group + 8, :])
                    continue
                value = pulled(pops, nbr, block, group, num, slots, row, lane)
                back = pops[OPP[num], block, PAD + 8 * group : PAD + 8 * group + 8, :]
                value = jnp.where(value < LIMIT, value, back)
                if C[num][2]:
                    value = jnp.where(depth == (0 if C[num][2] > 0 else 15), 0.0, value)
                g.append(value)
            mom = moments(g)
            spot = depth == 4 * block + group
            for at in range(N_MOM):
                mom_out[at, block, 8 * group : 8 * group + 8, :] = mom[at]
                pltpu.store(sides.at[0, at], turned(mom[at], 4 * block + group - 15), mask=spot)
                pltpu.store(sides.at[1, at], turned(mom[at], 4 * block + group), mask=spot)
    own = (lane >> 2) & 3
    tau = jnp.zeros((8, LANES), jnp.float32)
    for block in range(slots):
        tau = jnp.where(own == block, 1.0 - rate[block], tau)
    odd = lax.axis_index("dev") % 2 == 1
    for at in range(N_MSG):
        upper = tau if at == N_MSG - 1 else sides[0, at]
        lower = tau if at == N_MSG - 1 else sides[1, at]
        msg_even[at] = jnp.where(odd, lower, upper)
        msg_odd[at] = jnp.where(odd, upper, lower)


def second_kernel(
    pop_hbm, flags, nbr, rate, mom_in, msg_even, msg_odd, got_even, got_odd, out_hbm,
    raw, tiles, flag_tiles, pops, faces, sems, out_sems,
):
    slots = flags.shape[0]
    copies = [pltpu.make_async_copy(pop_hbm.at[b], raw.at[b], sems.at[b]) for b in range(slots)]
    for copy in copies:
        copy.start()
    row, lane = iotas()
    depth = lane & 15
    stage_flags(flags, flag_tiles, slots)
    fill_closed(pops, slots)
    odd = lax.axis_index("dev") % 2 == 1

    def upper_own(at):
        return jnp.where(odd, msg_odd[at], msg_even[at])

    def lower_own(at):
        return jnp.where(odd, msg_even[at], msg_odd[at])

    def upper_got(at):
        return jnp.where(odd, got_odd[at], got_even[at])

    def lower_got(at):
        return jnp.where(odd, got_even[at], got_odd[at])

    for side, sign in ((0, 1), (1, -1)):
        own_msg, got_msg = (upper_own, upper_got) if sign > 0 else (lower_own, lower_got)
        base = (sign + 1) * slots
        inward = DOWNWARD if sign > 0 else UPWARD
        outward = UPWARD if sign > 0 else DOWNWARD
        straight = slot_vector([nbr[b, column((0, 0, sign))] for b in range(slots)], base, lane, slots)
        naming = naming_vector([nbr[b, column((0, 0, sign))] for b in range(slots)], base, lane, slots)
        own_out = [own_msg(N_MOM + at) for at in range(5)]
        got_in = [got_msg(N_MOM + at) for at in range(5)]
        entering, leaving, sources = [], [], []
        for at, (cx, cy) in enumerate(FLAT):
            if cx or cy:
                toward = [nbr[b, column((-cx, -cy, sign))] for b in range(slots)]
                corner = slot_vector(toward, base, lane, slots)
                away = [nbr[b, column((cx, cy, sign))] for b in range(slots)]
                far_corner = naming_vector(away, base, lane, slots)
            else:
                corner, far_corner = straight, naming
            source = face_sources((cx, cy), straight, corner, row, lane)
            sources.append(source)
            value = face_pull(got_in[at], (cx, cy), source, row, lane)
            mirror = FLAT.index((-cx, -cy))
            entering.append(jnp.where(value < LIMIT, value, own_out[mirror]))
            far = face_sources((cx, cy), naming, far_corner, row, lane)
            value = face_pull(own_out[at], (cx, cy), far, row, lane)
            leaving.append(jnp.where(value < LIMIT, value, got_in[mirror]))
        for at in range(5):
            faces[side, at] = entering[at]
        mom = add_crossing([got_msg(at) for at in range(N_MOM)], leaving, float(sign))
        h = collided_from(mom, got_msg(N_MSG - 1), inward)
        for at, flat in enumerate(FLAT):
            value = jnp.where(got_in[0] < LIMIT, h[inward[at]], CLOSED)
            faces[side, 5 + at] = face_pull(value, flat, sources[at], row, lane)

    top, bottom = depth == 15, depth == 0
    sign = jnp.where(bottom, 1.0, -1.0)
    for block in range(slots):
        tau = 1.0 - rate[block]
        for group in range(4):
            shift = 4 * block + group
            crossing = []
            for at in range(5):
                value = jnp.where(top, turned(faces[0, at], 15 - shift), 0.0)
                crossing.append(jnp.where(bottom, turned(faces[1, at], -shift), value))
            mom = [mom_in[at, block, 8 * group : 8 * group + 8, :] for at in range(N_MOM)]
            h = collided_from(add_crossing(mom, crossing, sign), tau)
            fluid = wet(flag_tiles, block, group)
            for num in range(19):
                pops[num, block, PAD + 8 * group : PAD + 8 * group + 8, :] = jnp.where(fluid, h[num], CLOSED)
    fill_x_rims(pops, nbr, slots)
    outs = [pltpu.make_async_copy(raw.at[b], out_hbm.at[b], out_sems.at[b]) for b in range(slots)]
    for block in range(slots):
        for group in range(4):
            shift = 4 * block + group
            for num in range(19):
                back = pops[OPP[num], block, PAD + 8 * group : PAD + 8 * group + 8, :]
                if num:
                    cx, cy, cz = C[num]
                    value = pulled(pops, nbr, block, group, num, slots, row, lane)
                    if cz > 0:
                        value = jnp.where(bottom, turned(faces[1, 5 + UPWARD.index(num)], -shift), value)
                    elif cz < 0:
                        value = jnp.where(top, turned(faces[0, 5 + DOWNWARD.index(num)], 15 - shift), value)
                    value = jnp.where(value < LIMIT, value, back)
                else:
                    value = back
                tiles[pl.ds(tile_row(block, num, 8 * group) + num % 8, 8, stride=8), :] = value
        copies[block].wait()
        for tile in range(ROWS):
            fluid = flags[block : block + 1, LANES * tile : LANES * tile + LANES] > 0
            for first in (0, 8, 16):
                high = min(first + 8, 19)
                at = tile_row(block, first, tile)
                where = (block, slice(first, high), slice(LANES * tile, LANES * tile + LANES))
                raw[where] = jnp.where(fluid, tiles[at : at + high - first, :], raw[where])
        outs[block].start()
    for block in range(slots):
        outs[block].wait()


def body(populations, fluid_flags, neighbours, relax_rate):
    slots, _, cells = populations.shape
    assert cells == ROWS * LANES and slots <= 4
    peers = lax.axis_size("dev")
    assert peers % 2 == 0
    vmem = pl.BlockSpec(memory_space=pltpu.VMEM)
    smem = pl.BlockSpec(memory_space=pltpu.SMEM)
    anywhere = pl.BlockSpec(memory_space=pl.ANY)
    face = (8, LANES)
    raw = pltpu.VMEM((slots, 19, cells), jnp.float32)
    tiles = pltpu.VMEM((slots * 3 * ROWS * 8, LANES), jnp.float32)
    flag_tiles = pltpu.VMEM((8 * ROWS, LANES), jnp.int32)
    pops = pltpu.VMEM((19, slots + 1, HEIGHT, LANES), jnp.float32)
    message = jax.ShapeDtypeStruct((N_MSG,) + face, jnp.float32)
    mom, msg_even, msg_odd = pl.pallas_call(
        first_kernel,
        out_shape=(jax.ShapeDtypeStruct((N_MOM, slots, ROWS, LANES), jnp.float32), message, message),
        in_specs=[anywhere, vmem, smem, smem],
        out_specs=(vmem, vmem, vmem),
        scratch_shapes=[
            raw, tiles, flag_tiles, pops,
            pltpu.VMEM((2, N_MOM + 5) + face, jnp.float32),
            pltpu.SemaphoreType.DMA((slots,)),
        ],
        name="collide_and_stream",
    )(populations, fluid_flags, neighbours, relax_rate)
    even_pairs = [(i, i ^ 1) for i in range(peers)]
    odd_pairs = [(i, (i + 1) % peers if i % 2 else (i - 1) % peers) for i in range(peers)]
    got_odd = lax.ppermute(msg_odd, "dev", odd_pairs)
    got_even = lax.ppermute(msg_even, "dev", even_pairs)
    return pl.pallas_call(
        second_kernel,
        out_shape=jax.ShapeDtypeStruct(populations.shape, jnp.float32),
        in_specs=[anywhere, vmem, smem, smem, vmem, vmem, vmem, vmem, vmem],
        out_specs=anywhere,
        scratch_shapes=[
            raw, tiles, flag_tiles, pops,
            pltpu.VMEM((2, 10) + face, jnp.float32),
            pltpu.SemaphoreType.DMA((slots,)),
            pltpu.SemaphoreType.DMA((slots,)),
        ],
        name="finish",
    )(populations, fluid_flags, neighbours, relax_rate, mom, msg_even, msg_odd, got_even, got_odd)


def solution(mesh):
    placed = (
        P(("group", "dev"), None, None),
        P(("group", "dev"), None),
        P(("group", "dev"), None),
        P(("group", "dev")),
    )
    return jax.shard_map(
        body, mesh=mesh, in_specs=placed, out_specs=P(("group", "dev"), None, None), check_vma=False
    )
```

time: 1050 us -> 22.8 us (0.02); the launches traced: 1030 us -> 22.6 us
  local copies, waits for them, and re-layouts: 930 us -> 7.05 us
  other arithmetic: 67.3 us -> 0 us
  matrix products: 12 us -> 0 us
    scatter x124 -> x0, local copies, waits for them, and re-layouts: 618 us -> none  [the longest x60 429 us: propagate(): padded.at[(slice(None), lane_two) + spatial].set(face_values[:, member_num])]
    another operation x110 -> x0, local copies, waits for them, and re-layouts: 73.3 us -> none  [the longest x40 39.5 us: propagate(): jnp.stack(arrived_list, 1).reshape(block_count, 19, BLOCK * BLOCK * BLOCK)]
    squeeze x45 -> x0, local copies, waits for them, and re-layouts: 62.2 us -> none  [the longest x6 41.3 us: make_slabs(): lax.index_in_dim(blocked, layer_index, axis_num + 2, keepdims=False)]
    gather x56 -> x0, local copies, waits for them, and re-layouts: 53.9 us -> none  [the longest x12 25.6 us: make_slabs(): lax.index_in_dim(blocked, layer_index, axis_num + 2, keepdims=False)]
    select_n x12 -> x0, other arithmetic: 43.3 us -> none  [the longest x8 39.1 us: propagate(): jnp.where(open_here > 0, pulled, blocked[:, opposite[lane_num]])]
    while x92 -> x0, local copies, waits for them, and re-layouts: 38.8 us -> none
    slice x69 -> x0, local copies, waits for them, and re-layouts: 35.3 us -> none  [the longest x4 21.9 us: make_slabs(): lax.index_in_dim(blocked, layer_index, axis_num + 2, keepdims=False)]
    reshape x18 -> x0, local copies, waits for them, and re-layouts: 18.8 us -> none  [the longest x2 14.4 us: make_slabs(): blocked = collided.reshape(block_count, 19, BLOCK, BLOCK, BLOCK)]
  transfers between devices with their start and end apart: 4 -> 2, of which waited for: 0 -> 1; matrix products, arithmetic and copies ran while one was open for 2% -> 0% of each run, Pallas kernels for 0% -> 0%
where the time goes in v1:
time: 22.8 us; the launch traced here: 22.6 us
  Pallas kernels  9.2 us (40%)
  local copies, waits for them, and re-layouts  7.05 us (31%)
  starting transfers between devices  4.1 us (18%)
  waiting for transfers between devices  2.18 us (10%)
    pallas_call x1, Pallas kernels, body(): pl.pallas_call(first_kernel, out_shape=(jax.ShapeDtypeStruct((N_MOM, slot...  4.74 us
    pallas_call x1, Pallas kernels, body(): pl.pallas_call(second_kernel, out_shape=jax.ShapeDtypeStruct(populations....  4.46 us
    unnamed x5, local copies, waits for them, and re-layouts  3.81 us
    ppermute x1, starting transfers between devices, body(): got_odd = lax.ppermute(msg_odd, 'dev', odd_pairs)  3.55 us
    pallas_call x1, local copies, waits for them, and re-layouts, body(): pl.pallas_call(second_kernel, out_shape=jax.ShapeDtypeStruct(populations....  3.25 us
    ppermute x1, waiting for transfers between devices, body(): got_odd = lax.ppermute(msg_odd, 'dev', odd_pairs)  2.18 us
    ppermute x1, starting transfers between devices, body(): got_even = lax.ppermute(msg_even, 'dev', even_pairs)  0.56 us
  transfers between devices with their start and end apart: 2, of which 1 were waited for; matrix products, arithmetic and copies ran while one was open for 0% of the time, Pallas kernels for 0%

profile of v1, /device:TPU:0, one launch (start us, length us, event | category | flops | bytes accessed | tf_op | source)
XLA Modules:
  0.0 22.6 jit_solution(5323983782842025381)
XLA Ops:
  0.0 3.2 %copy.6.pop_hbm = f32[4,19,4096]{2,1,0:T(8,128)} copy(f32[4,19,4096]{2,0,1:T(4,128)} %param.4) | data formatting | bytes 2490368 | tf_op args[0]
  3.2 4.7 %collide_and_stream.1 = (f32[9,4,32,128]{3,2,1,0:T(8,128)}, f32[15,8,128]{2,1,0:T(8,128)}, f32[15,8,128]{2,1,0:T(8,128)}) custom-call(f32[4,19,4096]{2,1,0:T(8,128)} %copy.6.pop_hbm, s32[4,4096]{1,0:T(4,128)} %flags.3, s32[4,18]{1,0:T(4,128)} %nbr.3, f32[4]{0:T(128)} %rate.3), custom_call_target="tpu_custom_call" | custom-call | tf_op jit(solution)/shard_map/collide_and_stream/pallas_call | solution.py:424
  7.9 0.6 %collective-permute-start = (f32[15,8,128]{2,1,0:T(8,128)}, f32[15,8,128]{2,1,0:T(8,128)S(1)}, u32[]{:S(2)}, u32[]{:S(2)}) collective-permute-start(f32[15,8,128]{2,1,0:T(8,128)} %get-tuple-element.9.msg_even), channel_id=1, source_target_pairs={{0,1},{1,0},{2,3},{3,2},{4,5},{5,4},{6,7},{7,6},{8,9},{9,8},{10,11... | collective-permute-start | bytes 184328 | tf_op jit(solution)/shard_map/ppermute | solution.py:439
  8.5 3.5 %collective-permute-start.1 = (f32[15,8,128]{2,1,0:T(8,128)}, f32[15,8,128]{2,1,0:T(8,128)S(1)}, u32[]{:S(2)}, u32[]{:S(2)}) collective-permute-start(f32[15,8,128]{2,1,0:T(8,128)} %get-tuple-element.10.msg_odd), channel_id=1, source_target_pairs={{0,7},{1,2},{2,1},{3,4},{4,3},{5,6},{6,5},{7,0},{8,15},{9,10},{10,... | collective-permute-start | bytes 184328 | tf_op jit(solution)/shard_map/ppermute | solution.py:438
  12.0 0.0 collective-permute-done.got_even
  12.0 0.0 copy-start
  12.0 2.2 %collective-permute-done.1.got_odd = f32[15,8,128]{2,1,0:T(8,128)S(1)} collective-permute-done((f32[15,8,128]{2,1,0:T(8,128)}, f32[15,8,128]{2,1,0:T(8,128)S(1)}, u32[]{:S(2)}, u32[]{:S(2)}) %collective-permute-start.1) | collective-permute-done | bytes 61472 | tf_op jit(solution)/shard_map/ppermute | solution.py:438
  14.2 0.0 copy-start.1
  14.2 0.0 copy-done
  14.2 0.6 %copy-done.1 = f32[15,8,128]{2,1,0:T(8,128)} copy-done((f32[15,8,128]{2,1,0:T(8,128)}, f32[15,8,128]{2,1,0:T(8,128)S(1)}, u32[]{:S(2)}) %copy-start.1) | copy-done | bytes 61464
  14.8 4.5 %finish.1 = f32[4,19,4096]{2,1,0:T(8,128)} custom-call(f32[4,19,4096]{2,1,0:T(8,128)} %copy.6.pop_hbm, s32[4,4096]{1,0:T(4,128)} %flags.3, s32[4,18]{1,0:T(4,128)} %nbr.3, f32[4]{0:T(128)} %rate.3, f32[9,4,32,128]{3,2,1,0:T(8,128)} %get-tuple-element.8.mom_in, f32[15,8,128]{2,1,0:T(8,128)} %get-tuple-element.9.msg_even, ...), custom_call_target="tpu_custom_call" | custom-call | tf_op jit(solution)/shard_map/finish/pallas_call | solution.py:440
  19.3 3.2 %copy.7 = f32[4,19,4096]{2,0,1:T(4,128)} copy(f32[4,19,4096]{2,1,0:T(8,128)} %finish.1) | data formatting | bytes 2490368 | tf_op jit(solution)/shard_map/finish/pallas_call | solution.py:440
Async XLA Ops:
  7.9 4.1 %collective-permute-start = (f32[15,8,128]{2,1,0:T(8,128)}, f32[15,8,128]{2,1,0:T(8,128)S(1)}, u32[]{:S(2)}, u32[]{:S(2)}) collective-permute-start(f32[15,8,128]{2,1,0:T(8,128)} %get-tuple-element.9.msg_even), channel_id=1, source_target_pairs={{0,1},{1,0},{2,3},{3,2},{4,5},{5,4},{6,7},{7,6},{8,9},{9,8},{10,11... | collective-permute-start | bytes 184328 | tf_op jit(solution)/shard_map/ppermute | solution.py:439
  8.5 5.7 %collective-permute-start.1 = (f32[15,8,128]{2,1,0:T(8,128)}, f32[15,8,128]{2,1,0:T(8,128)S(1)}, u32[]{:S(2)}, u32[]{:S(2)}) collective-permute-start(f32[15,8,128]{2,1,0:T(8,128)} %get-tuple-element.10.msg_odd), channel_id=1, source_target_pairs={{0,7},{1,2},{2,1},{3,4},{4,3},{5,6},{6,5},{7,0},{8,15},{9,10},{10,... | collective-permute-start | bytes 184328 | tf_op jit(solution)/shard_map/ppermute | solution.py:438
  12.0 2.2 %copy-start = (f32[15,8,128]{2,1,0:T(8,128)}, f32[15,8,128]{2,1,0:T(8,128)S(1)}, u32[]{:S(2)}) copy-start(f32[15,8,128]{2,1,0:T(8,128)S(1)} %collective-permute-done.got_even) | copy-start | bytes 184324
  14.2 0.6 %copy-start.1 = (f32[15,8,128]{2,1,0:T(8,128)}, f32[15,8,128]{2,1,0:T(8,128)S(1)}, u32[]{:S(2)}) copy-start(f32[15,8,128]{2,1,0:T(8,128)S(1)} %collective-permute-done.1.got_odd) | copy-start | bytes 184324

commit v2 on v1

v2 whole, which is shorter than its diff:
```python
import jax
import jax.numpy as jnp
from jax import lax
from jax.experimental import pallas as pl
from jax.experimental.pallas import tpu as pltpu
from jax.sharding import PartitionSpec as P

EDGE = 16
LANES = 128
SUB = 8
CLOSED = 1.0e30
LIMIT = 1.0e29
GROUP = 4


def directions():
    listed = [(0, 0, 0)]
    for axis in range(3):
        for sign in (1, -1):
            vector = [0, 0, 0]
            vector[axis] = sign
            listed.append(tuple(vector))
    for one, two in ((0, 1), (0, 2), (1, 2)):
        for sign_one in (1, -1):
            for sign_two in (1, -1):
                vector = [0, 0, 0]
                vector[one] = sign_one
                vector[two] = sign_two
                listed.append(tuple(vector))
    return listed


C = directions()
INDEX = {vector: num for num, vector in enumerate(C)}
OPP = [INDEX[tuple(-part for part in vector)] for vector in C]
FLAT = ((0, 0), (1, 0), (-1, 0), (0, 1), (0, -1))
UPWARD = [INDEX[(a, b, 1)] for a, b in FLAT]
DOWNWARD = [INDEX[(a, b, -1)] for a, b in FLAT]
N_MOM = 9
N_MSG = N_MOM + 5 + 1


def column(vector):
    return INDEX[vector] - 1


def moments(g):
    sx, dx = g[1] + g[2], g[1] - g[2]
    sy, dy = g[3] + g[4], g[3] - g[4]
    sz, dz = g[5] + g[6], g[5] - g[6]
    pairs = []
    for base in (7, 11, 15):
        pairs.append((g[base] + g[base + 3], g[base] - g[base + 3], g[base + 1] + g[base + 2], g[base + 1] - g[base + 2]))
    (xys, xyd, xyt, xye), (xzs, xzd, xzt, xze), (yzs, yzd, yzt, yze) = pairs
    exy, exz, eyz = xys + xyt, xzs + xzt, yzs + yzt
    rho = g[0] * (1.0 / 3.0) + (sx + sy + sz) * (1.0 / 18.0) + (exy + exz + eyz) * (1.0 / 36.0)
    ux = dx * (1.0 / 6.0) + (xyd + xye + xzd + xze) * (1.0 / 12.0)
    uy = dy * (1.0 / 6.0) + (xyd - xye + yzd + yze) * (1.0 / 12.0)
    uz = dz * (1.0 / 6.0) + (xzd - xze + yzd - yze) * (1.0 / 12.0)
    qxy = (xys - xyt) * 0.25
    qxz = (xzs - xzt) * 0.25
    qyz = (yzs - yzt) * 0.25
    gxz = (sx - sz) * 0.5 + (exy - eyz) * 0.25
    gyz = (sy - sz) * 0.5 + (exy - exz) * 0.25
    return [rho, ux, uy, uz, qxy, qxz, qyz, gxz, gyz]


def add_crossing(mom, e, sign):
    ez, xp, xm, yp, ym = e
    rho, ux, uy, uz, qxy, qxz, qyz, gxz, gyz = mom
    xs, xd, ys, yd = xp + xm, xp - xm, yp + ym, yp - ym
    four = xs + ys
    half = ez * 0.5
    return [
        rho + ez * (1.0 / 18.0) + four * (1.0 / 36.0),
        ux + xd * (1.0 / 12.0),
        uy + yd * (1.0 / 12.0),
        uz + sign * (ez * (1.0 / 6.0) + four * (1.0 / 12.0)),
        qxy,
        qxz + (sign * 0.25) * xd,
        qyz + (sign * 0.25) * yd,
        gxz - ys * 0.25 - half,
        gyz - xs * 0.25 - half,
    ]


def collided_from(mom, tau, wanted=range(19)):
    rho, ux, uy, uz, qxy, qxz, qyz, gxz, gyz = mom
    xx, yy, zz = ux * ux, uy * uy, uz * uz
    base = rho - (xx + yy + zz) * (1.0 / 6.0)
    hx = gxz - (xx - zz)
    hy = gyz - (yy - zz)
    third = tau * (1.0 / 3.0)
    shear = {
        (0,): third * (hx + hx - hy),
        (1,): third * (hy + hy - hx),
        (2,): -third * (hx + hy),
        (0, 1): tau * (qxy - ux * uy),
        (0, 2): tau * (qxz - ux * uz),
        (1, 2): tau * (qyz - uy * uz),
    }
    u = (ux, uy, uz)
    out = {0: base}
    for num in wanted:
        if num in out:
            continue
        vector = C[num]
        axes = tuple(axis for axis in range(3) if vector[axis])
        if len(axes) == 1:
            speed = u[axes[0]]
            lead = vector[axes[0]]
            even = base + speed * speed * 0.5 + shear[axes]
        else:
            first, second = vector[axes[0]], vector[axes[1]]
            speed = u[axes[0]] + u[axes[1]] if first == second else u[axes[0]] - u[axes[1]]
            lead = first
            even = base + speed * speed * 0.5
            even = even + shear[axes] if first == second else even - shear[axes]
        plus = num if lead > 0 else OPP[num]
        out[plus] = even + speed
        out[OPP[plus]] = even - speed
    return out


def turned(value, shift):
    if isinstance(shift, int):
        shift = shift % LANES
        return value if shift == 0 else pltpu.roll(value, shift, 1)
    return pltpu.roll(value, (shift + LANES) % LANES, 1)


def picked(value, source):
    moved = jnp.take_along_axis(value, jnp.maximum(source, 0), axis=0)
    return jnp.where(source >= 0, moved, CLOSED)


class Place:
    def __init__(self, slots):
        self.slots = slots
        self.lane = lax.broadcasted_iota(jnp.int32, (SUB, LANES), 1)
        sub = lax.broadcasted_iota(jnp.int32, (SUB, LANES), 0)
        self.slot = sub % slots
        self.high = sub // slots
        self.depth = self.lane % EDGE

    def carry(self, cy):
        return self.lane >= LANES - EDGE if cy > 0 else self.lane < EDGE

    def named(self, entries, base):
        found = jnp.full((SUB, LANES), -1, jnp.int32)
        for slot, entry in enumerate(entries):
            found = jnp.where(self.slot == slot, jnp.where(entry >= 0, entry - base, -1), found)
        return found

    def naming(self, entries, base):
        found = jnp.full((SUB, LANES), -1, jnp.int32)
        for slot, entry in enumerate(entries):
            found = jnp.where(self.slot == entry - base, slot, found)
        return found

    def straight(self, found):
        return jnp.where(found >= 0, self.high * self.slots + found, -1)

    def across(self, same, corner, cy):
        inner = self.high == (1 if cy > 0 else 0)
        found = jnp.where(inner, same, corner)
        return jnp.where(found >= 0, (1 - self.high) * self.slots + found, -1)


def column_of(nbr, vector, slots):
    return [nbr[slot, column(vector)] for slot in range(slots)]


def plane_maps(place, nbr):
    slots = place.slots
    maps = {}
    for cx in (1, -1):
        side = place.named(column_of(nbr, (-cx, 0, 0), slots), slots)
        maps[cx, 0] = place.straight(side)
        for cy in (1, -1):
            corner = place.named(column_of(nbr, (-cx, -cy, 0), slots), slots)
            maps[cx, cy] = place.across(side, corner, cy)
    for cy in (1, -1):
        beside = place.named(column_of(nbr, (0, -cy, 0), slots), slots)
        maps[0, cy] = place.across(place.slot, beside, cy)
    return maps


def store_collided(place, maps, still, moved, x, h, fluid):
    kept = []
    for num in range(19):
        cx, cy, cz = C[num]
        value = jnp.where(fluid, h[num], CLOSED)
        kept.append(value)
        still[num, x] = value
        if num:
            if cy:
                value = jnp.where(place.carry(cy), picked(value, maps[0, cy]), value)
            moved[num, x + 1] = turned(value, EDGE * cy + cz)
    return kept


def store_rims(place, maps, still, moved):
    for num in range(1, 19):
        cx, cy, cz = C[num]
        if cx:
            source = still[num, EDGE - 1 if cx > 0 else 0]
            value = picked(source, maps[cx, 0])
            if cy:
                value = jnp.where(place.carry(cy), picked(source, maps[cx, cy]), value)
            moved[num, 0 if cx > 0 else EDGE + 1] = turned(value, EDGE * cy + cz)


def face_pull(place, plane, flat, straight, corner):
    cx, cy = flat
    value = picked(plane, place.straight(straight))
    if cx:
        end = picked(plane, place.straight(corner))
        return jnp.where(place.depth == (0 if cx > 0 else EDGE - 1), turned(end, cx - EDGE * cx), turned(value, cx))
    if cy:
        value = jnp.where(place.carry(cy), picked(plane, place.across(straight, corner, cy)), value)
        return turned(value, EDGE * cy)
    return value


def tau_plane(place, rate):
    tau = jnp.zeros((SUB, LANES), jnp.float32)
    for slot in range(place.slots):
        tau = jnp.where(place.slot == slot, 1.0 - rate[slot], tau)
    return tau


def looped(start, stop, step):
    def run(x, carried):
        step(x)
        return carried

    lax.fori_loop(start, stop, run, 0, unroll=UNROLL)


UNROLL = 4


def first_kernel(pop_hbm, flags, nbr, rate, mom_out, msg_even, msg_odd, raw, still, moved, sides, sems):
    slots = nbr.shape[0]
    place = Place(slots)
    parts = [pl.ds(first, GROUP) for first in range(0, EDGE, GROUP)]
    copies = [pltpu.make_async_copy(pop_hbm.at[:, part], raw.at[:, part], sems.at[at]) for at, part in enumerate(parts)]
    for copy in copies:
        copy.start()
    maps = plane_maps(place, nbr)
    tau = tau_plane(place, rate)
    depth = place.depth

    def collide(x):
        h = collided_from(moments([raw[num, x] for num in range(19)]), tau)
        kept = store_collided(place, maps, still, moved, x, h, flags[x] > 0)
        for at in range(5):
            pltpu.store(sides.at[0, N_MOM + at], turned(kept[UPWARD[at]], x - (EDGE - 1)), mask=depth == x)
            pltpu.store(sides.at[1, N_MOM + at], turned(kept[DOWNWARD[at]], x), mask=depth == x)

    for at, copy in enumerate(copies):
        copy.wait()
        looped(at * GROUP, (at + 1) * GROUP, collide)
    store_rims(place, maps, still, moved)
    keep = {1: depth != 0, -1: depth != EDGE - 1}

    def stream(x):
        g = [still[0, x]]
        for num in range(1, 19):
            value = moved[num, x + 1 - C[num][0]]
            value = jnp.where(value < LIMIT, value, still[OPP[num], x])
            if C[num][2]:
                value = jnp.where(keep[C[num][2]], value, 0.0)
            g.append(value)
        mom = moments(g)
        for at in range(N_MOM):
            mom_out[at, x] = mom[at]
            pltpu.store(sides.at[0, at], turned(mom[at], x - (EDGE - 1)), mask=depth == x)
            pltpu.store(sides.at[1, at], turned(mom[at], x), mask=depth == x)

    looped(0, EDGE, stream)
    odd = lax.axis_index("dev") % 2 == 1
    for at in range(N_MSG):
        upper = tau if at == N_MSG - 1 else sides[0, at]
        lower = tau if at == N_MSG - 1 else sides[1, at]
        msg_even[at] = jnp.where(odd, lower, upper)
        msg_odd[at] = jnp.where(odd, upper, lower)


def second_kernel(
    pop_hbm, flags, nbr, rate, mom_in, msg_even, msg_odd, got_even, got_odd, out_hbm,
    raw, still, moved, faces, sems, out_sems,
):
    slots = nbr.shape[0]
    place = Place(slots)
    incoming = pltpu.make_async_copy(pop_hbm, raw, sems.at[0])
    incoming.start()
    maps = plane_maps(place, nbr)
    tau = tau_plane(place, rate)
    depth = place.depth
    odd = lax.axis_index("dev") % 2 == 1

    def upper_own(at):
        return jnp.where(odd, msg_odd[at], msg_even[at])

    def lower_own(at):
        return jnp.where(odd, msg_even[at], msg_odd[at])

    def upper_got(at):
        return jnp.where(odd, got_odd[at], got_even[at])

    def lower_got(at):
        return jnp.where(odd, got_even[at], got_odd[at])

    for side, sign in ((0, 1), (1, -1)):
        own_msg, got_msg = (upper_own, upper_got) if sign > 0 else (lower_own, lower_got)
        base = (sign + 1) * slots
        inward = DOWNWARD if sign > 0 else UPWARD
        upright = column_of(nbr, (0, 0, sign), slots)
        straight, back_straight = place.named(upright, base), place.naming(upright, base)
        own_out = [own_msg(N_MOM + at) for at in range(5)]
        got_in = [got_msg(N_MOM + at) for at in range(5)]
        leaving, corners = [], []
        for at, (cx, cy) in enumerate(FLAT):
            corner = back_corner = None
            if cx or cy:
                corner = place.named(column_of(nbr, (-cx, -cy, sign), slots), base)
                back_corner = place.naming(column_of(nbr, (cx, cy, sign), slots), base)
            corners.append(corner)
            mirror = FLAT.index((-cx, -cy))
            value = face_pull(place, got_in[at], (cx, cy), straight, corner)
            faces[side, at] = jnp.where(value < LIMIT, value, own_out[mirror])
            value = face_pull(place, own_out[at], (cx, cy), back_straight, back_corner)
            leaving.append(jnp.where(value < LIMIT, value, got_in[mirror]))
        mom = add_crossing([got_msg(at) for at in range(N_MOM)], leaving, float(sign))
        h = collided_from(mom, got_msg(N_MSG - 1), inward)
        for at, flat in enumerate(FLAT):
            value = jnp.where(got_in[0] < LIMIT, h[inward[at]], CLOSED)
            faces[side, 5 + at] = face_pull(place, value, flat, straight, corners[at])

    top, bottom = depth == EDGE - 1, depth == 0
    sign = jnp.where(bottom, 1.0, -1.0)

    def collide(x):
        crossing = []
        for at in range(5):
            value = jnp.where(top, turned(faces[0, at], EDGE - 1 - x), 0.0)
            crossing.append(jnp.where(bottom, turned(faces[1, at], -x), value))
        mom = add_crossing([mom_in[at, x] for at in range(N_MOM)], crossing, sign)
        store_collided(place, maps, still, moved, x, collided_from(mom, tau), flags[x] > 0)

    looped(0, EDGE, collide)
    store_rims(place, maps, still, moved)
    incoming.wait()

    def stream(x):
        fluid = flags[x] > 0
        for num in range(19):
            value = back = still[OPP[num], x]
            if num:
                cx, cy, cz = C[num]
                value = moved[num, x + 1 - cx]
                if cz > 0:
                    value = jnp.where(bottom, turned(faces[1, 5 + UPWARD.index(num)], -x), value)
                elif cz < 0:
                    value = jnp.where(top, turned(faces[0, 5 + DOWNWARD.index(num)], EDGE - 1 - x), value)
                value = jnp.where(value < LIMIT, value, back)
            raw[num, x] = jnp.where(fluid, value, raw[num, x])

    outs = []
    for at, first in enumerate(range(0, EDGE, GROUP)):
        looped(first, first + GROUP, stream)
        part = pl.ds(first, GROUP)
        outs.append(pltpu.make_async_copy(raw.at[:, part], out_hbm.at[:, part], out_sems.at[at]))
        outs[-1].start()
    for out in outs:
        out.wait()


def body(populations, fluid_flags, neighbours, relax_rate):
    slots, velocities, cells = populations.shape
    assert cells == EDGE**3 and 2 * slots == SUB and velocities == 19
    peers = lax.axis_size("dev")
    assert peers % 2 == 0
    tiles = cells // LANES
    view = (EDGE, SUB, LANES)
    pops = populations.transpose(1, 0, 2).reshape(19, slots, tiles, LANES).transpose(0, 2, 1, 3).reshape((19,) + view)
    flags = fluid_flags.reshape(slots, tiles, LANES).transpose(1, 0, 2).reshape(view)
    vmem = pl.BlockSpec(memory_space=pltpu.VMEM)
    smem = pl.BlockSpec(memory_space=pltpu.SMEM)
    hbm = pl.BlockSpec(memory_space=pltpu.HBM)
    face = (SUB, LANES)
    scratch = [
        pltpu.VMEM((19,) + view, jnp.float32),
        pltpu.VMEM((19,) + view, jnp.float32),
        pltpu.VMEM((19, EDGE + 2) + face, jnp.float32),
    ]
    params = pltpu.CompilerParams(vmem_limit_bytes=16 * 2**20)
    message = jax.ShapeDtypeStruct((N_MSG,) + face, jnp.float32)
    mom, msg_even, msg_odd = pl.pallas_call(
        first_kernel,
        out_shape=(jax.ShapeDtypeStruct((N_MOM,) + view, jnp.float32), message, message),
        in_specs=[hbm, vmem, smem, smem],
        out_specs=(vmem, vmem, vmem),
        scratch_shapes=scratch + [
            pltpu.VMEM((2, N_MOM + 5) + face, jnp.float32),
            pltpu.SemaphoreType.DMA((EDGE // GROUP,)),
        ],
        compiler_params=params,
        name="collide_and_stream",
    )(pops, flags, neighbours, relax_rate)
    even_pairs = [(i, i ^ 1) for i in range(peers)]
    odd_pairs = [(i, (i + 1) % peers if i % 2 else (i - 1) % peers) for i in range(peers)]
    got_odd = lax.ppermute(msg_odd, "dev", odd_pairs)
    got_even = lax.ppermute(msg_even, "dev", even_pairs)
    out = pl.pallas_call(
        second_kernel,
        out_shape=jax.ShapeDtypeStruct(pops.shape, jnp.float32),
        in_specs=[hbm, vmem, smem, smem, vmem, vmem, vmem, vmem, vmem],
        out_specs=hbm,
        scratch_shapes=scratch + [
            pltpu.VMEM((2, 10) + face, jnp.float32),
            pltpu.SemaphoreType.DMA((1,)),
            pltpu.SemaphoreType.DMA((EDGE // GROUP,)),
        ],
        compiler_params=params,
        name="finish",
    )(pops, flags, neighbours, relax_rate, mom, msg_even, msg_odd, got_even, got_odd)
    out = out.reshape(19, tiles, slots, LANES).transpose(0, 2, 1, 3).reshape(19, slots, cells)
    return out.transpose(1, 0, 2)


def solution(mesh):
    placed = (
        P(("group", "dev"), None, None),
        P(("group", "dev"), None),
        P(("group", "dev"), None),
        P(("group", "dev")),
    )
    return jax.shard_map(
        body, mesh=mesh, in_specs=placed, out_specs=P(("group", "dev"), None, None), check_vma=False
    )
```

time: 22.8 us -> 15.4 us (0.68)
  local copies, waits for them, and re-layouts: 7.05 us -> 3.47 us
  Pallas kernels: 9.2 us -> 5.66 us
  waiting for transfers between devices: 2.18 us -> 1.9 us
    pallas_call x2, Pallas kernels: 9.2 us -> 5.66 us  [the longest x1 3.45 us: body(): pl.pallas_call(second_kernel, out_shape=jax.ShapeDtypeStruct(pops.shape,...]
    pallas_call x1 -> x0, local copies, waits for them, and re-layouts: 3.25 us -> none  [body(): pl.pallas_call(second_kernel, out_shape=jax.ShapeDtypeStruct(populations....]
    unnamed x5 -> x8, local copies, waits for them, and re-layouts: 3.81 us -> 3.47 us
    ppermute x1, waiting for transfers between devices: 2.18 us -> 1.9 us  [body(): got_odd = lax.ppermute(msg_odd, 'dev', odd_pairs)]
where the time goes in v2:
time: 15.4 us; the launch traced here: 15.1 us
  Pallas kernels  5.66 us (37%)
  starting transfers between devices  4.1 us (27%)
  local copies, waits for them, and re-layouts  3.47 us (23%)
  waiting for transfers between devices  1.9 us (12%)
    ppermute x1, starting transfers between devices, body(): got_odd = lax.ppermute(msg_odd, 'dev', odd_pairs)  3.54 us
    unnamed x8, local copies, waits for them, and re-layouts  3.47 us
    pallas_call x1, Pallas kernels, body(): pl.pallas_call(second_kernel, out_shape=jax.ShapeDtypeStruct(pops.shape,...  3.45 us
    pallas_call x1, Pallas kernels, body(): pl.pallas_call(first_kernel, out_shape=(jax.ShapeDtypeStruct((N_MOM,) + v...  2.22 us
    ppermute x1, waiting for transfers between devices, body(): got_odd = lax.ppermute(msg_odd, 'dev', odd_pairs)  1.9 us
    ppermute x1, starting transfers between devices, body(): got_even = lax.ppermute(msg_even, 'dev', even_pairs)  0.56 us
  transfers between devices with their start and end apart: 2, of which 1 were waited for; matrix products, arithmetic and copies ran while one was open for 0% of the time, Pallas kernels for 0%

profile of v2, /device:TPU:0, one launch (start us, length us, event | category | flops | bytes accessed | tf_op | source)
XLA Modules:
  0.0 15.1 jit_solution(14511046587204250343)
XLA Ops:
  0.0 0.0 copy-start
  0.0 1.3 %copy-done = f32[4,19,4096]{2,0,1:T(4,128)S(1)} copy-done((f32[4,19,4096]{2,0,1:T(4,128)S(1)}, f32[4,19,4096]{2,0,1:T(4,128)}, u32[]{:S(2)}) %copy-start) | copy-done | bytes 1245208
  1.3 0.0 copy-start.1
  1.3 0.8 %copy-done.1 = s32[4,4096]{1,0:T(4,128)S(1)} copy-done((s32[4,4096]{1,0:T(4,128)S(1)}, s32[4,4096]{1,0:T(4,128)}, u32[]{:S(2)}) %copy-start.1) | copy-done | bytes 65560
  2.1 0.0 copy-start.2
  2.1 0.7 %copy-done.2 = s32[4,18]{1,0:T(4,128)S(1)} copy-done((s32[4,18]{1,0:T(4,128)S(1)}, s32[4,18]{1,0:T(4,128)}, u32[]{:S(2)}) %copy-start.2) | copy-done | bytes 312
  2.8 0.0 copy-start.3
  2.8 0.7 %copy-done.3 = f32[4]{0:T(128)S(1)} copy-done((f32[4]{0:T(128)S(1)}, f32[4]{0:T(128)}, u32[]{:S(2)}) %copy-start.3) | copy-done | bytes 40
  3.5 2.2 %collide_and_stream.1 = (f32[9,16,8,128]{3,2,1,0:T(8,128)S(1)}, f32[15,8,128]{2,1,0:T(8,128)S(1)}, f32[15,8,128]{2,1,0:T(8,128)S(1)}) custom-call(f32[19,16,8,128]{3,2,1,0:T(8,128)S(1)} %bitcast.19, s32[16,8,128]{2,1,0:T(8,128)S(1)} %bitcast.21, s32[4,18]{1,0:T(4,128)S(1)} %copy-done.2, f32[4]{0:T(128)S(1)} %copy-done.3), custom_call_target="tpu_custom_call" | custom-call | tf_op jit(solution)/shard_map/collide_and_stream/pallas_call | solution.py:401
  5.7 0.6 %collective-permute-start = (f32[15,8,128]{2,1,0:T(8,128)S(1)}, f32[15,8,128]{2,1,0:T(8,128)S(1)}, u32[]{:S(2)}, u32[]{:S(2)}) collective-permute-start(f32[15,8,128]{2,1,0:T(8,128)S(1)} %get-tuple-element.9.msg_even), channel_id=1, source_target_pairs={{0,1},{1,0},{2,3},{3,2},{4,5},{5,4},{6,7},{7,6},{8,9},{9,8},{10,11... | collective-permute-start | bytes 184328 | tf_op jit(solution)/shard_map/ppermute | solution.py:416
  6.3 3.5 %collective-permute-start.1 = (f32[15,8,128]{2,1,0:T(8,128)S(1)}, f32[15,8,128]{2,1,0:T(8,128)S(1)}, u32[]{:S(2)}, u32[]{:S(2)}) collective-permute-start(f32[15,8,128]{2,1,0:T(8,128)S(1)} %get-tuple-element.10.msg_odd), channel_id=1, source_target_pairs={{0,7},{1,2},{2,1},{3,4},{4,3},{5,6},{6,5},{7,0},{8,15},{9,10},{10,... | collective-permute-start | bytes 184328 | tf_op jit(solution)/shard_map/ppermute | solution.py:415
  9.8 0.0 collective-permute-done.got_even
  9.8 1.9 %collective-permute-done.1.got_odd = f32[15,8,128]{2,1,0:T(8,128)S(1)} collective-permute-done((f32[15,8,128]{2,1,0:T(8,128)S(1)}, f32[15,8,128]{2,1,0:T(8,128)S(1)}, u32[]{:S(2)}, u32[]{:S(2)}) %collective-permute-start.1) | collective-permute-done | bytes 61472 | tf_op jit(solution)/shard_map/ppermute | solution.py:415
  11.7 3.4 %finish.1 = f32[19,16,8,128]{3,2,1,0:T(8,128)} custom-call(f32[19,16,8,128]{3,2,1,0:T(8,128)S(1)} %bitcast.20, s32[16,8,128]{2,1,0:T(8,128)S(1)} %bitcast.22, s32[4,18]{1,0:T(4,128)S(1)} %copy-done.2, f32[4]{0:T(128)S(1)} %copy-done.3, f32[9,16,8,128]{3,2,1,0:T(8,128)S(1)} %get-tuple-element.8.mom_in, f32[15,8,128]{2,1,0:T(8,128)S(1)} %get-tuple-element.9.msg_even, ...), custom_call_target="tpu_custom_call" | custom-call | tf_op jit(solution)/shard_map/finish/pallas_call | solution.py:417
Async XLA Ops:
  0.0 1.3 %copy-start = (f32[4,19,4096]{2,0,1:T(4,128)S(1)}, f32[4,19,4096]{2,0,1:T(4,128)}, u32[]{:S(2)}) copy-start(f32[4,19,4096]{2,0,1:T(4,128)} %param.4) | copy-start | bytes 3735556
  1.3 0.8 %copy-start.1 = (s32[4,4096]{1,0:T(4,128)S(1)}, s32[4,4096]{1,0:T(4,128)}, u32[]{:S(2)}) copy-start(s32[4,4096]{1,0:T(4,128)} %param.5) | copy-start | bytes 196612
  2.1 0.7 %copy-start.2 = (s32[4,18]{1,0:T(4,128)S(1)}, s32[4,18]{1,0:T(4,128)}, u32[]{:S(2)}) copy-start(s32[4,18]{1,0:T(4,128)} %nbr.3) | copy-start | bytes 868
  2.8 0.7 %copy-start.3 = (f32[4]{0:T(128)S(1)}, f32[4]{0:T(128)}, u32[]{:S(2)}) copy-start(f32[4]{0:T(128)} %rate.3) | copy-start | bytes 52
  5.7 4.1 %collective-permute-start = (f32[15,8,128]{2,1,0:T(8,128)S(1)}, f32[15,8,128]{2,1,0:T(8,128)S(1)}, u32[]{:S(2)}, u32[]{:S(2)}) collective-permute-start(f32[15,8,128]{2,1,0:T(8,128)S(1)} %get-tuple-element.9.msg_even), channel_id=1, source_target_pairs={{0,1},{1,0},{2,3},{3,2},{4,5},{5,4},{6,7},{7,6},{8,9},{9,8},{10,11... | collective-permute-start | bytes 184328 | tf_op jit(solution)/shard_map/ppermute | solution.py:416
  6.3 5.4 %collective-permute-start.1 = (f32[15,8,128]{2,1,0:T(8,128)S(1)}, f32[15,8,128]{2,1,0:T(8,128)S(1)}, u32[]{:S(2)}, u32[]{:S(2)}) collective-permute-start(f32[15,8,128]{2,1,0:T(8,128)S(1)} %get-tuple-element.10.msg_odd), channel_id=1, source_target_pairs={{0,7},{1,2},{2,1},{3,4},{4,3},{5,6},{6,5},{7,0},{8,15},{9,10},{10,... | collective-permute-start | bytes 184328 | tf_op jit(solution)/shard_map/ppermute | solution.py:415

commit v3 on v2

--- a/solution.py
+++ b/solution.py
@@ -241,13 +241,26 @@
 UNROLL = 4
 
 
-def first_kernel(pop_hbm, flags, nbr, rate, mom_out, msg_even, msg_odd, raw, still, moved, sides, sems):
+def small_copies(hbm_refs, refs, sems):
+    copies = [pltpu.make_async_copy(src, dst, sems.at[at]) for at, (src, dst) in enumerate(zip(hbm_refs, refs))]
+    for copy in copies:
+        copy.start()
+    return copies
+
+
+def first_kernel(
+    pop_hbm, flags_hbm, nbr_hbm, rate_hbm, mom_out, msg_even, msg_odd,
+    raw, still, moved, flags, nbr, rate, small_sems, sides, sems,
+):
     slots = nbr.shape[0]
     place = Place(slots)
+    small = small_copies((nbr_hbm, rate_hbm, flags_hbm), (nbr, rate, flags), small_sems)
     parts = [pl.ds(first, GROUP) for first in range(0, EDGE, GROUP)]
     copies = [pltpu.make_async_copy(pop_hbm.at[:, part], raw.at[:, part], sems.at[at]) for at, part in enumerate(parts)]
     for copy in copies:
         copy.start()
+    for copy in small:
+        copy.wait()
     maps = plane_maps(place, nbr)
     tau = tau_plane(place, rate)
     depth = place.depth
@@ -289,13 +302,16 @@
 
 
 def second_kernel(
-    pop_hbm, flags, nbr, rate, mom_in, msg_even, msg_odd, got_even, got_odd, out_hbm,
-    raw, still, moved, faces, sems, out_sems,
+    pop_hbm, flags_hbm, nbr_hbm, rate_hbm, mom_in, msg_even, msg_odd, got_even, got_odd, out_hbm,
+    raw, still, moved, flags, nbr, rate, small_sems, faces, sems, out_sems,
 ):
     slots = nbr.shape[0]
     place = Place(slots)
+    small = small_copies((nbr_hbm, rate_hbm, flags_hbm), (nbr, rate, flags), small_sems)
     incoming = pltpu.make_async_copy(pop_hbm, raw, sems.at[0])
     incoming.start()
+    for copy in small:
+        copy.wait()
     maps = plane_maps(place, nbr)
     tau = tau_plane(place, rate)
     depth = place.depth
@@ -387,21 +403,25 @@
     view = (EDGE, SUB, LANES)
     pops = populations.transpose(1, 0, 2).reshape(19, slots, tiles, LANES).transpose(0, 2, 1, 3).reshape((19,) + view)
     flags = fluid_flags.reshape(slots, tiles, LANES).transpose(1, 0, 2).reshape(view)
+    args = [pltpu.with_memory_space_constraint(arg, pltpu.HBM) for arg in (pops, flags, neighbours, relax_rate)]
     vmem = pl.BlockSpec(memory_space=pltpu.VMEM)
-    smem = pl.BlockSpec(memory_space=pltpu.SMEM)
     hbm = pl.BlockSpec(memory_space=pltpu.HBM)
     face = (SUB, LANES)
     scratch = [
         pltpu.VMEM((19,) + view, jnp.float32),
         pltpu.VMEM((19,) + view, jnp.float32),
         pltpu.VMEM((19, EDGE + 2) + face, jnp.float32),
+        pltpu.VMEM(view, jnp.int32),
+        pltpu.SMEM(neighbours.shape, jnp.int32),
+        pltpu.SMEM(relax_rate.shape, jnp.float32),
+        pltpu.SemaphoreType.DMA((3,)),
     ]
     params = pltpu.CompilerParams(vmem_limit_bytes=16 * 2**20)
-    message = jax.ShapeDtypeStruct((N_MSG,) + face, jnp.float32)
+    message = pltpu.VMEM((N_MSG,) + face, jnp.float32)
     mom, msg_even, msg_odd = pl.pallas_call(
         first_kernel,
-        out_shape=(jax.ShapeDtypeStruct((N_MOM,) + view, jnp.float32), message, message),
-        in_specs=[hbm, vmem, smem, smem],
+        out_shape=(pltpu.VMEM((N_MOM,) + view, jnp.float32), message, message),
+        in_specs=[hbm] * 4,
         out_specs=(vmem, vmem, vmem),
         scratch_shapes=scratch + [
             pltpu.VMEM((2, N_MOM + 5) + face, jnp.float32),
@@ -409,7 +429,7 @@
         ],
         compiler_params=params,
         name="collide_and_stream",
-    )(pops, flags, neighbours, relax_rate)
+    )(*args)
     even_pairs = [(i, i ^ 1) for i in range(peers)]
     odd_pairs = [(i, (i + 1) % peers if i % 2 else (i - 1) % peers) for i in range(peers)]
     got_odd = lax.ppermute(msg_odd, "dev", odd_pairs)
@@ -417,7 +437,7 @@
     out = pl.pallas_call(
         second_kernel,
         out_shape=jax.ShapeDtypeStruct(pops.shape, jnp.float32),
-        in_specs=[hbm, vmem, smem, smem, vmem, vmem, vmem, vmem, vmem],
+        in_specs=[hbm] * 4 + [vmem] * 5,
         out_specs=hbm,
         scratch_shapes=scratch + [
             pltpu.VMEM((2, 10) + face, jnp.float32),
@@ -426,7 +446,7 @@
         ],
         compiler_params=params,
         name="finish",
-    )(pops, flags, neighbours, relax_rate, mom, msg_even, msg_odd, got_even, got_odd)
+    )(*args, mom, msg_even, msg_odd, got_even, got_odd)
     out = out.reshape(19, tiles, slots, LANES).transpose(0, 2, 1, 3).reshape(19, slots, cells)
     return out.transpose(1, 0, 2)
 

time: 15.4 us -> 12.3 us (0.80)
  local copies, waits for them, and re-layouts: 3.47 us -> 0 us
  Pallas kernels: 5.66 us -> 6.1 us
    unnamed x8 -> x0, local copies, waits for them, and re-layouts: 3.47 us -> none
    pallas_call x1, Pallas kernels: 2.22 us -> 2.7 us  [body(): pl.pallas_call(first_kernel, out_shape=(pltpu.VMEM((N_MOM,) + view, jnp.f...]
where the time goes in v3:
time: 12.3 us; the launch traced here: 12.1 us
  Pallas kernels  6.1 us (50%)
  starting transfers between devices  4.1 us (33%)
  waiting for transfers between devices  1.9 us (15%)
    ppermute x1, starting transfers between devices, body(): got_odd = lax.ppermute(msg_odd, 'dev', odd_pairs)  3.54 us
    pallas_call x1, Pallas kernels, body(): pl.pallas_call(second_kernel, out_shape=jax.ShapeDtypeStruct(pops.shape,...  3.39 us
    pallas_call x1, Pallas kernels, body(): pl.pallas_call(first_kernel, out_shape=(pltpu.VMEM((N_MOM,) + view, jnp.f...  2.7 us
    ppermute x1, waiting for transfers between devices, body(): got_odd = lax.ppermute(msg_odd, 'dev', odd_pairs)  1.9 us
    ppermute x1, starting transfers between devices, body(): got_even = lax.ppermute(msg_even, 'dev', even_pairs)  0.56 us
  transfers between devices with their start and end apart: 2, of which 1 were waited for; matrix products, arithmetic and copies ran while one was open for 0% of the time, Pallas kernels for 0%

profile of v3, /device:TPU:0, one launch (start us, length us, event | category | flops | bytes accessed | tf_op | source)
XLA Modules:
  0.0 12.1 jit_solution(17851433913036173897)
XLA Ops:
  0.0 2.7 %collide_and_stream.1 = (f32[9,16,8,128]{3,2,1,0:T(8,128)S(1)}, f32[15,8,128]{2,1,0:T(8,128)S(1)}, f32[15,8,128]{2,1,0:T(8,128)S(1)}) custom-call(f32[19,16,8,128]{3,2,1,0:T(8,128)} %bitcast.19, s32[16,8,128]{2,1,0:T(8,128)} %bitcast.21, s32[4,18]{1,0:T(4,128)} %nbr_hbm.3, f32[4]{0:T(128)} %rate_hbm.3), custom_call_target="tpu_custom_call" | custom-call | tf_op jit(solution)/shard_map/collide_and_stream/pallas_call | solution.py:421
  2.7 0.6 %collective-permute-start = (f32[15,8,128]{2,1,0:T(8,128)S(1)}, f32[15,8,128]{2,1,0:T(8,128)S(1)}, u32[]{:S(2)}, u32[]{:S(2)}) collective-permute-start(f32[15,8,128]{2,1,0:T(8,128)S(1)} %get-tuple-element.9.msg_even), channel_id=1, source_target_pairs={{0,1},{1,0},{2,3},{3,2},{4,5},{5,4},{6,7},{7,6},{8,9},{9,8},{10,11... | collective-permute-start | bytes 184328 | tf_op jit(solution)/shard_map/ppermute | solution.py:436
  3.3 3.5 %collective-permute-start.1 = (f32[15,8,128]{2,1,0:T(8,128)S(1)}, f32[15,8,128]{2,1,0:T(8,128)S(1)}, u32[]{:S(2)}, u32[]{:S(2)}) collective-permute-start(f32[15,8,128]{2,1,0:T(8,128)S(1)} %get-tuple-element.10.msg_odd), channel_id=1, source_target_pairs={{0,7},{1,2},{2,1},{3,4},{4,3},{5,6},{6,5},{7,0},{8,15},{9,10},{10,... | collective-permute-start | bytes 184328 | tf_op jit(solution)/shard_map/ppermute | solution.py:435
  6.8 0.0 collective-permute-done.got_even
  6.8 1.9 %collective-permute-done.1.got_odd = f32[15,8,128]{2,1,0:T(8,128)S(1)} collective-permute-done((f32[15,8,128]{2,1,0:T(8,128)S(1)}, f32[15,8,128]{2,1,0:T(8,128)S(1)}, u32[]{:S(2)}, u32[]{:S(2)}) %collective-permute-start.1) | collective-permute-done | bytes 61472 | tf_op jit(solution)/shard_map/ppermute | solution.py:435
  8.7 3.4 %finish.1 = f32[19,16,8,128]{3,2,1,0:T(8,128)} custom-call(f32[19,16,8,128]{3,2,1,0:T(8,128)} %bitcast.20, s32[16,8,128]{2,1,0:T(8,128)} %bitcast.22, s32[4,18]{1,0:T(4,128)} %nbr_hbm.3, f32[4]{0:T(128)} %rate_hbm.3, f32[9,16,8,128]{3,2,1,0:T(8,128)S(1)} %get-tuple-element.8.mom_in, f32[15,8,128]{2,1,0:T(8,128)S(1)} %get-tuple-element.9.msg_even, ...), custom_call_target="tpu_custom_call" | custom-call | tf_op jit(solution)/shard_map/finish/pallas_call | solution.py:437
Async XLA Ops:
  2.7 4.1 %collective-permute-start = (f32[15,8,128]{2,1,0:T(8,128)S(1)}, f32[15,8,128]{2,1,0:T(8,128)S(1)}, u32[]{:S(2)}, u32[]{:S(2)}) collective-permute-start(f32[15,8,128]{2,1,0:T(8,128)S(1)} %get-tuple-element.9.msg_even), channel_id=1, source_target_pairs={{0,1},{1,0},{2,3},{3,2},{4,5},{5,4},{6,7},{7,6},{8,9},{9,8},{10,11... | collective-permute-start | bytes 184328 | tf_op jit(solution)/shard_map/ppermute | solution.py:436
  3.3 5.4 %collective-permute-start.1 = (f32[15,8,128]{2,1,0:T(8,128)S(1)}, f32[15,8,128]{2,1,0:T(8,128)S(1)}, u32[]{:S(2)}, u32[]{:S(2)}) collective-permute-start(f32[15,8,128]{2,1,0:T(8,128)S(1)} %get-tuple-element.10.msg_odd), channel_id=1, source_target_pairs={{0,7},{1,2},{2,1},{3,4},{4,3},{5,6},{6,5},{7,0},{8,15},{9,10},{10,... | collective-permute-start | bytes 184328 | tf_op jit(solution)/shard_map/ppermute | solution.py:435

commit v4 on v2

--- a/solution.py
+++ b/solution.py
@@ -10,7 +10,10 @@
 SUB = 8
 CLOSED = 1.0e30
 LIMIT = 1.0e29
-GROUP = 4
+ARRIVING = 8
+LEAVING = 4
+STREAMED = 8
+INNER = 8
 
 
 def directions():
@@ -36,6 +39,7 @@
 FLAT = ((0, 0), (1, 0), (-1, 0), (0, 1), (0, -1))
 UPWARD = [INDEX[(a, b, 1)] for a, b in FLAT]
 DOWNWARD = [INDEX[(a, b, -1)] for a, b in FLAT]
+MAP_KEYS = [(cx, cy) for cx in (0, 1, -1) for cy in (0, 1, -1) if cx or cy]
 N_MOM = 9
 N_MSG = N_MOM + 5 + 1
 
@@ -213,13 +217,28 @@
 
 def face_pull(place, plane, flat, straight, corner):
     cx, cy = flat
-    value = picked(plane, place.straight(straight))
+    value = picked(plane, straight)
     if cx:
-        end = picked(plane, place.straight(corner))
+        end = picked(plane, corner)
         return jnp.where(place.depth == (0 if cx > 0 else EDGE - 1), turned(end, cx - EDGE * cx), turned(value, cx))
     if cy:
-        value = jnp.where(place.carry(cy), picked(plane, place.across(straight, corner, cy)), value)
+        value = jnp.where(place.carry(cy), picked(plane, corner), value)
         return turned(value, EDGE * cy)
+    return value
+
+
+def face_shift(place, maps, plane, vector):
+    cx, cy, _ = vector
+    value = plane
+    if cy:
+        value = jnp.where(place.carry(cy), picked(plane, maps[0, cy]), plane)
+    value = turned(value, cx + EDGE * cy)
+    if cx:
+        end = picked(plane, maps[cx, 0])
+        if cy:
+            end = jnp.where(place.carry(cy), picked(plane, maps[cx, cy]), end)
+        end = turned(end, cx - EDGE * cx + EDGE * cy)
+        value = jnp.where(place.depth == (0 if cx > 0 else EDGE - 1), end, value)
     return value
 
 
@@ -230,26 +249,41 @@
     return tau
 
 
-def looped(start, stop, step):
+def small_copies(hbm_refs, refs, sems):
+    copies = [pltpu.make_async_copy(src, dst, sems.at[at]) for at, (src, dst) in enumerate(zip(hbm_refs, refs))]
+    for copy in copies:
+        copy.start()
+    return copies
+
+
+def looped(start, stop, step, unroll=1):
     def run(x, carried):
         step(x)
         return carried
 
-    lax.fori_loop(start, stop, run, 0, unroll=UNROLL)
-
-
-UNROLL = 4
-
-
-def first_kernel(pop_hbm, flags, nbr, rate, mom_out, msg_even, msg_odd, raw, still, moved, sides, sems):
+    lax.fori_loop(start, stop, run, 0, unroll=unroll)
+
+
+def first_kernel(
+    pop_hbm, flags_hbm, nbr_hbm, rate_hbm, mom_out, msg_even, msg_odd, raw, flags, maps_out,
+    still, moved, nbr, rate, small_sems, sides, sems,
+):
     slots = nbr.shape[0]
     place = Place(slots)
-    parts = [pl.ds(first, GROUP) for first in range(0, EDGE, GROUP)]
-    copies = [pltpu.make_async_copy(pop_hbm.at[:, part], raw.at[:, part], sems.at[at]) for at, part in enumerate(parts)]
-    for copy in copies:
-        copy.start()
+    small = small_copies((nbr_hbm, rate_hbm, flags_hbm), (nbr, rate, flags), small_sems)
+
+    def arrival(at):
+        part = pl.ds(at * ARRIVING, ARRIVING)
+        return pltpu.make_async_copy(pop_hbm.at[:, part], raw.at[:, part], sems.at[at])
+
+    for at in range(EDGE // ARRIVING):
+        arrival(at).start()
+    for copy in small:
+        copy.wait()
     maps = plane_maps(place, nbr)
     tau = tau_plane(place, rate)
+    for at, key in enumerate(MAP_KEYS):
+        maps_out[at] = maps[key]
     depth = place.depth
 
     def collide(x):
@@ -259,10 +293,6 @@
             pltpu.store(sides.at[0, N_MOM + at], turned(kept[UPWARD[at]], x - (EDGE - 1)), mask=depth == x)
             pltpu.store(sides.at[1, N_MOM + at], turned(kept[DOWNWARD[at]], x), mask=depth == x)
 
-    for at, copy in enumerate(copies):
-        copy.wait()
-        looped(at * GROUP, (at + 1) * GROUP, collide)
-    store_rims(place, maps, still, moved)
     keep = {1: depth != 0, -1: depth != EDGE - 1}
 
     def stream(x):
@@ -279,7 +309,13 @@
             pltpu.store(sides.at[0, at], turned(mom[at], x - (EDGE - 1)), mask=depth == x)
             pltpu.store(sides.at[1, at], turned(mom[at], x), mask=depth == x)
 
-    looped(0, EDGE, stream)
+    def collide_arrived(at):
+        arrival(at).wait()
+        looped(0, ARRIVING, lambda part: collide(at * ARRIVING + part), ARRIVING)
+
+    looped(0, EDGE // ARRIVING, collide_arrived)
+    store_rims(place, maps, still, moved)
+    looped(0, EDGE, stream, STREAMED)
     odd = lax.axis_index("dev") % 2 == 1
     for at in range(N_MSG):
         upper = tau if at == N_MSG - 1 else sides[0, at]
@@ -288,71 +324,16 @@
         msg_odd[at] = jnp.where(odd, upper, lower)
 
 
-def second_kernel(
-    pop_hbm, flags, nbr, rate, mom_in, msg_even, msg_odd, got_even, got_odd, out_hbm,
-    raw, still, moved, faces, sems, out_sems,
-):
+def interior_kernel(nbr_hbm, msg_even, mom_in, raw, flags, maps_in, res, packs, face_maps, still, moved, nbr, small_sems):
     slots = nbr.shape[0]
     place = Place(slots)
-    incoming = pltpu.make_async_copy(pop_hbm, raw, sems.at[0])
-    incoming.start()
-    maps = plane_maps(place, nbr)
-    tau = tau_plane(place, rate)
+    small = small_copies((nbr_hbm,), (nbr,), small_sems)
+    maps = {key: maps_in[at] for at, key in enumerate(MAP_KEYS)}
     depth = place.depth
-    odd = lax.axis_index("dev") % 2 == 1
-
-    def upper_own(at):
-        return jnp.where(odd, msg_odd[at], msg_even[at])
-
-    def lower_own(at):
-        return jnp.where(odd, msg_even[at], msg_odd[at])
-
-    def upper_got(at):
-        return jnp.where(odd, got_odd[at], got_even[at])
-
-    def lower_got(at):
-        return jnp.where(odd, got_even[at], got_odd[at])
-
-    for side, sign in ((0, 1), (1, -1)):
-        own_msg, got_msg = (upper_own, upper_got) if sign > 0 else (lower_own, lower_got)
-        base = (sign + 1) * slots
-        inward = DOWNWARD if sign > 0 else UPWARD
-        upright = column_of(nbr, (0, 0, sign), slots)
-        straight, back_straight = place.named(upright, base), place.naming(upright, base)
-        own_out = [own_msg(N_MOM + at) for at in range(5)]
-        got_in = [got_msg(N_MOM + at) for at in range(5)]
-        leaving, corners = [], []
-        for at, (cx, cy) in enumerate(FLAT):
-            corner = back_corner = None
-            if cx or cy:
-                corner = place.named(column_of(nbr, (-cx, -cy, sign), slots), base)
-                back_corner = place.naming(column_of(nbr, (cx, cy, sign), slots), base)
-            corners.append(corner)
-            mirror = FLAT.index((-cx, -cy))
-            value = face_pull(place, got_in[at], (cx, cy), straight, corner)
-            faces[side, at] = jnp.where(value < LIMIT, value, own_out[mirror])
-            value = face_pull(place, own_out[at], (cx, cy), back_straight, back_corner)
-            leaving.append(jnp.where(value < LIMIT, value, got_in[mirror]))
-        mom = add_crossing([got_msg(at) for at in range(N_MOM)], leaving, float(sign))
-        h = collided_from(mom, got_msg(N_MSG - 1), inward)
-        for at, flat in enumerate(FLAT):
-            value = jnp.where(got_in[0] < LIMIT, h[inward[at]], CLOSED)
-            faces[side, 5 + at] = face_pull(place, value, flat, straight, corners[at])
-
-    top, bottom = depth == EDGE - 1, depth == 0
-    sign = jnp.where(bottom, 1.0, -1.0)
-
+    tau = msg_even[N_MSG - 1]
     def collide(x):
-        crossing = []
-        for at in range(5):
-            value = jnp.where(top, turned(faces[0, at], EDGE - 1 - x), 0.0)
-            crossing.append(jnp.where(bottom, turned(faces[1, at], -x), value))
-        mom = add_crossing([mom_in[at, x] for at in range(N_MOM)], crossing, sign)
-        store_collided(place, maps, still, moved, x, collided_from(mom, tau), flags[x] > 0)
-
-    looped(0, EDGE, collide)
-    store_rims(place, maps, still, moved)
-    incoming.wait()
+        h = collided_from([mom_in[at, x] for at in range(N_MOM)], tau)
+        store_collided(place, maps, still, moved, x, h, flags[x] > 0)
 
     def stream(x):
         fluid = flags[x] > 0
@@ -362,20 +343,123 @@
                 cx, cy, cz = C[num]
                 value = moved[num, x + 1 - cx]
                 if cz > 0:
-                    value = jnp.where(bottom, turned(faces[1, 5 + UPWARD.index(num)], -x), value)
-                elif cz < 0:
-                    value = jnp.where(top, turned(faces[0, 5 + DOWNWARD.index(num)], EDGE - 1 - x), value)
+                    pltpu.store(packs.at[0, UPWARD.index(num)], turned(value, x - (EDGE - 1)), mask=depth == x)
+                if cz < 0:
+                    pltpu.store(packs.at[1, DOWNWARD.index(num)], turned(value, x), mask=depth == x)
                 value = jnp.where(value < LIMIT, value, back)
-            raw[num, x] = jnp.where(fluid, value, raw[num, x])
-
-    outs = []
-    for at, first in enumerate(range(0, EDGE, GROUP)):
-        looped(first, first + GROUP, stream)
-        part = pl.ds(first, GROUP)
-        outs.append(pltpu.make_async_copy(raw.at[:, part], out_hbm.at[:, part], out_sems.at[at]))
-        outs[-1].start()
-    for out in outs:
-        out.wait()
+                if cz > 0:
+                    pltpu.store(packs.at[1, 5 + UPWARD.index(num)], turned(value, x - 1), mask=depth == x)
+                if cz < 0:
+                    pltpu.store(packs.at[0, 5 + DOWNWARD.index(num)], turned(value, x - (EDGE - 2)), mask=depth == x)
+            res[num, x] = jnp.where(fluid, value, raw[num, x])
+
+    looped(0, EDGE, collide, INNER)
+    store_rims(place, maps, still, moved)
+    looped(0, EDGE, stream, INNER)
+    small[0].wait()
+    for side, sign in ((0, 1), (1, -1)):
+        base = (sign + 1) * slots
+        upright = column_of(nbr, (0, 0, sign), slots)
+        straight, back = place.named(upright, base), place.naming(upright, base)
+        face_maps[side, 0] = place.straight(straight)
+        face_maps[side, 5] = place.straight(back)
+        for at, (cx, cy) in enumerate(FLAT):
+            if at:
+                corner = place.named(column_of(nbr, (-cx, -cy, sign), slots), base)
+                far = place.naming(column_of(nbr, (cx, cy, sign), slots), base)
+                face_maps[side, at] = place.straight(corner) if cx else place.across(straight, corner, cy)
+                face_maps[side, 5 + at] = place.straight(far) if cx else place.across(back, far, cy)
+
+
+def last_kernel(
+    msg_even, msg_odd, got_even, got_odd, flags, maps_in, res, packs, face_maps, out_hbm,
+    raw, layers, out_sems,
+):
+    place = Place(SUB // 2)
+    maps = {key: maps_in[at] for at, key in enumerate(MAP_KEYS)}
+    depth = place.depth
+    odd = lax.axis_index("dev") % 2 == 1
+    tau = msg_even[N_MSG - 1]
+
+    def upper_own(at):
+        return jnp.where(odd, msg_odd[at], msg_even[at])
+
+    def lower_own(at):
+        return jnp.where(odd, msg_even[at], msg_odd[at])
+
+    def upper_got(at):
+        return jnp.where(odd, got_odd[at], got_even[at])
+
+    def lower_got(at):
+        return jnp.where(odd, got_even[at], got_odd[at])
+
+    def opened(value, back):
+        return jnp.where(value < LIMIT, value, back)
+
+    edges, nexts = {}, {}
+    for side, sign in ((0, 1), (1, -1)):
+        own_msg, got_msg = (upper_own, upper_got) if sign > 0 else (lower_own, lower_got)
+        inward, outward = (DOWNWARD, UPWARD) if sign > 0 else (UPWARD, DOWNWARD)
+        own_out = [own_msg(N_MOM + at) for at in range(5)]
+        got_in = [got_msg(N_MOM + at) for at in range(5)]
+        entering, leaving = [], []
+        for at, flat in enumerate(FLAT):
+            mirror = FLAT.index((-flat[0], -flat[1]))
+            value = face_pull(place, got_in[at], flat, face_maps[side, 0], face_maps[side, at])
+            entering.append(opened(value, own_out[mirror]))
+            value = face_pull(place, own_out[at], flat, face_maps[side, 5], face_maps[side, 5 + at])
+            leaving.append(opened(value, got_in[mirror]))
+        far_mom = add_crossing([got_msg(at) for at in range(N_MOM)], leaving, float(sign))
+        far = collided_from(far_mom, got_msg(N_MSG - 1), inward)
+        mom = add_crossing([own_msg(at) for at in range(N_MOM)], entering, float(-sign))
+        fluid = own_out[0] < LIMIT
+        h = collided_from(mom, tau)
+        h = [jnp.where(fluid, h[num], CLOSED) for num in range(19)]
+        edges[side, 0] = h[0]
+        for num in range(1, 19):
+            if not C[num][2]:
+                edges[side, num] = opened(face_shift(place, maps, h[num], C[num]), h[OPP[num]])
+        for at, flat in enumerate(FLAT):
+            value = jnp.where(got_in[0] < LIMIT, far[inward[at]], CLOSED)
+            value = face_pull(place, value, flat, face_maps[side, 0], face_maps[side, at])
+            edges[side, inward[at]] = opened(value, h[OPP[inward[at]]])
+            edges[side, outward[at]] = opened(packs[side, at], h[OPP[outward[at]]])
+            value = face_shift(place, maps, h[inward[at]], C[inward[at]])
+            nexts[inward[at]] = opened(value, packs[side, 5 + at])
+
+    phase = depth % 4
+    for num in range(19):
+        bottom = edges[1, num]
+        top = turned(edges[0, num], EDGE - 1)
+        extra = None
+        if C[num][2] > 0:
+            extra, offset = turned(nexts[num], 1), 1
+        elif C[num][2] < 0:
+            extra, offset = turned(nexts[num], EDGE - 2), 2
+        for r in range(4):
+            value = jnp.where(phase == r, bottom, top)
+            if extra is not None:
+                value = jnp.where(phase == (r + offset) % 4, extra, value)
+            layers[num, r] = value
+
+    ends = (depth == 0) | (depth == EDGE - 1)
+    lanes = {0: ends, 1: ends | (depth == 1), -1: ends | (depth == EDGE - 2)}
+
+    def departure(at):
+        part = pl.ds(at * LEAVING, LEAVING)
+        return pltpu.make_async_copy(raw.at[:, part], out_hbm.at[:, part], out_sems.at[at])
+
+    def leave(at):
+        for part in range(LEAVING):
+            x = at * LEAVING + part
+            fluid = flags[x] > 0
+            for num in range(19):
+                value = turned(layers[num, part % 4], -x)
+                raw[num, x] = jnp.where(fluid & lanes[C[num][2]], value, res[num, x])
+        departure(at).start()
+
+    looped(0, EDGE // LEAVING, leave)
+    looped(0, EDGE // LEAVING, lambda at: departure(at).wait())
 
 
 def body(populations, fluid_flags, neighbours, relax_rate):
@@ -387,25 +471,31 @@
     view = (EDGE, SUB, LANES)
     pops = populations.transpose(1, 0, 2).reshape(19, slots, tiles, LANES).transpose(0, 2, 1, 3).reshape((19,) + view)
     flags = fluid_flags.reshape(slots, tiles, LANES).transpose(1, 0, 2).reshape(view)
+    pops, flags, neighbours, relax_rate = [
+        pltpu.with_memory_space_constraint(arg, pltpu.HBM) for arg in (pops, flags, neighbours, relax_rate)
+    ]
     vmem = pl.BlockSpec(memory_space=pltpu.VMEM)
-    smem = pl.BlockSpec(memory_space=pltpu.SMEM)
     hbm = pl.BlockSpec(memory_space=pltpu.HBM)
     face = (SUB, LANES)
-    scratch = [
-        pltpu.VMEM((19,) + view, jnp.float32),
-        pltpu.VMEM((19,) + view, jnp.float32),
-        pltpu.VMEM((19, EDGE + 2) + face, jnp.float32),
-    ]
+    still = pltpu.VMEM((19,) + view, jnp.float32)
+    moved = pltpu.VMEM((19, EDGE + 2) + face, jnp.float32)
+    nbr = pltpu.SMEM(neighbours.shape, jnp.int32)
+    rate = pltpu.SMEM(relax_rate.shape, jnp.float32)
+    dma = pltpu.SemaphoreType.DMA
     params = pltpu.CompilerParams(vmem_limit_bytes=16 * 2**20)
-    message = jax.ShapeDtypeStruct((N_MSG,) + face, jnp.float32)
-    mom, msg_even, msg_odd = pl.pallas_call(
+    message = pltpu.VMEM((N_MSG,) + face, jnp.float32)
+    mom, msg_even, msg_odd, raw, flags_here, maps = pl.pallas_call(
         first_kernel,
-        out_shape=(jax.ShapeDtypeStruct((N_MOM,) + view, jnp.float32), message, message),
-        in_specs=[hbm, vmem, smem, smem],
-        out_specs=(vmem, vmem, vmem),
-        scratch_shapes=scratch + [
-            pltpu.VMEM((2, N_MOM + 5) + face, jnp.float32),
-            pltpu.SemaphoreType.DMA((EDGE // GROUP,)),
+        out_shape=(
+            pltpu.VMEM((N_MOM,) + view, jnp.float32), message, message,
+            pltpu.VMEM((19,) + view, jnp.float32), pltpu.VMEM(view, jnp.int32),
+            pltpu.VMEM((len(MAP_KEYS),) + face, jnp.int32),
+        ),
+        in_specs=[hbm] * 4,
+        out_specs=(vmem,) * 6,
+        scratch_shapes=[
+            still, moved, nbr, rate, dma((3,)),
+            pltpu.VMEM((2, N_MOM + 5) + face, jnp.float32), dma((EDGE // ARRIVING,)),
         ],
         compiler_params=params,
         name="collide_and_stream",
@@ -414,19 +504,32 @@
     odd_pairs = [(i, (i + 1) % peers if i % 2 else (i - 1) % peers) for i in range(peers)]
     got_odd = lax.ppermute(msg_odd, "dev", odd_pairs)
     got_even = lax.ppermute(msg_even, "dev", even_pairs)
+    res, packs, face_maps = pl.pallas_call(
+        interior_kernel,
+        out_shape=(
+            pltpu.VMEM((19,) + view, jnp.float32),
+            pltpu.VMEM((2, 10) + face, jnp.float32),
+            pltpu.VMEM((2, 10) + face, jnp.int32),
+        ),
+        in_specs=[hbm] + [vmem] * 5,
+        out_specs=(vmem,) * 3,
+        scratch_shapes=[still, moved, nbr, dma((1,))],
+        compiler_params=params,
+        cost_estimate=pl.CostEstimate(flops=12_000_000, bytes_accessed=4_000_000, transcendentals=0),
+        name="interior",
+    )(neighbours, msg_even, mom, raw, flags_here, maps)
     out = pl.pallas_call(
-        second_kernel,
+        last_kernel,
         out_shape=jax.ShapeDtypeStruct(pops.shape, jnp.float32),
-        in_specs=[hbm, vmem, smem, smem, vmem, vmem, vmem, vmem, vmem],
+        in_specs=[vmem] * 9,
         out_specs=hbm,
-        scratch_shapes=scratch + [
-            pltpu.VMEM((2, 10) + face, jnp.float32),
-            pltpu.SemaphoreType.DMA((1,)),
-            pltpu.SemaphoreType.DMA((EDGE // GROUP,)),
+        scratch_shapes=[
+            pltpu.VMEM((19,) + view, jnp.float32), pltpu.VMEM((19, 4) + face, jnp.float32),
+            dma((EDGE // LEAVING,)),
         ],
         compiler_params=params,
         name="finish",
-    )(pops, flags, neighbours, relax_rate, mom, msg_even, msg_odd, got_even, got_odd)
+    )(msg_even, msg_odd, got_even, got_odd, flags_here, maps, res, packs, face_maps)
     out = out.reshape(19, tiles, slots, LANES).transpose(0, 2, 1, 3).reshape(19, slots, cells)
     return out.transpose(1, 0, 2)
 

time: 15.4 us -> 9.62 us (0.62)
  local copies, waits for them, and re-layouts: 3.47 us -> 0 us
  waiting for transfers between devices: 1.9 us -> 0.68 us
  starting transfers between devices: 4.1 us -> 3.43 us
  Pallas kernels: 5.66 us -> 5.33 us
    unnamed x8 -> x0, local copies, waits for them, and re-layouts: 3.47 us -> none
    ppermute x1, waiting for transfers between devices: 1.9 us -> 0.67 us  [body(): got_odd = lax.ppermute(msg_odd, 'dev', odd_pairs)]
    ppermute x1, starting transfers between devices: 0.56 us -> 0.01 us  [body(): got_even = lax.ppermute(msg_even, 'dev', even_pairs)]
    pallas_call x2 -> x3, Pallas kernels: 5.66 us -> 5.33 us  [the longest x1 2.41 us: body(): pl.pallas_call(first_kernel, out_shape=(pltpu.VMEM((N_MOM,) + view, jnp.f...]
  transfers between devices with their start and end apart: 2 -> 2, of which waited for: 1 -> 1; matrix products, arithmetic and copies ran while one was open for 0% -> 0% of each run, Pallas kernels for 0% -> 13%
where the time goes in v4:
time: 9.62 us; the launch traced here: 9.45 us
  Pallas kernels  5.33 us (55%)
  starting transfers between devices  3.43 us (36%)
  waiting for transfers between devices  0.68 us (7%)
    ppermute x1, starting transfers between devices, body(): got_odd = lax.ppermute(msg_odd, 'dev', odd_pairs)  3.43 us
    pallas_call x1, Pallas kernels, body(): pl.pallas_call(first_kernel, out_shape=(pltpu.VMEM((N_MOM,) + view, jnp.f...  2.41 us
    pallas_call x1, Pallas kernels, body(): pl.pallas_call(last_kernel, out_shape=jax.ShapeDtypeStruct(pops.shape, jn...  1.7 us
    pallas_call x1, Pallas kernels, body(): pl.pallas_call(interior_kernel, out_shape=(pltpu.VMEM((19,) + view, jnp.f...  1.22 us
    ppermute x1, waiting for transfers between devices, body(): got_odd = lax.ppermute(msg_odd, 'dev', odd_pairs)  0.67 us
  transfers between devices with their start and end apart: 2, of which 1 were waited for; matrix products, arithmetic and copies ran while one was open for 0% of the time, Pallas kernels for 13%

profile of v4, /device:TPU:0, one launch (start us, length us, event | category | flops | bytes accessed | tf_op | source)
XLA Modules:
  0.0 9.5 jit_solution(13517778944065078563)
XLA Ops:
  0.0 2.4 %collide_and_stream.1 = (f32[9,16,8,128]{3,2,1,0:T(8,128)S(1)}, f32[15,8,128]{2,1,0:T(8,128)S(1)}, f32[15,8,128]{2,1,0:T(8,128)S(1)}, f32[19,16,8,128]{3,2,1,0:T...) custom-call(f32[19,16,8,128]{3,2,1,0:T(8,128)} %bitcast.19, s32[16,8,128]{2,1,0:T(8,128)} %bitcast.20, ...), custom_call_target="tpu_custom_call" | custom-call | tf_op jit(solution)/shard_map/collide_and_stream/pallas_call | solution.py:487
  2.4 3.4 %collective-permute-start.1 = (f32[15,8,128]{2,1,0:T(8,128)S(1)}, f32[15,8,128]{2,1,0:T(8,128)S(1)}, u32[]{:S(2)}, u32[]{:S(2)}) collective-permute-start(f32[15,8,128]{2,1,0:T(8,128)S(1)} %get-tuple-element.15.msg_odd), channel_id=1, source_target_pairs={{0,7},{1,2},{2,1},{3,4},{4,3},{5,6},{6,5},{7,0},{8,15},{9,10},{10,... | collective-permute-start | bytes 184328 | tf_op jit(solution)/shard_map/ppermute | solution.py:505
  5.8 0.0 collective-permute-start
  5.8 1.2 %interior.1 = (f32[19,16,8,128]{3,2,1,0:T(8,128)S(1)}, f32[2,10,8,128]{3,2,1,0:T(8,128)S(1)}, s32[2,10,8,128]{3,2,1,0:T(8,128)S(1)}) custom-call(s32[4,18]{1,0:T(4,128)} %nbr_hbm.3, f32[15,8,128]{2,1,0:T(8,128)S(1)} %get-tuple-element.14.msg_even, f32[9,16,8,128]{3,2,1,0:T(8,128)S(1)} %get-tuple-element.18.mom_in, ...), custom_call_target="tpu_custom_call" | custom-call | flops 12000000 | bytes 4000000 | tf_op jit(solution)/shard_map/interior/pallas_call | solution.py:507
  7.1 0.7 %collective-permute-done.1.got_odd = f32[15,8,128]{2,1,0:T(8,128)S(1)} collective-permute-done((f32[15,8,128]{2,1,0:T(8,128)S(1)}, f32[15,8,128]{2,1,0:T(8,128)S(1)}, u32[]{:S(2)}, u32[]{:S(2)}) %collective-permute-start.1) | collective-permute-done | bytes 61472 | tf_op jit(solution)/shard_map/ppermute | solution.py:505
  7.8 0.0 collective-permute-done.got_even
  7.8 1.7 %finish.1 = f32[19,16,8,128]{3,2,1,0:T(8,128)} custom-call(f32[15,8,128]{2,1,0:T(8,128)S(1)} %get-tuple-element.14.msg_even, f32[15,8,128]{2,1,0:T(8,128)S(1)} %get-tuple-element.15.msg_odd, f32[15,8,128]{2,1,0:T(8,128)S(1)} %collective-permute-done.got_even, f32[15,8,128]{2,1,0:T(8,128)S(1)} %collective-permute-done.1.got_odd, ...), custom_call_target="tpu_custom_call" | custom-call | tf_op jit(solution)/shard_map/finish/pallas_call | solution.py:521
Async XLA Ops:
  2.4 5.3 %collective-permute-start.1 = (f32[15,8,128]{2,1,0:T(8,128)S(1)}, f32[15,8,128]{2,1,0:T(8,128)S(1)}, u32[]{:S(2)}, u32[]{:S(2)}) collective-permute-start(f32[15,8,128]{2,1,0:T(8,128)S(1)} %get-tuple-element.15.msg_odd), channel_id=1, source_target_pairs={{0,7},{1,2},{2,1},{3,4},{4,3},{5,6},{6,5},{7,0},{8,15},{9,10},{10,... | collective-permute-start | bytes 184328 | tf_op jit(solution)/shard_map/ppermute | solution.py:505
  5.8 1.9 %collective-permute-start = (f32[15,8,128]{2,1,0:T(8,128)S(1)}, f32[15,8,128]{2,1,0:T(8,128)S(1)}, u32[]{:S(2)}, u32[]{:S(2)}) collective-permute-start(f32[15,8,128]{2,1,0:T(8,128)S(1)} %get-tuple-element.14.msg_even), channel_id=1, source_target_pairs={{0,1},{1,0},{2,3},{3,2},{4,5},{5,4},{6,7},{7,6},{8,9},{9,8},{10,11... | collective-permute-start | bytes 184328 | tf_op jit(solution)/shard_map/ppermute | solution.py:506

commit v5 on v4

--- a/solution.py
+++ b/solution.py
@@ -11,8 +11,7 @@
 CLOSED = 1.0e30
 LIMIT = 1.0e29
 ARRIVING = 8
-LEAVING = 4
-STREAMED = 8
+LEAVING = 8
 INNER = 8
 
 
@@ -138,6 +137,10 @@
     return jnp.where(source >= 0, moved, CLOSED)
 
 
+def opened(value, back):
+    return jnp.where(value < LIMIT, value, back)
+
+
 class Place:
     def __init__(self, slots):
         self.slots = slots
@@ -190,17 +193,19 @@
     return maps
 
 
-def store_collided(place, maps, still, moved, x, h, fluid):
-    kept = []
+def store_moved(place, maps, moved, x, kept):
+    for num in range(1, 19):
+        cx, cy, cz = C[num]
+        value = kept[num]
+        if cy:
+            value = jnp.where(place.carry(cy), picked(value, maps[0, cy]), value)
+        moved[num, x + 1] = turned(value, EDGE * cy + cz)
+
+
+def store_still(still, x, h, fluid):
+    kept = [jnp.where(fluid, h[num], CLOSED) for num in range(19)]
     for num in range(19):
-        cx, cy, cz = C[num]
-        value = jnp.where(fluid, h[num], CLOSED)
-        kept.append(value)
-        still[num, x] = value
-        if num:
-            if cy:
-                value = jnp.where(place.carry(cy), picked(value, maps[0, cy]), value)
-            moved[num, x + 1] = turned(value, EDGE * cy + cz)
+        still[num, x] = kept[num]
     return kept
 
 
@@ -242,6 +247,14 @@
     return value
 
 
+def unlayered(place, layers, num, z):
+    phase = place.depth % 4
+    value = layers[num, (0 - z) % 4]
+    for at in range(1, 4):
+        value = jnp.where(phase == at, layers[num, (at - z) % 4], value)
+    return turned(value, -z)
+
+
 def tau_plane(place, rate):
     tau = jnp.zeros((SUB, LANES), jnp.float32)
     for slot in range(place.slots):
@@ -265,8 +278,8 @@
 
 
 def first_kernel(
-    pop_hbm, flags_hbm, nbr_hbm, rate_hbm, mom_out, msg_even, msg_odd, raw, flags, maps_out,
-    still, moved, nbr, rate, small_sems, sides, sems,
+    pop_hbm, flags_hbm, nbr_hbm, rate_hbm, still, msg_even, msg_odd, raw, flags, maps_out,
+    nbr, rate, small_sems, layers, sems,
 ):
     slots = nbr.shape[0]
     place = Place(slots)
@@ -286,54 +299,63 @@
         maps_out[at] = maps[key]
     depth = place.depth
 
-    def collide(x):
+    def collide(x, phase):
         h = collided_from(moments([raw[num, x] for num in range(19)]), tau)
-        kept = store_collided(place, maps, still, moved, x, h, flags[x] > 0)
-        for at in range(5):
-            pltpu.store(sides.at[0, N_MOM + at], turned(kept[UPWARD[at]], x - (EDGE - 1)), mask=depth == x)
-            pltpu.store(sides.at[1, N_MOM + at], turned(kept[DOWNWARD[at]], x), mask=depth == x)
-
-    keep = {1: depth != 0, -1: depth != EDGE - 1}
-
-    def stream(x):
-        g = [still[0, x]]
-        for num in range(1, 19):
-            value = moved[num, x + 1 - C[num][0]]
-            value = jnp.where(value < LIMIT, value, still[OPP[num], x])
-            if C[num][2]:
-                value = jnp.where(keep[C[num][2]], value, 0.0)
-            g.append(value)
-        mom = moments(g)
-        for at in range(N_MOM):
-            mom_out[at, x] = mom[at]
-            pltpu.store(sides.at[0, at], turned(mom[at], x - (EDGE - 1)), mask=depth == x)
-            pltpu.store(sides.at[1, at], turned(mom[at], x), mask=depth == x)
+        kept = store_still(still, x, h, flags[x] > 0)
+        near = ((depth - x + 2) & (EDGE - 1)) < 4
+        for num in range(19):
+            pltpu.store(layers.at[num, phase], turned(kept[num], x), mask=near)
 
     def collide_arrived(at):
         arrival(at).wait()
-        looped(0, ARRIVING, lambda part: collide(at * ARRIVING + part), ARRIVING)
+        for part in range(ARRIVING):
+            collide(at * ARRIVING + part, part % 4)
 
     looped(0, EDGE // ARRIVING, collide_arrived)
-    store_rims(place, maps, still, moved)
-    looped(0, EDGE, stream, STREAMED)
+    messages = []
+    for sign in (1, -1):
+        inward, outward = (DOWNWARD, UPWARD) if sign > 0 else (UPWARD, DOWNWARD)
+        face, within = (EDGE - 1, EDGE - 2) if sign > 0 else (0, 1)
+        h = [unlayered(place, layers, num, face) for num in range(19)]
+        g = [None] * 19
+        g[0] = h[0]
+        for num in range(1, 19):
+            if num in inward:
+                g[num] = jnp.zeros((SUB, LANES), jnp.float32)
+                continue
+            source = unlayered(place, layers, num, within) if num in outward else h[num]
+            g[num] = opened(face_shift(place, maps, source, C[num]), h[OPP[num]])
+        messages.append(moments(g) + [h[num] for num in outward] + [tau])
     odd = lax.axis_index("dev") % 2 == 1
-    for at in range(N_MSG):
-        upper = tau if at == N_MSG - 1 else sides[0, at]
-        lower = tau if at == N_MSG - 1 else sides[1, at]
+    for at, (upper, lower) in enumerate(zip(*messages)):
         msg_even[at] = jnp.where(odd, lower, upper)
         msg_odd[at] = jnp.where(odd, upper, lower)
 
 
-def interior_kernel(nbr_hbm, msg_even, mom_in, raw, flags, maps_in, res, packs, face_maps, still, moved, nbr, small_sems):
+def interior_kernel(
+    nbr_hbm, msg_even, first_still, raw, flags, maps_in, res, packs, face_maps,
+    still, moved, first_moved, nbr, small_sems,
+):
     slots = nbr.shape[0]
     place = Place(slots)
     small = small_copies((nbr_hbm,), (nbr,), small_sems)
     maps = {key: maps_in[at] for at, key in enumerate(MAP_KEYS)}
     depth = place.depth
     tau = msg_even[N_MSG - 1]
+    keep = {1: depth != 0, -1: depth != EDGE - 1}
+
     def collide(x):
-        h = collided_from([mom_in[at, x] for at in range(N_MOM)], tau)
-        store_collided(place, maps, still, moved, x, h, flags[x] > 0)
+        g = [first_still[0, x]]
+        for num in range(1, 19):
+            value = opened(first_moved[num, x + 1 - C[num][0]], first_still[OPP[num], x])
+            if C[num][2]:
+                value = jnp.where(keep[C[num][2]], value, 0.0)
+            g.append(value)
+        h = collided_from(moments(g), tau)
+        store_moved(place, maps, moved, x, store_still(still, x, h, flags[x] > 0))
+
+    def move(x):
+        store_moved(place, maps, first_moved, x, [first_still[num, x] for num in range(19)])
 
     def stream(x):
         fluid = flags[x] > 0
@@ -353,6 +375,8 @@
                     pltpu.store(packs.at[0, 5 + DOWNWARD.index(num)], turned(value, x - (EDGE - 2)), mask=depth == x)
             res[num, x] = jnp.where(fluid, value, raw[num, x])
 
+    looped(0, EDGE, move, INNER)
+    store_rims(place, maps, first_still, first_moved)
     looped(0, EDGE, collide, INNER)
     store_rims(place, maps, still, moved)
     looped(0, EDGE, stream, INNER)
@@ -392,9 +416,6 @@
 
     def lower_got(at):
         return jnp.where(odd, got_even[at], got_odd[at])
-
-    def opened(value, back):
-        return jnp.where(value < LIMIT, value, back)
 
     edges, nexts = {}, {}
     for side, sign in ((0, 1), (1, -1)):
@@ -484,21 +505,19 @@
     dma = pltpu.SemaphoreType.DMA
     params = pltpu.CompilerParams(vmem_limit_bytes=16 * 2**20)
     message = pltpu.VMEM((N_MSG,) + face, jnp.float32)
-    mom, msg_even, msg_odd, raw, flags_here, maps = pl.pallas_call(
+    first_still, msg_even, msg_odd, raw, flags_here, maps = pl.pallas_call(
         first_kernel,
         out_shape=(
-            pltpu.VMEM((N_MOM,) + view, jnp.float32), message, message,
-            pltpu.VMEM((19,) + view, jnp.float32), pltpu.VMEM(view, jnp.int32),
+            still, message, message, still, pltpu.VMEM(view, jnp.int32),
             pltpu.VMEM((len(MAP_KEYS),) + face, jnp.int32),
         ),
         in_specs=[hbm] * 4,
         out_specs=(vmem,) * 6,
         scratch_shapes=[
-            still, moved, nbr, rate, dma((3,)),
-            pltpu.VMEM((2, N_MOM + 5) + face, jnp.float32), dma((EDGE // ARRIVING,)),
+            nbr, rate, dma((3,)), pltpu.VMEM((19, 4) + face, jnp.float32), dma((EDGE // ARRIVING,)),
         ],
         compiler_params=params,
-        name="collide_and_stream",
+        name="collide_first",
     )(pops, flags, neighbours, relax_rate)
     even_pairs = [(i, i ^ 1) for i in range(peers)]
     odd_pairs = [(i, (i + 1) % peers if i % 2 else (i - 1) % peers) for i in range(peers)]
@@ -513,11 +532,11 @@
         ),
         in_specs=[hbm] + [vmem] * 5,
         out_specs=(vmem,) * 3,
-        scratch_shapes=[still, moved, nbr, dma((1,))],
+        scratch_shapes=[still, moved, moved, nbr, dma((1,))],
         compiler_params=params,
         cost_estimate=pl.CostEstimate(flops=12_000_000, bytes_accessed=4_000_000, transcendentals=0),
         name="interior",
-    )(neighbours, msg_even, mom, raw, flags_here, maps)
+    )(neighbours, msg_even, first_still, raw, flags_here, maps)
     out = pl.pallas_call(
         last_kernel,
         out_shape=jax.ShapeDtypeStruct(pops.shape, jnp.float32),

time: 9.62 us -> 9.17 us (0.953)
  waiting for transfers between devices: 0.68 us -> 0.01 us
  Pallas kernels: 5.33 us -> 5.52 us
    pallas_call x1, Pallas kernels: 1.22 us -> 1.95 us  [body(): pl.pallas_call(interior_kernel, out_shape=(pltpu.VMEM((19,) + view, jnp.f...]
    ppermute x1, waiting for transfers between devices: 0.67 us -> 0.01 us  [body(): got_odd = lax.ppermute(msg_odd, 'dev', odd_pairs)]
    pallas_call x1, Pallas kernels: 2.41 us -> 1.92 us  [body(): pl.pallas_call(first_kernel, out_shape=(still, message, message, still, p...]
  transfers between devices with their start and end apart: 2 -> 2, of which waited for: 1 -> 0; matrix products, arithmetic and copies ran while one was open for 0% -> 0% of each run, Pallas kernels for 13% -> 22%
where the time goes in v5:
time: 9.17 us; the launch traced here: 8.99 us
  Pallas kernels  5.52 us (60%)
  starting transfers between devices  3.43 us (37%)
    ppermute x1, starting transfers between devices, body(): got_odd = lax.ppermute(msg_odd, 'dev', odd_pairs)  3.43 us
    pallas_call x1, Pallas kernels, body(): pl.pallas_call(interior_kernel, out_shape=(pltpu.VMEM((19,) + view, jnp.f...  1.95 us
    pallas_call x1, Pallas kernels, body(): pl.pallas_call(first_kernel, out_shape=(still, message, message, still, p...  1.92 us
    pallas_call x1, Pallas kernels, body(): pl.pallas_call(last_kernel, out_shape=jax.ShapeDtypeStruct(pops.shape, jn...  1.66 us
  transfers between devices with their start and end apart: 2, of which 0 were waited for; matrix products, arithmetic and copies ran while one was open for 0% of the time, Pallas kernels for 22%

profile of v5, /device:TPU:0, one launch (start us, length us, event | category | flops | bytes accessed | tf_op | source)
XLA Modules:
  0.0 9.0 jit_solution(7580925931972291077)
XLA Ops:
  0.0 1.9 %collide_first.1 = (f32[19,16,8,128]{3,2,1,0:T(8,128)S(1)}, f32[15,8,128]{2,1,0:T(8,128)S(1)}, f32[15,8,128]{2,1,0:T(8,128)S(1)}, f32[19,16,8,128]{3,2,1,0:T(8,1...) custom-call(f32[19,16,8,128]{3,2,1,0:T(8,128)} %bitcast.19, s32[16,8,128]{2,1,0:T(8,128)} %bitcast.20, ...), custom_call_target="tpu_custom_call" | custom-call | tf_op jit(solution)/shard_map/collide_first/pallas_call | solution.py:508
  1.9 3.4 %collective-permute-start.1 = (f32[15,8,128]{2,1,0:T(8,128)S(1)}, f32[15,8,128]{2,1,0:T(8,128)S(1)}, u32[]{:S(2)}, u32[]{:S(2)}) collective-permute-start(f32[15,8,128]{2,1,0:T(8,128)S(1)} %get-tuple-element.15.msg_odd), channel_id=1, source_target_pairs={{0,7},{1,2},{2,1},{3,4},{4,3},{5,6},{6,5},{7,0},{8,15},{9,10},{10,... | collective-permute-start | bytes 184328 | tf_op jit(solution)/shard_map/ppermute | solution.py:524
  5.4 0.0 collective-permute-start
  5.4 1.9 %interior.1 = (f32[19,16,8,128]{3,2,1,0:T(8,128)S(1)}, f32[2,10,8,128]{3,2,1,0:T(8,128)S(1)}, s32[2,10,8,128]{3,2,1,0:T(8,128)S(1)}) custom-call(s32[4,18]{1,0:T(4,128)} %nbr_hbm.3, f32[15,8,128]{2,1,0:T(8,128)S(1)} %get-tuple-element.14.msg_even, f32[19,16,8,128]{3,2,1,0:T(8,128)S(1)} %get-tuple-element.18.first_still, ...), custom_call_target="tpu_custom_call" | custom-call | flops 12000000 | bytes 4000000 | tf_op jit(solution)/shard_map/interior/pallas_call | solution.py:526
  7.3 0.0 collective-permute-done.1.got_odd
  7.3 0.0 collective-permute-done.got_even
  7.3 1.7 %finish.1 = f32[19,16,8,128]{3,2,1,0:T(8,128)} custom-call(f32[15,8,128]{2,1,0:T(8,128)S(1)} %get-tuple-element.14.msg_even, f32[15,8,128]{2,1,0:T(8,128)S(1)} %get-tuple-element.15.msg_odd, f32[15,8,128]{2,1,0:T(8,128)S(1)} %collective-permute-done.got_even, f32[15,8,128]{2,1,0:T(8,128)S(1)} %collective-permute-done.1.got_odd, ...), custom_call_target="tpu_custom_call" | custom-call | tf_op jit(solution)/shard_map/finish/pallas_call | solution.py:540
Async XLA Ops:
  1.9 5.4 %collective-permute-start.1 = (f32[15,8,128]{2,1,0:T(8,128)S(1)}, f32[15,8,128]{2,1,0:T(8,128)S(1)}, u32[]{:S(2)}, u32[]{:S(2)}) collective-permute-start(f32[15,8,128]{2,1,0:T(8,128)S(1)} %get-tuple-element.15.msg_odd), channel_id=1, source_target_pairs={{0,7},{1,2},{2,1},{3,4},{4,3},{5,6},{6,5},{7,0},{8,15},{9,10},{10,... | collective-permute-start | bytes 184328 | tf_op jit(solution)/shard_map/ppermute | solution.py:524
  5.4 2.0 %collective-permute-start = (f32[15,8,128]{2,1,0:T(8,128)S(1)}, f32[15,8,128]{2,1,0:T(8,128)S(1)}, u32[]{:S(2)}, u32[]{:S(2)}) collective-permute-start(f32[15,8,128]{2,1,0:T(8,128)S(1)} %get-tuple-element.14.msg_even), channel_id=1, source_target_pairs={{0,1},{1,0},{2,3},{3,2},{4,5},{5,4},{6,7},{7,6},{8,9},{9,8},{10,11... | collective-permute-start | bytes 184328 | tf_op jit(solution)/shard_map/ppermute | solution.py:525

commit v6 on v5

--- a/solution.py
+++ b/solution.py
@@ -11,6 +11,7 @@
 CLOSED = 1.0e30
 LIMIT = 1.0e29
 ARRIVING = 8
+TRIP = 8
 LEAVING = 8
 INNER = 8
 
@@ -40,7 +41,8 @@
 DOWNWARD = [INDEX[(a, b, -1)] for a, b in FLAT]
 MAP_KEYS = [(cx, cy) for cx in (0, 1, -1) for cy in (0, 1, -1) if cx or cy]
 N_MOM = 9
-N_MSG = N_MOM + 5 + 1
+SENT = (0, 1, 2, 3, 5, 6)
+N_MSG = len(SENT) + 1 + 5 + 1
 
 
 def column(vector):
@@ -195,7 +197,7 @@
 
 def store_moved(place, maps, moved, x, kept):
     for num in range(1, 19):
-        cx, cy, cz = C[num]
+        _, cy, cz = C[num]
         value = kept[num]
         if cy:
             value = jnp.where(place.carry(cy), picked(value, maps[0, cy]), value)
@@ -247,12 +249,12 @@
     return value
 
 
-def unlayered(place, layers, num, z):
-    phase = place.depth % 4
-    value = layers[num, (0 - z) % 4]
-    for at in range(1, 4):
-        value = jnp.where(phase == at, layers[num, (at - z) % 4], value)
-    return turned(value, -z)
+def layers_of(num):
+    cz = C[num][2]
+    return (0, EDGE - 1) + ((EDGE - 2,) if cz > 0 else (1,) if cz < 0 else ())
+
+
+LAYERS = [(num, z) for num in range(19) for z in layers_of(num)]
 
 
 def tau_plane(place, rate):
@@ -278,7 +280,7 @@
 
 
 def first_kernel(
-    pop_hbm, flags_hbm, nbr_hbm, rate_hbm, still, msg_even, msg_odd, raw, flags, maps_out,
+    pop_hbm, flags_hbm, nbr_hbm, rate_hbm, still, msg_even, msg_odd, raw, flags, maps_out, tau_out, sides,
     nbr, rate, small_sems, layers, sems,
 ):
     slots = nbr.shape[0]
@@ -295,37 +297,45 @@
         copy.wait()
     maps = plane_maps(place, nbr)
     tau = tau_plane(place, rate)
+    tau_out[...] = tau
     for at, key in enumerate(MAP_KEYS):
         maps_out[at] = maps[key]
     depth = place.depth
 
-    def collide(x, phase):
+    def collide(x):
         h = collided_from(moments([raw[num, x] for num in range(19)]), tau)
         kept = store_still(still, x, h, flags[x] > 0)
-        near = ((depth - x + 2) & (EDGE - 1)) < 4
+        at_z = {z: depth == ((x + z) & (EDGE - 1)) for z in (0, 1, EDGE - 2, EDGE - 1)}
         for num in range(19):
-            pltpu.store(layers.at[num, phase], turned(kept[num], x), mask=near)
+            value = turned(kept[num], x)
+            for z in layers_of(num):
+                pltpu.store(layers.at[LAYERS.index((num, z))], value, mask=at_z[z])
 
     def collide_arrived(at):
-        arrival(at).wait()
-        for part in range(ARRIVING):
-            collide(at * ARRIVING + part, part % 4)
-
-    looped(0, EDGE // ARRIVING, collide_arrived)
+        for part in range(TRIP):
+            if part % ARRIVING == 0:
+                arrival(at * (TRIP // ARRIVING) + part // ARRIVING).wait()
+            collide(at * TRIP + part)
+
+    looped(0, EDGE // TRIP, collide_arrived)
     messages = []
-    for sign in (1, -1):
+    for side, sign in ((0, 1), (1, -1)):
         inward, outward = (DOWNWARD, UPWARD) if sign > 0 else (UPWARD, DOWNWARD)
         face, within = (EDGE - 1, EDGE - 2) if sign > 0 else (0, 1)
-        h = [unlayered(place, layers, num, face) for num in range(19)]
+        h = [turned(layers[LAYERS.index((num, face))], -face) for num in range(19)]
         g = [None] * 19
         g[0] = h[0]
         for num in range(1, 19):
             if num in inward:
                 g[num] = jnp.zeros((SUB, LANES), jnp.float32)
                 continue
-            source = unlayered(place, layers, num, within) if num in outward else h[num]
+            source = turned(layers[LAYERS.index((num, within))], -within) if num in outward else h[num]
             g[num] = opened(face_shift(place, maps, source, C[num]), h[OPP[num]])
-        messages.append(moments(g) + [h[num] for num in outward] + [tau])
+        mom = moments(g)
+        out = [h[num] for num in outward]
+        for at, value in enumerate(mom + out):
+            sides[side, at] = value
+        messages.append([mom[at] for at in SENT] + [mom[7] + mom[8]] + out + [tau])
     odd = lax.axis_index("dev") % 2 == 1
     for at, (upper, lower) in enumerate(zip(*messages)):
         msg_even[at] = jnp.where(odd, lower, upper)
@@ -333,15 +343,15 @@
 
 
 def interior_kernel(
-    nbr_hbm, msg_even, first_still, raw, flags, maps_in, res, packs, face_maps,
-    still, moved, first_moved, nbr, small_sems,
+    nbr_hbm, tau_in, sides, first_still, raw, flags, maps_in, res, packs, face_maps, pulls,
+    still, moved, first_moved, layers, nbr, small_sems,
 ):
     slots = nbr.shape[0]
     place = Place(slots)
     small = small_copies((nbr_hbm,), (nbr,), small_sems)
     maps = {key: maps_in[at] for at, key in enumerate(MAP_KEYS)}
     depth = place.depth
-    tau = msg_even[N_MSG - 1]
+    tau = tau_in[...]
     keep = {1: depth != 0, -1: depth != EDGE - 1}
 
     def collide(x):
@@ -357,22 +367,26 @@
     def move(x):
         store_moved(place, maps, first_moved, x, [first_still[num, x] for num in range(19)])
 
+    end = {1: depth == EDGE - 1, -1: depth == 0}
+
     def stream(x):
         fluid = flags[x] > 0
+        near = {
+            1: (depth == ((x + EDGE - 1) & (EDGE - 1))) | (depth == ((x + 1) & (EDGE - 1))),
+            -1: (depth == x) | (depth == ((x + EDGE - 2) & (EDGE - 1))),
+        }
         for num in range(19):
             value = back = still[OPP[num], x]
             if num:
-                cx, cy, cz = C[num]
+                cx, _, cz = C[num]
                 value = moved[num, x + 1 - cx]
-                if cz > 0:
-                    pltpu.store(packs.at[0, UPWARD.index(num)], turned(value, x - (EDGE - 1)), mask=depth == x)
-                if cz < 0:
-                    pltpu.store(packs.at[1, DOWNWARD.index(num)], turned(value, x), mask=depth == x)
-                value = jnp.where(value < LIMIT, value, back)
-                if cz > 0:
-                    pltpu.store(packs.at[1, 5 + UPWARD.index(num)], turned(value, x - 1), mask=depth == x)
-                if cz < 0:
-                    pltpu.store(packs.at[0, 5 + DOWNWARD.index(num)], turned(value, x - (EDGE - 2)), mask=depth == x)
+                if cz:
+                    value = jnp.where((value < LIMIT) | end[cz], value, back)
+                    at = (UPWARD if cz > 0 else DOWNWARD).index(num)
+                    part = lax.rem(x, 4)
+                    pltpu.store(layers.at[(1 - cz) // 2, at, part], turned(value, x), mask=near[cz])
+                else:
+                    value = opened(value, back)
             res[num, x] = jnp.where(fluid, value, raw[num, x])
 
     looped(0, EDGE, move, INNER)
@@ -386,30 +400,32 @@
         upright = column_of(nbr, (0, 0, sign), slots)
         straight, back = place.named(upright, base), place.naming(upright, base)
         face_maps[side, 0] = place.straight(straight)
-        face_maps[side, 5] = place.straight(back)
         for at, (cx, cy) in enumerate(FLAT):
             if at:
                 corner = place.named(column_of(nbr, (-cx, -cy, sign), slots), base)
                 far = place.naming(column_of(nbr, (cx, cy, sign), slots), base)
                 face_maps[side, at] = place.straight(corner) if cx else place.across(straight, corner, cy)
-                face_maps[side, 5 + at] = place.straight(far) if cx else place.across(back, far, cy)
+                own_far = place.straight(far) if cx else place.across(back, far, cy)
+            pulls[side, at] = face_pull(place, sides[side, N_MOM + at], (cx, cy), place.straight(back), own_far if at else None)
+    phase = depth % 4
+    for way, picks in ((0, ((0, 0, EDGE - 1), (1, 5, 1))), (1, ((1, 0, 0), (0, 5, EDGE - 2)))):
+        for at in range(5):
+            for side, first, z in picks:
+                value = layers[way, at, (0 - z) % 4]
+                for step in range(1, 4):
+                    value = jnp.where(phase == step, layers[way, at, (step - z) % 4], value)
+                packs[side, first + at] = turned(value, -z)
 
 
 def last_kernel(
-    msg_even, msg_odd, got_even, got_odd, flags, maps_in, res, packs, face_maps, out_hbm,
+    tau_in, sides, got_even, got_odd, flags, maps_in, res, packs, face_maps, pulls, out_hbm,
     raw, layers, out_sems,
 ):
     place = Place(SUB // 2)
     maps = {key: maps_in[at] for at, key in enumerate(MAP_KEYS)}
     depth = place.depth
     odd = lax.axis_index("dev") % 2 == 1
-    tau = msg_even[N_MSG - 1]
-
-    def upper_own(at):
-        return jnp.where(odd, msg_odd[at], msg_even[at])
-
-    def lower_own(at):
-        return jnp.where(odd, msg_even[at], msg_odd[at])
+    tau = tau_in[...]
 
     def upper_got(at):
         return jnp.where(odd, got_odd[at], got_even[at])
@@ -419,20 +435,22 @@
 
     edges, nexts = {}, {}
     for side, sign in ((0, 1), (1, -1)):
-        own_msg, got_msg = (upper_own, upper_got) if sign > 0 else (lower_own, lower_got)
+        got_msg = upper_got if sign > 0 else lower_got
         inward, outward = (DOWNWARD, UPWARD) if sign > 0 else (UPWARD, DOWNWARD)
-        own_out = [own_msg(N_MOM + at) for at in range(5)]
-        got_in = [got_msg(N_MOM + at) for at in range(5)]
+        own_out = [sides[side, N_MOM + at] for at in range(5)]
+        got_in = [got_msg(len(SENT) + 1 + at) for at in range(5)]
         entering, leaving = [], []
         for at, flat in enumerate(FLAT):
             mirror = FLAT.index((-flat[0], -flat[1]))
             value = face_pull(place, got_in[at], flat, face_maps[side, 0], face_maps[side, at])
             entering.append(opened(value, own_out[mirror]))
-            value = face_pull(place, own_out[at], flat, face_maps[side, 5], face_maps[side, 5 + at])
-            leaving.append(opened(value, got_in[mirror]))
-        far_mom = add_crossing([got_msg(at) for at in range(N_MOM)], leaving, float(sign))
-        far = collided_from(far_mom, got_msg(N_MSG - 1), inward)
-        mom = add_crossing([own_msg(at) for at in range(N_MOM)], entering, float(-sign))
+            leaving.append(opened(pulls[side, at], got_in[mirror]))
+        zero = jnp.zeros((SUB, LANES), jnp.float32)
+        got_mom = [zero] * N_MOM
+        for at, which in enumerate(SENT + (7,)):
+            got_mom[which] = got_msg(at)
+        far = collided_from(add_crossing(got_mom, leaving, float(sign)), got_msg(N_MSG - 1), inward)
+        mom = add_crossing([sides[side, at] for at in range(N_MOM)], entering, float(-sign))
         fluid = own_out[0] < LIMIT
         h = collided_from(mom, tau)
         h = [jnp.where(fluid, h[num], CLOSED) for num in range(19)]
@@ -505,42 +523,54 @@
     dma = pltpu.SemaphoreType.DMA
     params = pltpu.CompilerParams(vmem_limit_bytes=16 * 2**20)
     message = pltpu.VMEM((N_MSG,) + face, jnp.float32)
-    first_still, msg_even, msg_odd, raw, flags_here, maps = pl.pallas_call(
+    plane = pltpu.VMEM(face, jnp.float32)
+    first_still, msg_even, msg_odd, raw, flags_here, maps, tau, sides = pl.pallas_call(
         first_kernel,
         out_shape=(
             still, message, message, still, pltpu.VMEM(view, jnp.int32),
-            pltpu.VMEM((len(MAP_KEYS),) + face, jnp.int32),
+            pltpu.VMEM((len(MAP_KEYS),) + face, jnp.int32), plane, pltpu.VMEM((2, N_MOM + 5) + face, jnp.float32),
         ),
         in_specs=[hbm] * 4,
-        out_specs=(vmem,) * 6,
+        out_specs=(vmem,) * 8,
         scratch_shapes=[
-            nbr, rate, dma((3,)), pltpu.VMEM((19, 4) + face, jnp.float32), dma((EDGE // ARRIVING,)),
+            nbr, rate, dma((3,)), pltpu.VMEM((len(LAYERS),) + face, jnp.float32), dma((EDGE // ARRIVING,)),
         ],
         compiler_params=params,
         name="collide_first",
     )(pops, flags, neighbours, relax_rate)
     even_pairs = [(i, i ^ 1) for i in range(peers)]
-    odd_pairs = [(i, (i + 1) % peers if i % 2 else (i - 1) % peers) for i in range(peers)]
-    got_odd = lax.ppermute(msg_odd, "dev", odd_pairs)
+    groups = lax.axis_size("group")
+    odd_pairs = []
+    for i in range(groups * peers):
+        group, dev = divmod(i, peers)
+        to = dev + 1 if dev % 2 else dev - 1
+        if 0 <= to < peers:
+            odd_pairs.append((i, group * peers + to))
+        elif groups % 2 == 0:
+            odd_pairs.append((i, (group ^ 1) * peers + dev))
+        else:
+            odd_pairs.append((i, group * peers + to % peers))
+    got_odd = lax.ppermute(msg_odd, ("group", "dev"), odd_pairs)
     got_even = lax.ppermute(msg_even, "dev", even_pairs)
-    res, packs, face_maps = pl.pallas_call(
+    res, packs, face_maps, pulls = pl.pallas_call(
         interior_kernel,
         out_shape=(
             pltpu.VMEM((19,) + view, jnp.float32),
             pltpu.VMEM((2, 10) + face, jnp.float32),
-            pltpu.VMEM((2, 10) + face, jnp.int32),
+            pltpu.VMEM((2, 5) + face, jnp.int32),
+            pltpu.VMEM((2, 5) + face, jnp.float32),
         ),
-        in_specs=[hbm] + [vmem] * 5,
-        out_specs=(vmem,) * 3,
-        scratch_shapes=[still, moved, moved, nbr, dma((1,))],
+        in_specs=[hbm] + [vmem] * 6,
+        out_specs=(vmem,) * 4,
+        scratch_shapes=[still, moved, moved, pltpu.VMEM((2, 5, 4) + face, jnp.float32), nbr, dma((1,))],
         compiler_params=params,
         cost_estimate=pl.CostEstimate(flops=12_000_000, bytes_accessed=4_000_000, transcendentals=0),
         name="interior",
-    )(neighbours, msg_even, first_still, raw, flags_here, maps)
+    )(neighbours, tau, sides, first_still, raw, flags_here, maps)
     out = pl.pallas_call(
         last_kernel,
         out_shape=jax.ShapeDtypeStruct(pops.shape, jnp.float32),
-        in_specs=[vmem] * 9,
+        in_specs=[vmem] * 10,
         out_specs=hbm,
         scratch_shapes=[
             pltpu.VMEM((19,) + view, jnp.float32), pltpu.VMEM((19, 4) + face, jnp.float32),
@@ -548,7 +578,7 @@
         ],
         compiler_params=params,
         name="finish",
-    )(msg_even, msg_odd, got_even, got_odd, flags_here, maps, res, packs, face_maps)
+    )(tau, sides, got_even, got_odd, flags_here, maps, res, packs, face_maps, pulls)
     out = out.reshape(19, tiles, slots, LANES).transpose(0, 2, 1, 3).reshape(19, slots, cells)
     return out.transpose(1, 0, 2)
 

time: 9.17 us -> 8.97 us (0.978)
  starting transfers between devices: 3.43 us -> 3.2 us
  waiting for transfers between devices: 0.01 us -> 0.21 us
  Pallas kernels: 5.52 us -> 5.37 us
    ppermute x1, starting transfers between devices: 3.43 us -> 2.64 us  [body(): got_odd = lax.ppermute(msg_odd, ('group', 'dev'), odd_pairs)]
    ppermute x1, starting transfers between devices: 0.01 us -> 0.56 us  [body(): got_even = lax.ppermute(msg_even, 'dev', even_pairs)]
    ppermute x1, waiting for transfers between devices: 0.01 us -> 0.21 us  [body(): got_odd = lax.ppermute(msg_odd, ('group', 'dev'), odd_pairs)]
  transfers between devices with their start and end apart: 2 -> 2, of which waited for: 0 -> 1; matrix products, arithmetic and copies ran while one was open for 0% -> 0% of each run, Pallas kernels for 22% -> 21%
where the time goes in v6:
time: 8.97 us; the launch traced here: 8.81 us
  Pallas kernels  5.37 us (60%)
  starting transfers between devices  3.2 us (36%)
  waiting for transfers between devices  0.21 us (2%)
    ppermute x1, starting transfers between devices, body(): got_odd = lax.ppermute(msg_odd, ('group', 'dev'), odd_pairs)  2.64 us
    pallas_call x1, Pallas kernels, body(): pl.pallas_call(interior_kernel, out_shape=(pltpu.VMEM((19,) + view, jnp.f...  1.88 us
    pallas_call x1, Pallas kernels, body(): pl.pallas_call(first_kernel, out_shape=(still, message, message, still, p...  1.88 us
    pallas_call x1, Pallas kernels, body(): pl.pallas_call(last_kernel, out_shape=jax.ShapeDtypeStruct(pops.shape, jn...  1.61 us
    ppermute x1, starting transfers between devices, body(): got_even = lax.ppermute(msg_even, 'dev', even_pairs)  0.56 us
    ppermute x1, waiting for transfers between devices, body(): got_odd = lax.ppermute(msg_odd, ('group', 'dev'), odd_pairs)  0.21 us
  transfers between devices with their start and end apart: 2, of which 1 were waited for; matrix products, arithmetic and copies ran while one was open for 0% of the time, Pallas kernels for 21%

profile of v6, /device:TPU:0, one launch (start us, length us, event | category | flops | bytes accessed | tf_op | source)
XLA Modules:
  0.0 8.8 jit_solution(2038515805433891511)
XLA Ops:
  0.0 1.9 %collide_first.1 = (f32[19,16,8,128]{3,2,1,0:T(8,128)S(1)}, f32[13,8,128]{2,1,0:T(8,128)S(1)}, f32[13,8,128]{2,1,0:T(8,128)S(1)}, f32[19,16,8,128]{3,2,1,0:T(8,1...) custom-call(f32[19,16,8,128]{3,2,1,0:T(8,128)} %bitcast.19, ...), custom_call_target="tpu_custom_call" | custom-call | tf_op jit(solution)/shard_map/collide_first/pallas_call | solution.py:527
  1.9 0.6 %collective-permute-start = (f32[13,8,128]{2,1,0:T(8,128)S(1)}, f32[13,8,128]{2,1,0:T(8,128)S(1)}, u32[]{:S(2)}, u32[]{:S(2)}) collective-permute-start(f32[13,8,128]{2,1,0:T(8,128)S(1)} %get-tuple-element.19), channel_id=1, source_target_pairs={{0,1},{1,0},{2,3},{3,2},{4,5},{5,4},{6,7},{7,6},{8,9},{9,8},{10,11... | collective-permute-start | bytes 159752 | tf_op jit(solution)/shard_map/ppermute | solution.py:554
  2.4 2.6 %collective-permute-start.1 = (f32[13,8,128]{2,1,0:T(8,128)S(1)}, f32[13,8,128]{2,1,0:T(8,128)S(1)}, u32[]{:S(2)}, u32[]{:S(2)}) collective-permute-start(f32[13,8,128]{2,1,0:T(8,128)S(1)} %get-tuple-element.20), channel_id=1, source_target_pairs={{0,8},{1,2},{2,1},{3,4},{4,3},{5,6},{6,5},{7,15},{8,0},{9,10},{10,... | collective-permute-start | bytes 159752 | tf_op jit(solution)/shard_map/ppermute | solution.py:553
  5.1 1.9 %interior.1 = (f32[19,16,8,128]{3,2,1,0:T(8,128)S(1)}, f32[2,10,8,128]{3,2,1,0:T(8,128)S(1)}, s32[2,5,8,128]{3,2,1,0:T(8,128)S(1)}, f32[2,5,8,128]{3,2,1,0:T(8,128)S(1)}) custom-call(s32[4,18]{1,0:T(4,128)} %nbr_hbm.3, f32[8,128]{1,0:T(8,128)S(1)} %get-tuple-element.17.tau_in, f32[2,14,8,128]{3,2,1,0:T(8,128)S(1)} %get-tuple-element.18.sides, ...), custom_call_target="tpu_custom_call" | custom-call | flops 12000000 | bytes 4000000 | tf_op jit(solution)/shard_map/interior/pallas_call | solution.py:555
  7.0 0.0 collective-permute-done.got_even
  7.0 0.2 %collective-permute-done.1.got_odd = f32[13,8,128]{2,1,0:T(8,128)S(1)} collective-permute-done((f32[13,8,128]{2,1,0:T(8,128)S(1)}, f32[13,8,128]{2,1,0:T(8,128)S(1)}, u32[]{:S(2)}, u32[]{:S(2)}) %collective-permute-start.1) | collective-permute-done | bytes 53280 | tf_op jit(solution)/shard_map/ppermute | solution.py:553
  7.2 1.6 %finish.1 = f32[19,16,8,128]{3,2,1,0:T(8,128)} custom-call(f32[8,128]{1,0:T(8,128)S(1)} %get-tuple-element.17.tau_in, f32[2,14,8,128]{3,2,1,0:T(8,128)S(1)} %get-tuple-element.18.sides, f32[13,8,128]{2,1,0:T(8,128)S(1)} %collective-permute-done.got_even, f32[13,8,128]{2,1,0:T(8,128)S(1)} %collective-permute-done.1.got_odd, ...), custom_call_target="tpu_custom_call" | custom-call | tf_op jit(solution)/shard_map/finish/pallas_call | solution.py:570
Async XLA Ops:
  1.9 5.1 %collective-permute-start = (f32[13,8,128]{2,1,0:T(8,128)S(1)}, f32[13,8,128]{2,1,0:T(8,128)S(1)}, u32[]{:S(2)}, u32[]{:S(2)}) collective-permute-start(f32[13,8,128]{2,1,0:T(8,128)S(1)} %get-tuple-element.19), channel_id=1, source_target_pairs={{0,1},{1,0},{2,3},{3,2},{4,5},{5,4},{6,7},{7,6},{8,9},{9,8},{10,11... | collective-permute-start | bytes 159752 | tf_op jit(solution)/shard_map/ppermute | solution.py:554
  2.4 4.8 %collective-permute-start.1 = (f32[13,8,128]{2,1,0:T(8,128)S(1)}, f32[13,8,128]{2,1,0:T(8,128)S(1)}, u32[]{:S(2)}, u32[]{:S(2)}) collective-permute-start(f32[13,8,128]{2,1,0:T(8,128)S(1)} %get-tuple-element.20), channel_id=1, source_target_pairs={{0,8},{1,2},{2,1},{3,4},{4,3},{5,6},{6,5},{7,15},{8,0},{9,10},{10,... | collective-permute-start | bytes 159752 | tf_op jit(solution)/shard_map/ppermute | solution.py:553

commit v7 on v6

--- a/solution.py
+++ b/solution.py
@@ -488,16 +488,13 @@
         part = pl.ds(at * LEAVING, LEAVING)
         return pltpu.make_async_copy(raw.at[:, part], out_hbm.at[:, part], out_sems.at[at])
 
-    def leave(at):
-        for part in range(LEAVING):
-            x = at * LEAVING + part
+    for at in range(EDGE // LEAVING):
+        for x in range(at * LEAVING, (at + 1) * LEAVING):
             fluid = flags[x] > 0
             for num in range(19):
-                value = turned(layers[num, part % 4], -x)
+                value = turned(layers[num, x % 4], -x)
                 raw[num, x] = jnp.where(fluid & lanes[C[num][2]], value, res[num, x])
         departure(at).start()
-
-    looped(0, EDGE // LEAVING, leave)
     looped(0, EDGE // LEAVING, lambda at: departure(at).wait())
 
 

time: 8.97 us -> 8.88 us (0.990)
  transfers between devices with their start and end apart: 2 -> 2, of which waited for: 1 -> 1; matrix products, arithmetic and copies ran while one was open for 0% -> 0% of each run, Pallas kernels for 21% -> 22%
where the time goes in v7:
time: 8.88 us; the launch traced here: 8.72 us
  Pallas kernels  5.29 us (60%)
  starting transfers between devices  3.2 us (36%)
  waiting for transfers between devices  0.21 us (2%)
    ppermute x1, starting transfers between devices, body(): got_odd = lax.ppermute(msg_odd, ('group', 'dev'), odd_pairs)  2.64 us
    pallas_call x1, Pallas kernels, body(): pl.pallas_call(interior_kernel, out_shape=(pltpu.VMEM((19,) + view, jnp.f...  1.88 us
    pallas_call x1, Pallas kernels, body(): pl.pallas_call(first_kernel, out_shape=(still, message, message, still, p...  1.88 us
    pallas_call x1, Pallas kernels, body(): pl.pallas_call(last_kernel, out_shape=jax.ShapeDtypeStruct(pops.shape, jn...  1.52 us
    ppermute x1, starting transfers between devices, body(): got_even = lax.ppermute(msg_even, 'dev', even_pairs)  0.56 us
    ppermute x1, waiting for transfers between devices, body(): got_odd = lax.ppermute(msg_odd, ('group', 'dev'), odd_pairs)  0.21 us
  transfers between devices with their start and end apart: 2, of which 1 were waited for; matrix products, arithmetic and copies ran while one was open for 0% of the time, Pallas kernels for 22%

profile of v7, /device:TPU:0, one launch (start us, length us, event | category | flops | bytes accessed | tf_op | source)
XLA Modules:
  0.0 8.7 jit_solution(5064083604200866438)
XLA Ops:
  0.0 1.9 %collide_first.1 = (f32[19,16,8,128]{3,2,1,0:T(8,128)S(1)}, f32[13,8,128]{2,1,0:T(8,128)S(1)}, f32[13,8,128]{2,1,0:T(8,128)S(1)}, f32[19,16,8,128]{3,2,1,0:T(8,1...) custom-call(f32[19,16,8,128]{3,2,1,0:T(8,128)} %bitcast.19, ...), custom_call_target="tpu_custom_call" | custom-call | tf_op jit(solution)/shard_map/collide_first/pallas_call | solution.py:524
  1.9 0.6 %collective-permute-start = (f32[13,8,128]{2,1,0:T(8,128)S(1)}, f32[13,8,128]{2,1,0:T(8,128)S(1)}, u32[]{:S(2)}, u32[]{:S(2)}) collective-permute-start(f32[13,8,128]{2,1,0:T(8,128)S(1)} %get-tuple-element.19), channel_id=1, source_target_pairs={{0,1},{1,0},{2,3},{3,2},{4,5},{5,4},{6,7},{7,6},{8,9},{9,8},{10,11... | collective-permute-start | bytes 159752 | tf_op jit(solution)/shard_map/ppermute | solution.py:551
  2.4 2.6 %collective-permute-start.1 = (f32[13,8,128]{2,1,0:T(8,128)S(1)}, f32[13,8,128]{2,1,0:T(8,128)S(1)}, u32[]{:S(2)}, u32[]{:S(2)}) collective-permute-start(f32[13,8,128]{2,1,0:T(8,128)S(1)} %get-tuple-element.20), channel_id=1, source_target_pairs={{0,8},{1,2},{2,1},{3,4},{4,3},{5,6},{6,5},{7,15},{8,0},{9,10},{10,... | collective-permute-start | bytes 159752 | tf_op jit(solution)/shard_map/ppermute | solution.py:550
  5.1 1.9 %interior.1 = (f32[19,16,8,128]{3,2,1,0:T(8,128)S(1)}, f32[2,10,8,128]{3,2,1,0:T(8,128)S(1)}, s32[2,5,8,128]{3,2,1,0:T(8,128)S(1)}, f32[2,5,8,128]{3,2,1,0:T(8,128)S(1)}) custom-call(s32[4,18]{1,0:T(4,128)} %nbr_hbm.3, f32[8,128]{1,0:T(8,128)S(1)} %get-tuple-element.17.tau_in, f32[2,14,8,128]{3,2,1,0:T(8,128)S(1)} %get-tuple-element.18.sides, ...), custom_call_target="tpu_custom_call" | custom-call | flops 12000000 | bytes 4000000 | tf_op jit(solution)/shard_map/interior/pallas_call | solution.py:552
  7.0 0.0 collective-permute-done.got_even
  7.0 0.2 %collective-permute-done.1.got_odd = f32[13,8,128]{2,1,0:T(8,128)S(1)} collective-permute-done((f32[13,8,128]{2,1,0:T(8,128)S(1)}, f32[13,8,128]{2,1,0:T(8,128)S(1)}, u32[]{:S(2)}, u32[]{:S(2)}) %collective-permute-start.1) | collective-permute-done | bytes 53280 | tf_op jit(solution)/shard_map/ppermute | solution.py:550
  7.2 1.5 %finish.1 = f32[19,16,8,128]{3,2,1,0:T(8,128)} custom-call(f32[8,128]{1,0:T(8,128)S(1)} %get-tuple-element.17.tau_in, f32[2,14,8,128]{3,2,1,0:T(8,128)S(1)} %get-tuple-element.18.sides, f32[13,8,128]{2,1,0:T(8,128)S(1)} %collective-permute-done.got_even, f32[13,8,128]{2,1,0:T(8,128)S(1)} %collective-permute-done.1.got_odd, ...), custom_call_target="tpu_custom_call" | custom-call | tf_op jit(solution)/shard_map/finish/pallas_call | solution.py:567
Async XLA Ops:
  1.9 5.1 %collective-permute-start = (f32[13,8,128]{2,1,0:T(8,128)S(1)}, f32[13,8,128]{2,1,0:T(8,128)S(1)}, u32[]{:S(2)}, u32[]{:S(2)}) collective-permute-start(f32[13,8,128]{2,1,0:T(8,128)S(1)} %get-tuple-element.19), channel_id=1, source_target_pairs={{0,1},{1,0},{2,3},{3,2},{4,5},{5,4},{6,7},{7,6},{8,9},{9,8},{10,11... | collective-permute-start | bytes 159752 | tf_op jit(solution)/shard_map/ppermute | solution.py:551
  2.4 4.8 %collective-permute-start.1 = (f32[13,8,128]{2,1,0:T(8,128)S(1)}, f32[13,8,128]{2,1,0:T(8,128)S(1)}, u32[]{:S(2)}, u32[]{:S(2)}) collective-permute-start(f32[13,8,128]{2,1,0:T(8,128)S(1)} %get-tuple-element.20), channel_id=1, source_target_pairs={{0,8},{1,2},{2,1},{3,4},{4,3},{5,6},{6,5},{7,15},{8,0},{9,10},{10,... | collective-permute-start | bytes 159752 | tf_op jit(solution)/shard_map/ppermute | solution.py:550

commit v8 on v7

--- a/solution.py
+++ b/solution.py
@@ -383,7 +383,7 @@
                 if cz:
                     value = jnp.where((value < LIMIT) | end[cz], value, back)
                     at = (UPWARD if cz > 0 else DOWNWARD).index(num)
-                    part = lax.rem(x, 4)
+                    part = x % 4
                     pltpu.store(layers.at[(1 - cz) // 2, at, part], turned(value, x), mask=near[cz])
                 else:
                     value = opened(value, back)
@@ -393,7 +393,8 @@
     store_rims(place, maps, first_still, first_moved)
     looped(0, EDGE, collide, INNER)
     store_rims(place, maps, still, moved)
-    looped(0, EDGE, stream, INNER)
+    for x in range(EDGE):
+        stream(x)
     small[0].wait()
     for side, sign in ((0, 1), (1, -1)):
         base = (sign + 1) * slots

time: 8.88 us -> 8.88 us (level)
  Pallas kernels: 5.29 us -> 5.13 us
  waiting for transfers between devices: 0.21 us -> 0.37 us
    pallas_call x1, Pallas kernels: 1.88 us -> 1.73 us  [body(): pl.pallas_call(interior_kernel, out_shape=(pltpu.VMEM((19,) + view, jnp.f...]
    ppermute x1, waiting for transfers between devices: 0.21 us -> 0.37 us  [body(): got_odd = lax.ppermute(msg_odd, ('group', 'dev'), odd_pairs)]
  transfers between devices with their start and end apart: 2 -> 2, of which waited for: 1 -> 1; matrix products, arithmetic and copies ran while one was open for 0% -> 0% of each run, Pallas kernels for 22% -> 20%
where the time goes in v8:
time: 8.88 us; the launch traced here: 8.72 us
  Pallas kernels  5.13 us (58%)
  starting transfers between devices  3.2 us (36%)
  waiting for transfers between devices  0.37 us (4%)
    ppermute x1, starting transfers between devices, body(): got_odd = lax.ppermute(msg_odd, ('group', 'dev'), odd_pairs)  2.64 us
    pallas_call x1, Pallas kernels, body(): pl.pallas_call(first_kernel, out_shape=(still, message, message, still, p...  1.88 us
    pallas_call x1, Pallas kernels, body(): pl.pallas_call(interior_kernel, out_shape=(pltpu.VMEM((19,) + view, jnp.f...  1.73 us
    pallas_call x1, Pallas kernels, body(): pl.pallas_call(last_kernel, out_shape=jax.ShapeDtypeStruct(pops.shape, jn...  1.52 us
    ppermute x1, starting transfers between devices, body(): got_even = lax.ppermute(msg_even, 'dev', even_pairs)  0.56 us
    ppermute x1, waiting for transfers between devices, body(): got_odd = lax.ppermute(msg_odd, ('group', 'dev'), odd_pairs)  0.37 us
  transfers between devices with their start and end apart: 2, of which 1 were waited for; matrix products, arithmetic and copies ran while one was open for 0% of the time, Pallas kernels for 20%

profile of v8, /device:TPU:0, one launch (start us, length us, event | category | flops | bytes accessed | tf_op | source)
XLA Modules:
  0.0 8.7 jit_solution(14435161204051686159)
XLA Ops:
  0.0 1.9 %collide_first.1 = (f32[19,16,8,128]{3,2,1,0:T(8,128)S(1)}, f32[13,8,128]{2,1,0:T(8,128)S(1)}, f32[13,8,128]{2,1,0:T(8,128)S(1)}, f32[19,16,8,128]{3,2,1,0:T(8,1...) custom-call(f32[19,16,8,128]{3,2,1,0:T(8,128)} %bitcast.19, ...), custom_call_target="tpu_custom_call" | custom-call | tf_op jit(solution)/shard_map/collide_first/pallas_call | solution.py:525
  1.9 0.6 %collective-permute-start = (f32[13,8,128]{2,1,0:T(8,128)S(1)}, f32[13,8,128]{2,1,0:T(8,128)S(1)}, u32[]{:S(2)}, u32[]{:S(2)}) collective-permute-start(f32[13,8,128]{2,1,0:T(8,128)S(1)} %get-tuple-element.19), channel_id=1, source_target_pairs={{0,1},{1,0},{2,3},{3,2},{4,5},{5,4},{6,7},{7,6},{8,9},{9,8},{10,11... | collective-permute-start | bytes 159752 | tf_op jit(solution)/shard_map/ppermute | solution.py:552
  2.4 2.6 %collective-permute-start.1 = (f32[13,8,128]{2,1,0:T(8,128)S(1)}, f32[13,8,128]{2,1,0:T(8,128)S(1)}, u32[]{:S(2)}, u32[]{:S(2)}) collective-permute-start(f32[13,8,128]{2,1,0:T(8,128)S(1)} %get-tuple-element.20), channel_id=1, source_target_pairs={{0,8},{1,2},{2,1},{3,4},{4,3},{5,6},{6,5},{7,15},{8,0},{9,10},{10,... | collective-permute-start | bytes 159752 | tf_op jit(solution)/shard_map/ppermute | solution.py:551
  5.1 1.7 %interior.1 = (f32[19,16,8,128]{3,2,1,0:T(8,128)S(1)}, f32[2,10,8,128]{3,2,1,0:T(8,128)S(1)}, s32[2,5,8,128]{3,2,1,0:T(8,128)S(1)}, f32[2,5,8,128]{3,2,1,0:T(8,128)S(1)}) custom-call(s32[4,18]{1,0:T(4,128)} %nbr_hbm.3, f32[8,128]{1,0:T(8,128)S(1)} %get-tuple-element.17.tau_in, f32[2,14,8,128]{3,2,1,0:T(8,128)S(1)} %get-tuple-element.18.sides, ...), custom_call_target="tpu_custom_call" | custom-call | flops 12000000 | bytes 4000000 | tf_op jit(solution)/shard_map/interior/pallas_call | solution.py:553
  6.8 0.0 collective-permute-done.got_even
  6.8 0.4 %collective-permute-done.1.got_odd = f32[13,8,128]{2,1,0:T(8,128)S(1)} collective-permute-done((f32[13,8,128]{2,1,0:T(8,128)S(1)}, f32[13,8,128]{2,1,0:T(8,128)S(1)}, u32[]{:S(2)}, u32[]{:S(2)}) %collective-permute-start.1) | collective-permute-done | bytes 53280 | tf_op jit(solution)/shard_map/ppermute | solution.py:551
  7.2 1.5 %finish.1 = f32[19,16,8,128]{3,2,1,0:T(8,128)} custom-call(f32[8,128]{1,0:T(8,128)S(1)} %get-tuple-element.17.tau_in, f32[2,14,8,128]{3,2,1,0:T(8,128)S(1)} %get-tuple-element.18.sides, f32[13,8,128]{2,1,0:T(8,128)S(1)} %collective-permute-done.got_even, f32[13,8,128]{2,1,0:T(8,128)S(1)} %collective-permute-done.1.got_odd, ...), custom_call_target="tpu_custom_call" | custom-call | tf_op jit(solution)/shard_map/finish/pallas_call | solution.py:568
Async XLA Ops:
  1.9 4.9 %collective-permute-start = (f32[13,8,128]{2,1,0:T(8,128)S(1)}, f32[13,8,128]{2,1,0:T(8,128)S(1)}, u32[]{:S(2)}, u32[]{:S(2)}) collective-permute-start(f32[13,8,128]{2,1,0:T(8,128)S(1)} %get-tuple-element.19), channel_id=1, source_target_pairs={{0,1},{1,0},{2,3},{3,2},{4,5},{5,4},{6,7},{7,6},{8,9},{9,8},{10,11... | collective-permute-start | bytes 159752 | tf_op jit(solution)/shard_map/ppermute | solution.py:552
  2.4 4.8 %collective-permute-start.1 = (f32[13,8,128]{2,1,0:T(8,128)S(1)}, f32[13,8,128]{2,1,0:T(8,128)S(1)}, u32[]{:S(2)}, u32[]{:S(2)}) collective-permute-start(f32[13,8,128]{2,1,0:T(8,128)S(1)} %get-tuple-element.20), channel_id=1, source_target_pairs={{0,8},{1,2},{2,1},{3,4},{4,3},{5,6},{6,5},{7,15},{8,0},{9,10},{10,... | collective-permute-start | bytes 159752 | tf_op jit(solution)/shard_map/ppermute | solution.py:551

commit v9 on v8

--- a/solution.py
+++ b/solution.py
@@ -12,7 +12,7 @@
 LIMIT = 1.0e29
 ARRIVING = 8
 TRIP = 8
-LEAVING = 8
+LEAVING = ((0, 8), (8, 13), (13, 16))
 INNER = 8
 
 
@@ -486,17 +486,18 @@
     lanes = {0: ends, 1: ends | (depth == 1), -1: ends | (depth == EDGE - 2)}
 
     def departure(at):
-        part = pl.ds(at * LEAVING, LEAVING)
+        part = pl.ds(LEAVING[at][0], LEAVING[at][1] - LEAVING[at][0])
         return pltpu.make_async_copy(raw.at[:, part], out_hbm.at[:, part], out_sems.at[at])
 
-    for at in range(EDGE // LEAVING):
-        for x in range(at * LEAVING, (at + 1) * LEAVING):
+    for at in range(len(LEAVING)):
+        for x in range(*LEAVING[at]):
             fluid = flags[x] > 0
             for num in range(19):
                 value = turned(layers[num, x % 4], -x)
                 raw[num, x] = jnp.where(fluid & lanes[C[num][2]], value, res[num, x])
         departure(at).start()
-    looped(0, EDGE // LEAVING, lambda at: departure(at).wait())
+    for at in range(len(LEAVING)):
+        departure(at).wait()
 
 
 def body(populations, fluid_flags, neighbours, relax_rate):
@@ -572,7 +573,7 @@
         out_specs=hbm,
         scratch_shapes=[
             pltpu.VMEM((19,) + view, jnp.float32), pltpu.VMEM((19, 4) + face, jnp.float32),
-            dma((EDGE // LEAVING,)),
+            dma((len(LEAVING),)),
         ],
         compiler_params=params,
         name="finish",

time: 8.88 us -> 8.88 us (level)
  no operation moved by 1% of the time
where the time goes in v9:
time: 8.88 us; the launch traced here: 8.72 us
  Pallas kernels  5.13 us (58%)
  starting transfers between devices  3.2 us (36%)
  waiting for transfers between devices  0.37 us (4%)
    ppermute x1, starting transfers between devices, body(): got_odd = lax.ppermute(msg_odd, ('group', 'dev'), odd_pairs)  2.64 us
    pallas_call x1, Pallas kernels, body(): pl.pallas_call(first_kernel, out_shape=(still, message, message, still, p...  1.88 us
    pallas_call x1, Pallas kernels, body(): pl.pallas_call(interior_kernel, out_shape=(pltpu.VMEM((19,) + view, jnp.f...  1.73 us
    pallas_call x1, Pallas kernels, body(): pl.pallas_call(last_kernel, out_shape=jax.ShapeDtypeStruct(pops.shape, jn...  1.52 us
    ppermute x1, starting transfers between devices, body(): got_even = lax.ppermute(msg_even, 'dev', even_pairs)  0.56 us
    ppermute x1, waiting for transfers between devices, body(): got_odd = lax.ppermute(msg_odd, ('group', 'dev'), odd_pairs)  0.37 us
  transfers between devices with their start and end apart: 2, of which 1 were waited for; matrix products, arithmetic and copies ran while one was open for 0% of the time, Pallas kernels for 20%

profile of v9, /device:TPU:0, one launch (start us, length us, event | category | flops | bytes accessed | tf_op | source)
XLA Modules:
  0.0 8.7 jit_solution(6714633803277231657)
XLA Ops:
  0.0 1.9 %collide_first.1 = (f32[19,16,8,128]{3,2,1,0:T(8,128)S(1)}, f32[13,8,128]{2,1,0:T(8,128)S(1)}, f32[13,8,128]{2,1,0:T(8,128)S(1)}, f32[19,16,8,128]{3,2,1,0:T(8,1...) custom-call(f32[19,16,8,128]{3,2,1,0:T(8,128)} %bitcast.19, ...), custom_call_target="tpu_custom_call" | custom-call | tf_op jit(solution)/shard_map/collide_first/pallas_call | solution.py:526
  1.9 0.6 %collective-permute-start = (f32[13,8,128]{2,1,0:T(8,128)S(1)}, f32[13,8,128]{2,1,0:T(8,128)S(1)}, u32[]{:S(2)}, u32[]{:S(2)}) collective-permute-start(f32[13,8,128]{2,1,0:T(8,128)S(1)} %get-tuple-element.19), channel_id=1, source_target_pairs={{0,1},{1,0},{2,3},{3,2},{4,5},{5,4},{6,7},{7,6},{8,9},{9,8},{10,11... | collective-permute-start | bytes 159752 | tf_op jit(solution)/shard_map/ppermute | solution.py:553
  2.4 2.6 %collective-permute-start.1 = (f32[13,8,128]{2,1,0:T(8,128)S(1)}, f32[13,8,128]{2,1,0:T(8,128)S(1)}, u32[]{:S(2)}, u32[]{:S(2)}) collective-permute-start(f32[13,8,128]{2,1,0:T(8,128)S(1)} %get-tuple-element.20), channel_id=1, source_target_pairs={{0,8},{1,2},{2,1},{3,4},{4,3},{5,6},{6,5},{7,15},{8,0},{9,10},{10,... | collective-permute-start | bytes 159752 | tf_op jit(solution)/shard_map/ppermute | solution.py:552
  5.1 1.7 %interior.1 = (f32[19,16,8,128]{3,2,1,0:T(8,128)S(1)}, f32[2,10,8,128]{3,2,1,0:T(8,128)S(1)}, s32[2,5,8,128]{3,2,1,0:T(8,128)S(1)}, f32[2,5,8,128]{3,2,1,0:T(8,128)S(1)}) custom-call(s32[4,18]{1,0:T(4,128)} %nbr_hbm.3, f32[8,128]{1,0:T(8,128)S(1)} %get-tuple-element.17.tau_in, f32[2,14,8,128]{3,2,1,0:T(8,128)S(1)} %get-tuple-element.18.sides, ...), custom_call_target="tpu_custom_call" | custom-call | flops 12000000 | bytes 4000000 | tf_op jit(solution)/shard_map/interior/pallas_call | solution.py:554
  6.8 0.0 collective-permute-done.got_even
  6.8 0.4 %collective-permute-done.1.got_odd = f32[13,8,128]{2,1,0:T(8,128)S(1)} collective-permute-done((f32[13,8,128]{2,1,0:T(8,128)S(1)}, f32[13,8,128]{2,1,0:T(8,128)S(1)}, u32[]{:S(2)}, u32[]{:S(2)}) %collective-permute-start.1) | collective-permute-done | bytes 53280 | tf_op jit(solution)/shard_map/ppermute | solution.py:552
  7.2 1.5 %finish.1 = f32[19,16,8,128]{3,2,1,0:T(8,128)} custom-call(f32[8,128]{1,0:T(8,128)S(1)} %get-tuple-element.17.tau_in, f32[2,14,8,128]{3,2,1,0:T(8,128)S(1)} %get-tuple-element.18.sides, f32[13,8,128]{2,1,0:T(8,128)S(1)} %collective-permute-done.got_even, f32[13,8,128]{2,1,0:T(8,128)S(1)} %collective-permute-done.1.got_odd, ...), custom_call_target="tpu_custom_call" | custom-call | tf_op jit(solution)/shard_map/finish/pallas_call | solution.py:569
Async XLA Ops:
  1.9 4.9 %collective-permute-start = (f32[13,8,128]{2,1,0:T(8,128)S(1)}, f32[13,8,128]{2,1,0:T(8,128)S(1)}, u32[]{:S(2)}, u32[]{:S(2)}) collective-permute-start(f32[13,8,128]{2,1,0:T(8,128)S(1)} %get-tuple-element.19), channel_id=1, source_target_pairs={{0,1},{1,0},{2,3},{3,2},{4,5},{5,4},{6,7},{7,6},{8,9},{9,8},{10,11... | collective-permute-start | bytes 159752 | tf_op jit(solution)/shard_map/ppermute | solution.py:553
  2.4 4.8 %collective-permute-start.1 = (f32[13,8,128]{2,1,0:T(8,128)S(1)}, f32[13,8,128]{2,1,0:T(8,128)S(1)}, u32[]{:S(2)}, u32[]{:S(2)}) collective-permute-start(f32[13,8,128]{2,1,0:T(8,128)S(1)} %get-tuple-element.20), channel_id=1, source_target_pairs={{0,8},{1,2},{2,1},{3,4},{4,3},{5,6},{6,5},{7,15},{8,0},{9,10},{10,... | collective-permute-start | bytes 159752 | tf_op jit(solution)/shard_map/ppermute | solution.py:552
